TPU v7x, 32 devices: a whole 2x2x4 slice. The times are simulated.
32 devices in a mesh: segment: 2 (over core), seq: 8 (over z, y), tp: 2 (over x).
Axes of the slice: x: 2, y: 2, z: 4, core: 2. Of those that a mesh axis runs over, the one named last changes fastest.
Arguments:
- inputs: bfloat16 [2, 2048, 2688], P(None, 'seq', 'tp'), may hold values from -6 to 6
- lengths: int32 [2, 8], replicated, may hold values from 64 to 256
- boundary: int32 [2], replicated, may hold values from 0 to 2047
- attn_gain: float32 [2, 2688], P('segment'), may hold values from 0.5 to 1.5
- query_weight: bfloat16 [2, 2688, 2048], P('segment', 'seq', 'tp')
- key_weight: bfloat16 [2, 2688, 1024], P('segment', None, 'tp')
- value_weight: bfloat16 [2, 2688, 1024], P('segment', None, 'tp'), may hold values from -0.125 to 0.125
- out_weight: bfloat16 [2, 2048, 2688], P('segment', 'tp', 'seq'), may hold values from -0.125 to 0.125
Outputs:
- layer_states: bfloat16 [2, 2, 2048, 2688], P('segment', None, 'seq', 'tp')
All inputs are finite; a program needn't handle non-finite values.
Results may differ from a plain program's by a relative error of at most 0.02.
Values may be sent and summed in bfloat16 or wider, within the bound.
No kernel may reach another device: no remote copies, remote signals or barrier semaphores. Data moves between devices by JAX's collectives and lax.ppermute only.
A program may use at most 128 MiB of HBM per device.

v0:
```python
import math

import jax
import jax.numpy as jnp
from jax import lax
from jax.sharding import PartitionSpec as P

HEADS = 16
KV = 8
HEAD_DIM = 128
WINDOW = 1024


norm_epsilon = 1e-06


def passed_along(value, axis, steps):
    count = lax.axis_size(axis)
    initial, last = (max(0, -steps), min(count, count - steps))
    return lax.ppermute(value, axis, [(source, source + steps) for source in range(initial, last)])


def normalize(state, norm_gain):
    widened = state.astype(jnp.float32)
    mean_square = jnp.mean(widened * widened, axis=-1, keepdims=True)
    return (widened * lax.rsqrt(mean_square + norm_epsilon) * norm_gain).astype(jnp.bfloat16)


def rotate(tensor, positions):
    half_dim = tensor.shape[-1] // 2
    inverse = jnp.exp(
        -math.log(10000.0) * jnp.arange(half_dim, dtype=jnp.float32) * (2.0 / tensor.shape[-1])
    )
    angles = positions.astype(jnp.float32)[:, None] * inverse[None, :]
    cosine = jnp.cos(angles)[:, None, :]
    sine_part = jnp.sin(angles)[:, None, :]
    first_half = tensor[..., :half_dim]
    second_half = tensor[..., half_dim:]
    return jnp.concatenate(
        [
            first_half * cosine - second_half * sine_part,
            second_half * cosine + first_half * sine_part,
        ],
        axis=-1,
    )


def per_device(
    inputs, lengths, boundary, attn_gain, query_weight, key_weight, value_weight, out_weight
):
    segment_index = lax.axis_index("segment")
    segment_count = lax.axis_size("segment")
    seq_index = lax.axis_index("seq")
    batch_count = inputs.shape[0]
    block_len = inputs.shape[1]
    width_half = inputs.shape[2]
    seq_count = lengths.shape[1]
    reach_blocks = max(1, WINDOW // block_len)
    group_size = HEADS // KV
    query_rows = lax.all_gather(query_weight, "seq", axis=1, tiled=True)[0]
    output_cols = lax.all_gather(out_weight, "seq", axis=2, tiled=True)[0]
    key_matrix = key_weight[0]
    value_matrix = value_weight[0]
    norm_gain = attn_gain[0]
    kv_local = key_matrix.shape[1] // HEAD_DIM
    width_full = output_cols.shape[1]
    row_ids = jnp.arange(block_len, dtype=jnp.int32)
    query_slots = seq_index * block_len + row_ids

    def project(full_state):
        normed = normalize(full_state, norm_gain)
        queries = jnp.dot(normed, query_rows, preferred_element_type=jnp.float32).reshape(
            block_len, -1, HEAD_DIM
        )
        queries = (
            rotate(queries, query_slots)
            .astype(jnp.bfloat16)
            .reshape(block_len, kv_local, group_size, HEAD_DIM)
        )
        key_rows = jnp.dot(normed, key_matrix, preferred_element_type=jnp.float32).reshape(
            block_len, kv_local, HEAD_DIM
        )
        key_rows = (
            rotate(key_rows, query_slots)
            .astype(jnp.bfloat16)
            .reshape(block_len, kv_local * HEAD_DIM)
        )
        value_rows = jnp.dot(normed, value_matrix, preferred_element_type=jnp.float32).astype(
            jnp.bfloat16
        )
        return (queries, key_rows, value_rows)

    def project_empty(full_state):
        return (
            jnp.zeros((block_len, kv_local, group_size, HEAD_DIM), jnp.bfloat16),
            jnp.zeros((block_len, kv_local * HEAD_DIM), jnp.bfloat16),
            jnp.zeros((block_len, kv_local * HEAD_DIM), jnp.bfloat16),
        )

    def window_rows(key_rows, value_rows):
        key_parts = []
        value_parts = []
        for distance in range(reach_blocks, 0, -1):
            far_keys, far_values = passed_along((key_rows, value_rows), "seq", distance)
            key_parts.append(far_keys)
            value_parts.append(far_values)
        key_parts.append(key_rows)
        value_parts.append(value_rows)
        key_all = jnp.concatenate(key_parts, axis=0)
        value_all = jnp.concatenate(value_parts, axis=0)
        return (key_all, value_all)

    def make_mix(micro_index):

        def mix_rows(operands):
            queries, key_all, value_all = operands
            lengths_row = jnp.sum(
                jnp.where(
                    jnp.arange(batch_count, dtype=jnp.int32)[:, None] == micro_index, lengths, 0
                ),
                axis=0,
            )
            episode_start = jnp.sum(
                jnp.where(jnp.arange(batch_count, dtype=jnp.int32) == micro_index, boundary, 0)
            )
            block_ids = seq_index - reach_blocks + jnp.arange(reach_blocks + 1, dtype=jnp.int32)
            block_lengths = jnp.sum(
                jnp.where(
                    block_ids[:, None] == jnp.arange(seq_count, dtype=jnp.int32)[None, :],
                    lengths_row[None, :],
                    0,
                ),
                axis=1,
            )
            key_slots = (block_ids[:, None] * block_len + row_ids[None, :]).reshape(-1)
            key_valid = (row_ids[None, :] < block_lengths[:, None]).reshape(-1)
            own_length = jnp.sum(
                jnp.where(jnp.arange(seq_count, dtype=jnp.int32) == seq_index, lengths_row, 0)
            )
            query_valid = row_ids < own_length
            inside = (key_slots[None, :] <= query_slots[:, None]) & (
                key_slots[None, :] > query_slots[:, None] - WINDOW
            )
            episode = (query_slots[:, None] < episode_start) | (key_slots[None, :] >= episode_start)
            visible = inside & episode & key_valid[None, :] & query_valid[:, None]
            key_heads = key_all.reshape(-1, kv_local, HEAD_DIM)
            value_heads = value_all.reshape(-1, kv_local, HEAD_DIM)
            scores = jnp.einsum(
                "qgjd,kgd->gjqk", queries, key_heads, preferred_element_type=jnp.float32
            ) * HEAD_DIM ** (-0.5)
            masked = jnp.where(visible, scores, -1e30)
            row_max = jnp.max(masked, axis=-1, keepdims=True)
            exp_terms = jnp.where(visible, jnp.exp(masked - row_max), 0.0)
            row_total = jnp.sum(exp_terms, axis=-1, keepdims=True)
            row_total = jnp.where(query_valid[:, None], row_total, 1.0)
            weights = (exp_terms / row_total).astype(jnp.bfloat16)
            mixed_heads = jnp.einsum(
                "gjqk,kgd->qgjd", weights, value_heads, preferred_element_type=jnp.float32
            ).astype(jnp.bfloat16)
            return jnp.dot(
                mixed_heads.reshape(block_len, -1), output_cols, preferred_element_type=jnp.float32
            )

        return mix_rows

    def mix_empty(operands):
        return jnp.zeros((block_len, width_full), jnp.float32)

    def attend(full_state, micro_index, active):
        queries, key_rows, value_rows = lax.cond(active, project, project_empty, full_state)
        key_all, value_all = window_rows(key_rows, value_rows)
        return lax.cond(active, make_mix(micro_index), mix_empty, (queries, key_all, value_all))

    def advance(state_half, micro_index, active):
        full_state = lax.all_gather(state_half, "tp", axis=1, tiled=True)
        partial_value = attend(full_state, micro_index, active)
        summed = lax.psum_scatter(partial_value, "tp", scatter_dimension=1, tiled=True)
        return (state_half.astype(jnp.float32) + summed).astype(jnp.bfloat16)

    def relay_tick(tick_index, loop_state):
        incoming, states = loop_state
        micro_index = tick_index - segment_index
        active = (micro_index >= 0) & (micro_index < batch_count)
        buffer_slot = jnp.clip(micro_index, 0, batch_count - 1)
        source = jnp.where(
            segment_index == 0,
            lax.dynamic_index_in_dim(inputs, buffer_slot, 0, keepdims=False),
            incoming,
        )
        result = advance(source, buffer_slot, active)
        current = lax.dynamic_index_in_dim(states, buffer_slot, 0, keepdims=False)
        states = lax.dynamic_update_index_in_dim(
            states, jnp.where(active, result, current), buffer_slot, 0
        )
        incoming = passed_along(result, "segment", 1)
        return (incoming, states)

    start_state = (
        jnp.zeros(inputs.shape[1:], jnp.bfloat16),
        jnp.zeros((batch_count, block_len, width_half), jnp.bfloat16),
    )
    final_state = lax.fori_loop(0, segment_count + batch_count - 1, relay_tick, start_state)
    return final_state[1][None]


def solution(mesh):
    return jax.shard_map(
        per_device,
        mesh=mesh,
        in_specs=(
            P(None, "seq", "tp"),
            P(),
            P(),
            P("segment", None),
            P("segment", "seq", "tp"),
            P("segment", None, "tp"),
            P("segment", None, "tp"),
            P("segment", "tp", "seq"),
        ),
        out_specs=P("segment", None, "seq", "tp"),
        check_vma=False,
    )
```

profile of v0, /device:TPU:1, one launch (start us, length us, event | category | flops | bytes accessed | tf_op | source)
XLA Modules:
  0.0 725.9 jit_solution(5875920562288065173)
XLA Ops:
  8.0 92.3 %all-gather.6.cloned.1.call-done = bf16[1,1024,2688]{1,2,0:T(8,128)(2,1)} async-done(((bf16[1,1024,336]{1,2,0:T(8,128)(2,1)}), bf16[1,1024,2688]{1,2,0:T(8,128)(2,1)}) %all-gather.6.cloned.1.call-update) | async-done | bytes 5505040 | tf_op jit(solution)/shard_map/all_gather | solution.py:61
  100.3 8.0 %copy.41 = bf16[1024,2688]{1,0:T(8,128)(2,1)} copy(bf16[1024,2688]{0,1:T(8,128)(2,1)} %bitcast.68) | data formatting | bytes 11010048
  108.4 81.8 %all-gather.4.cloned.1.call-done = bf16[1,2688,1024]{2,1,0:T(8,128)(2,1)} async-done(((bf16[1,336,1024]{2,1,0:T(8,128)(2,1)}), bf16[1,2688,1024]{2,1,0:T(8,128)(2,1)}) %all-gather.4.cloned.1.call-update) | async-done | bytes 5505040 | tf_op jit(solution)/shard_map/all_gather | solution.py:60
  191.4 527.6 %while.18 = (s32[]{:T(128)}, bf16[256,1344]{0,1:T(8,128)(2,1)S(1)}, bf16[2,256,1344]{1,2,0:T(8,128)(2,1)}, pred[]{:T(512)}, s32[]{:T(128)}, /*index=5*/bf16[2,25...) while((s32[]{:T(128)}, bf16[256,1344]{0,1:T(8,128)(2,1)S(1)}, ...), condition=%wide.region_13.14_spmd.clone.clone, body=%wide.region_0.13_spmd.clone.clone.sunk | while | flops 5606286336 | bytes 155790400 | solution.py:202
  191.5 2.0 bitcast_select_fusion.5
  193.6 24.2 %all-gather.8.cloned.1.call-done = bf16[256,2688]{0,1:T(8,128)(2,1)} async-done(((bf16[256,1344]{0,1:T(8,128)(2,1)}), bf16[256,2688]{0,1:T(8,128)(2,1)}) %all-gather.8.cloned.1.call-update) | async-done | bytes 1376272 | tf_op jit(solution)/shard_map/while/body/eval_jaxpr/all_gather | solution.py:175
  218.1 4.0 collective-permute-start.4
  222.2 4.0 collective-permute-start.5
  227.5 2.8 collective-permute-start.7
  231.7 3.4 collective-permute-start.1
  238.0 2.9 collective-permute-start.3
  247.2 2.2 copy.75
  250.8 105.8 %reduce-scatter.6.cloned.1.call-done = f32[1344,256]{1,0:T(8,128)} async-done(((f32[2688,256]{1,0:T(8,128)}), f32[1344,256]{1,0:T(8,128)}) %reduce-scatter.6.cloned.1.call-update) | async-done | bytes 1376272 | tf_op jit(solution)/shard_map/while
  359.4 2.7 collective-permute-done.8
  362.2 2.0 bitcast_select_fusion.5
  364.3 24.6 %all-gather.8.cloned.1.call-done = bf16[256,2688]{0,1:T(8,128)(2,1)} async-done(((bf16[256,1344]{0,1:T(8,128)(2,1)}), bf16[256,2688]{0,1:T(8,128)(2,1)}) %all-gather.8.cloned.1.call-update) | async-done | bytes 1376272 | tf_op jit(solution)/shard_map/while/body/eval_jaxpr/all_gather | solution.py:175
  388.9 14.1 %conditional.8 = (bf16[256,4,2,128]{3,2,1,0:T(2,128)(2,1)S(1)}, bf16[256,512]{1,0:T(8,128)(2,1)S(1)}, bf16[256,512]{0,1:T(8,128)(2,1)S(1)}) conditional(s32[]{:T(128)} %convert_element_type.86, () %tuple.84, (bf16[256,2688]{0,1:T(8,128)(2,1)}, f32[1,2688]{1,0:T(1,128)S(1)}, bf16[2688,1024]{1,0:T(8,128)(2,1)}, s32[256]{0:T(256)S(1)}, ...), branch_computations={%region_1.1_spmd, %region_2.3_spmd} | conditional | flops 2832187904 | bytes 40695864 | solution.py:170
  391.1 2.7 fusion.31
  395.5 4.3 convolution_bitcast_fusion
  403.0 4.0 collective-permute-start.4
  407.1 4.0 collective-permute-start.5
  412.4 2.8 collective-permute-start.7
  416.6 11.8 %collective-permute-start.1 = (bf16[256,512]{1,0:T(8,128)(2,1)S(1)}, bf16[256,512]{1,0:T(8,128)(2,1)S(1)}, u32[]{:S(2)}, u32[]{:S(2)}) collective-permute-start(bf16[256,512]{1,0:T(8,128)(2,1)S(1)} %get-tuple-element.695), channel_id=1, source_target_pairs={{0,6},{2,8},{4,10},{6,12},{8,14},{1,7},{3,9},{5,11},{7,13},{9,15},... | collective-permute-start | bytes 786440 | tf_op jit(solution)/shard_map/while/body/eval_jaxpr/ppermute | solution.py:20
  431.2 6.3 collective-permute-start.3
  443.5 23.8 %conditional.9 = (f32[256,2688]{1,0:T(8,128)S(1)}) conditional(s32[]{:T(128)} %convert_element_type.86, () %tuple.83, (s32[]{:T(128)}, s32[256]{0:T(256)S(1)}, s32[256]{0:T(256)S(1)}, s32[256]{0:T(256)S(1)}, s32[]{:T(128)}, /*index=5*/s32[2]{0:T(128)}, s32[2,8]{1,0:T(2,128)}, s32[256]{0:T(256)S(1)}, bf16[1280,512]{1,0:T(8,128)(2,1)}, ...), branch_computations={%region_4.4_spmd, %region_5.11_spmd} | conditional | flops 2772377600 | bytes 53291148 | solution.py:172
  449.7 2.7 reshape.148
  452.4 7.2 fusion.36
  459.6 5.4 fusion.12
  467.3 2.2 copy.75
  470.9 70.6 %reduce-scatter.6.cloned.1.call-done = f32[1344,256]{1,0:T(8,128)} async-done(((f32[2688,256]{1,0:T(8,128)}), f32[1344,256]{1,0:T(8,128)}) %reduce-scatter.6.cloned.1.call-update) | async-done | bytes 1376272 | tf_op jit(solution)/shard_map/while
  544.4 2.7 collective-permute-done.8
  547.1 2.0 bitcast_select_fusion.5
  549.2 24.8 %all-gather.8.cloned.1.call-done = bf16[256,2688]{0,1:T(8,128)(2,1)} async-done(((bf16[256,1344]{0,1:T(8,128)(2,1)}), bf16[256,2688]{0,1:T(8,128)(2,1)}) %all-gather.8.cloned.1.call-update) | async-done | bytes 1376272 | tf_op jit(solution)/shard_map/while/body/eval_jaxpr/all_gather | solution.py:175
  574.0 14.1 %conditional.8 = (bf16[256,4,2,128]{3,2,1,0:T(2,128)(2,1)S(1)}, bf16[256,512]{1,0:T(8,128)(2,1)S(1)}, bf16[256,512]{0,1:T(8,128)(2,1)S(1)}) conditional(s32[]{:T(128)} %convert_element_type.86, () %tuple.84, (bf16[256,2688]{0,1:T(8,128)(2,1)}, f32[1,2688]{1,0:T(1,128)S(1)}, bf16[2688,1024]{1,0:T(8,128)(2,1)}, s32[256]{0:T(256)S(1)}, ...), branch_computations={%region_1.1_spmd, %region_2.3_spmd} | conditional | flops 2832187904 | bytes 40695864 | solution.py:170
  576.2 2.7 fusion.31
  580.6 4.3 convolution_bitcast_fusion
  588.2 4.0 collective-permute-start.4
  592.2 4.0 collective-permute-start.5
  597.6 2.8 collective-permute-start.7
  601.7 10.6 %collective-permute-start.1 = (bf16[256,512]{1,0:T(8,128)(2,1)S(1)}, bf16[256,512]{1,0:T(8,128)(2,1)S(1)}, u32[]{:S(2)}, u32[]{:S(2)}) collective-permute-start(bf16[256,512]{1,0:T(8,128)(2,1)S(1)} %get-tuple-element.695), channel_id=1, source_target_pairs={{0,6},{2,8},{4,10},{6,12},{8,14},{1,7},{3,9},{5,11},{7,13},{9,15},... | collective-permute-start | bytes 786440 | tf_op jit(solution)/shard_map/while/body/eval_jaxpr/ppermute | solution.py:20
  615.2 5.7 collective-permute-start.3
  626.9 23.8 %conditional.9 = (f32[256,2688]{1,0:T(8,128)S(1)}) conditional(s32[]{:T(128)} %convert_element_type.86, () %tuple.83, (s32[]{:T(128)}, s32[256]{0:T(256)S(1)}, s32[256]{0:T(256)S(1)}, s32[256]{0:T(256)S(1)}, s32[]{:T(128)}, /*index=5*/s32[2]{0:T(128)}, s32[2,8]{1,0:T(2,128)}, s32[256]{0:T(256)S(1)}, bf16[1280,512]{1,0:T(8,128)(2,1)}, ...), branch_computations={%region_4.4_spmd, %region_5.11_spmd} | conditional | flops 2772377600 | bytes 53291148 | solution.py:172
  633.1 2.7 reshape.148
  635.8 7.2 fusion.36
  643.0 5.4 fusion.12
  650.7 2.2 copy.75
  654.3 59.1 %reduce-scatter.6.cloned.1.call-done = f32[1344,256]{1,0:T(8,128)} async-done(((f32[2688,256]{1,0:T(8,128)}), f32[1344,256]{1,0:T(8,128)}) %reduce-scatter.6.cloned.1.call-update) | async-done | bytes 1376272 | tf_op jit(solution)/shard_map/while
  716.3 2.7 collective-permute-done.8
  (200 shorter events, 81.8 us)
Async XLA Ops:
  6.5 93.8 %all-gather.6.cloned.1.call-start = ((), (), s32[]{:S(2)}) async-start(), calls=%async_computation.2 | async-start | bytes 6193152 | tf_op jit(solution)/shard_map/all_gather | solution.py:61
  7.3 182.9 %all-gather.4.cloned.1.call-start = ((), (), s32[]{:S(2)}) async-start(), calls=%async_computation.1 | async-start | bytes 6193152 | tf_op jit(solution)/shard_map/all_gather | solution.py:60
  108.3 83.1 %copy-start.3 = (f32[1,2688]{1,0:T(1,128)S(1)}, f32[1,2688]{1,0:T(1,128)}, u32[]{:S(2)}) copy-start(f32[1,2688]{1,0:T(1,128)} %param.17) | copy-start | bytes 32260
  191.4 26.4 %all-gather.8.cloned.1.call-start = ((), (), s32[]{:S(2)}) async-start(), calls=%async_computation.3 | async-start | bytes 2064384 | tf_op jit(solution)/shard_map/while/body/eval_jaxpr/all_gather | solution.py:175
  193.5 163.0 %reduce-scatter.6.cloned.1.call-start = ((), (), s32[]{:S(2)}) async-start(), calls=%async_computation.4 | async-start | bytes 4128768 | tf_op jit(solution)/shard_map/while
  218.1 13.6 %collective-permute-start.4 = (bf16[256,512]{0,1:T(8,128)(2,1)S(1)}, bf16[256,512]{0,1:T(8,128)(2,1)S(1)}, u32[]{:S(2)}, u32[]{:S(2)}) collective-permute-start(bf16[256,512]{0,1:T(8,128)(2,1)S(1)} %get-tuple-element.697), channel_id=1, source_target_pairs={{0,8},{2,10},{4,12},{6,14},{1,9},{3,11},{5,13},{7,15},{16,24},{18,... | collective-permute-start | bytes 786440 | tf_op jit(solution)/shard_map/while/body/eval_jaxpr/ppermute | solution.py:20
  222.2 13.7 %collective-permute-start.5 = (bf16[256,512]{0,1:T(8,128)(2,1)S(1)}, bf16[256,512]{0,1:T(8,128)(2,1)S(1)}, u32[]{:S(2)}, u32[]{:S(2)}) collective-permute-start(bf16[256,512]{0,1:T(8,128)(2,1)S(1)} %get-tuple-element.697), channel_id=1, source_target_pairs={{0,6},{2,8},{4,10},{6,12},{8,14},{1,7},{3,9},{5,11},{7,13},{9,15},... | collective-permute-start | bytes 786440 | tf_op jit(solution)/shard_map/while/body/eval_jaxpr/ppermute | solution.py:20
  226.2 11.7 %collective-permute-start.6 = (bf16[256,512]{0,1:T(8,128)(2,1)S(1)}, bf16[256,512]{0,1:T(8,128)(2,1)S(1)}, u32[]{:S(2)}, u32[]{:S(2)}) collective-permute-start(bf16[256,512]{0,1:T(8,128)(2,1)S(1)} %get-tuple-element.697), channel_id=1, source_target_pairs={{0,4},{2,6},{4,8},{6,10},{8,12},{10,14},{1,5},{3,7},{5,9},{7,11},{... | collective-permute-start | bytes 786440 | tf_op jit(solution)/shard_map/while/body/eval_jaxpr/ppermute | solution.py:20
  227.5 14.1 %collective-permute-start.7 = (bf16[256,512]{0,1:T(8,128)(2,1)S(1)}, bf16[256,512]{0,1:T(8,128)(2,1)S(1)}, u32[]{:S(2)}, u32[]{:S(2)}) collective-permute-start(bf16[256,512]{0,1:T(8,128)(2,1)S(1)} %get-tuple-element.697), channel_id=1, source_target_pairs={{0,2},{2,4},{4,6},{6,8},{8,10},{10,12},{12,14},{1,3},{3,5},{5,7},{... | collective-permute-start | bytes 786440 | tf_op jit(solution)/shard_map/while/body/eval_jaxpr/ppermute | solution.py:20
  230.4 12.9 %collective-permute-start = (bf16[256,512]{1,0:T(8,128)(2,1)S(1)}, bf16[256,512]{1,0:T(8,128)(2,1)S(1)}, u32[]{:S(2)}, u32[]{:S(2)}) collective-permute-start(bf16[256,512]{1,0:T(8,128)(2,1)S(1)} %get-tuple-element.695), channel_id=1, source_target_pairs={{0,8},{2,10},{4,12},{6,14},{1,9},{3,11},{5,13},{7,15},{16,24},{18,... | collective-permute-start | bytes 786440 | tf_op jit(solution)/shard_map/while/body/eval_jaxpr/ppermute | solution.py:20
  231.7 12.3 %collective-permute-start.1 = (bf16[256,512]{1,0:T(8,128)(2,1)S(1)}, bf16[256,512]{1,0:T(8,128)(2,1)S(1)}, u32[]{:S(2)}, u32[]{:S(2)}) collective-permute-start(bf16[256,512]{1,0:T(8,128)(2,1)S(1)} %get-tuple-element.695), channel_id=1, source_target_pairs={{0,6},{2,8},{4,10},{6,12},{8,14},{1,7},{3,9},{5,11},{7,13},{9,15},... | collective-permute-start | bytes 786440 | tf_op jit(solution)/shard_map/while/body/eval_jaxpr/ppermute | solution.py:20
  235.9 8.9 %collective-permute-start.2 = (bf16[256,512]{1,0:T(8,128)(2,1)S(1)}, bf16[256,512]{1,0:T(8,128)(2,1)S(1)}, u32[]{:S(2)}, u32[]{:S(2)}) collective-permute-start(bf16[256,512]{1,0:T(8,128)(2,1)S(1)} %get-tuple-element.695), channel_id=1, source_target_pairs={{0,4},{2,6},{4,8},{6,10},{8,12},{10,14},{1,5},{3,7},{5,9},{7,11},{... | collective-permute-start | bytes 786440 | tf_op jit(solution)/shard_map/while/body/eval_jaxpr/ppermute | solution.py:20
  238.0 7.6 %collective-permute-start.3 = (bf16[256,512]{1,0:T(8,128)(2,1)S(1)}, bf16[256,512]{1,0:T(8,128)(2,1)S(1)}, u32[]{:S(2)}, u32[]{:S(2)}) collective-permute-start(bf16[256,512]{1,0:T(8,128)(2,1)S(1)} %get-tuple-element.695), channel_id=1, source_target_pairs={{0,2},{2,4},{4,6},{6,8},{8,10},{10,12},{12,14},{1,3},{3,5},{5,7},{... | collective-permute-start | bytes 786440 | tf_op jit(solution)/shard_map/while/body/eval_jaxpr/ppermute | solution.py:20
  249.4 107.1 %copy-start = (bf16[256,1344]{0,1:T(8,128)(2,1)S(1)}, bf16[256,1344]{0,1:T(8,128)(2,1)}, u32[]{:S(2)}) copy-start(bf16[256,1344]{0,1:T(8,128)(2,1)} %bitcast_select_fusion.5) | copy-start | bytes 2064388 | tf_op jit(solution)/shard_map/while
  358.1 4.1 copy-start.2
  358.1 4.0 collective-permute-start.8
  362.2 26.7 %all-gather.8.cloned.1.call-start = ((), (), s32[]{:S(2)}) async-start(), calls=%async_computation.3 | async-start | bytes 2064384 | tf_op jit(solution)/shard_map/while/body/eval_jaxpr/all_gather | solution.py:175
  364.2 177.3 %reduce-scatter.6.cloned.1.call-start = ((), (), s32[]{:S(2)}) async-start(), calls=%async_computation.4 | async-start | bytes 4128768 | tf_op jit(solution)/shard_map/while
  400.0 2.0 copy-start.4
  403.0 13.6 %collective-permute-start.4 = (bf16[256,512]{0,1:T(8,128)(2,1)S(1)}, bf16[256,512]{0,1:T(8,128)(2,1)S(1)}, u32[]{:S(2)}, u32[]{:S(2)}) collective-permute-start(bf16[256,512]{0,1:T(8,128)(2,1)S(1)} %get-tuple-element.697), channel_id=1, source_target_pairs={{0,8},{2,10},{4,12},{6,14},{1,9},{3,11},{5,13},{7,15},{16,24},{18,... | collective-permute-start | bytes 786440 | tf_op jit(solution)/shard_map/while/body/eval_jaxpr/ppermute | solution.py:20
  407.1 22.0 %collective-permute-start.5 = (bf16[256,512]{0,1:T(8,128)(2,1)S(1)}, bf16[256,512]{0,1:T(8,128)(2,1)S(1)}, u32[]{:S(2)}, u32[]{:S(2)}) collective-permute-start(bf16[256,512]{0,1:T(8,128)(2,1)S(1)} %get-tuple-element.697), channel_id=1, source_target_pairs={{0,6},{2,8},{4,10},{6,12},{8,14},{1,7},{3,9},{5,11},{7,13},{9,15},... | collective-permute-start | bytes 786440 | tf_op jit(solution)/shard_map/while/body/eval_jaxpr/ppermute | solution.py:20
  411.1 20.1 %collective-permute-start.6 = (bf16[256,512]{0,1:T(8,128)(2,1)S(1)}, bf16[256,512]{0,1:T(8,128)(2,1)S(1)}, u32[]{:S(2)}, u32[]{:S(2)}) collective-permute-start(bf16[256,512]{0,1:T(8,128)(2,1)S(1)} %get-tuple-element.697), channel_id=1, source_target_pairs={{0,4},{2,6},{4,8},{6,10},{8,12},{10,14},{1,5},{3,7},{5,9},{7,11},{... | collective-permute-start | bytes 786440 | tf_op jit(solution)/shard_map/while/body/eval_jaxpr/ppermute | solution.py:20
  412.4 25.9 %collective-permute-start.7 = (bf16[256,512]{0,1:T(8,128)(2,1)S(1)}, bf16[256,512]{0,1:T(8,128)(2,1)S(1)}, u32[]{:S(2)}, u32[]{:S(2)}) collective-permute-start(bf16[256,512]{0,1:T(8,128)(2,1)S(1)} %get-tuple-element.697), channel_id=1, source_target_pairs={{0,2},{2,4},{4,6},{6,8},{8,10},{10,12},{12,14},{1,3},{3,5},{5,7},{... | collective-permute-start | bytes 786440 | tf_op jit(solution)/shard_map/while/body/eval_jaxpr/ppermute | solution.py:20
  415.3 24.6 %collective-permute-start = (bf16[256,512]{1,0:T(8,128)(2,1)S(1)}, bf16[256,512]{1,0:T(8,128)(2,1)S(1)}, u32[]{:S(2)}, u32[]{:S(2)}) collective-permute-start(bf16[256,512]{1,0:T(8,128)(2,1)S(1)} %get-tuple-element.695), channel_id=1, source_target_pairs={{0,8},{2,10},{4,12},{6,14},{1,9},{3,11},{5,13},{7,15},{16,24},{18,... | collective-permute-start | bytes 786440 | tf_op jit(solution)/shard_map/while/body/eval_jaxpr/ppermute | solution.py:20
  416.6 24.0 %collective-permute-start.1 = (bf16[256,512]{1,0:T(8,128)(2,1)S(1)}, bf16[256,512]{1,0:T(8,128)(2,1)S(1)}, u32[]{:S(2)}, u32[]{:S(2)}) collective-permute-start(bf16[256,512]{1,0:T(8,128)(2,1)S(1)} %get-tuple-element.695), channel_id=1, source_target_pairs={{0,6},{2,8},{4,10},{6,12},{8,14},{1,7},{3,9},{5,11},{7,13},{9,15},... | collective-permute-start | bytes 786440 | tf_op jit(solution)/shard_map/while/body/eval_jaxpr/ppermute | solution.py:20
  429.1 12.2 %collective-permute-start.2 = (bf16[256,512]{1,0:T(8,128)(2,1)S(1)}, bf16[256,512]{1,0:T(8,128)(2,1)S(1)}, u32[]{:S(2)}, u32[]{:S(2)}) collective-permute-start(bf16[256,512]{1,0:T(8,128)(2,1)S(1)} %get-tuple-element.695), channel_id=1, source_target_pairs={{0,4},{2,6},{4,8},{6,10},{8,12},{10,14},{1,5},{3,7},{5,9},{7,11},{... | collective-permute-start | bytes 786440 | tf_op jit(solution)/shard_map/while/body/eval_jaxpr/ppermute | solution.py:20
  431.2 10.9 %collective-permute-start.3 = (bf16[256,512]{1,0:T(8,128)(2,1)S(1)}, bf16[256,512]{1,0:T(8,128)(2,1)S(1)}, u32[]{:S(2)}, u32[]{:S(2)}) collective-permute-start(bf16[256,512]{1,0:T(8,128)(2,1)S(1)} %get-tuple-element.695), channel_id=1, source_target_pairs={{0,2},{2,4},{4,6},{6,8},{8,10},{10,12},{12,14},{1,3},{3,5},{5,7},{... | collective-permute-start | bytes 786440 | tf_op jit(solution)/shard_map/while/body/eval_jaxpr/ppermute | solution.py:20
  459.6 5.6 slice-start
  459.6 5.9 slice-start.1
  469.5 72.0 %copy-start = (bf16[256,1344]{0,1:T(8,128)(2,1)S(1)}, bf16[256,1344]{0,1:T(8,128)(2,1)}, u32[]{:S(2)}) copy-start(bf16[256,1344]{0,1:T(8,128)(2,1)} %bitcast_select_fusion.5) | copy-start | bytes 2064388 | tf_op jit(solution)/shard_map/while
  543.1 4.1 copy-start.2
  543.1 4.0 collective-permute-start.8
  547.1 26.9 %all-gather.8.cloned.1.call-start = ((), (), s32[]{:S(2)}) async-start(), calls=%async_computation.3 | async-start | bytes 2064384 | tf_op jit(solution)/shard_map/while/body/eval_jaxpr/all_gather | solution.py:175
  549.2 164.2 %reduce-scatter.6.cloned.1.call-start = ((), (), s32[]{:S(2)}) async-start(), calls=%async_computation.4 | async-start | bytes 4128768 | tf_op jit(solution)/shard_map/while
  585.1 2.0 copy-start.4
  588.2 13.6 %collective-permute-start.4 = (bf16[256,512]{0,1:T(8,128)(2,1)S(1)}, bf16[256,512]{0,1:T(8,128)(2,1)S(1)}, u32[]{:S(2)}, u32[]{:S(2)}) collective-permute-start(bf16[256,512]{0,1:T(8,128)(2,1)S(1)} %get-tuple-element.697), channel_id=1, source_target_pairs={{0,8},{2,10},{4,12},{6,14},{1,9},{3,11},{5,13},{7,15},{16,24},{18,... | collective-permute-start | bytes 786440 | tf_op jit(solution)/shard_map/while/body/eval_jaxpr/ppermute | solution.py:20
  592.2 20.9 %collective-permute-start.5 = (bf16[256,512]{0,1:T(8,128)(2,1)S(1)}, bf16[256,512]{0,1:T(8,128)(2,1)S(1)}, u32[]{:S(2)}, u32[]{:S(2)}) collective-permute-start(bf16[256,512]{0,1:T(8,128)(2,1)S(1)} %get-tuple-element.697), channel_id=1, source_target_pairs={{0,6},{2,8},{4,10},{6,12},{8,14},{1,7},{3,9},{5,11},{7,13},{9,15},... | collective-permute-start | bytes 786440 | tf_op jit(solution)/shard_map/while/body/eval_jaxpr/ppermute | solution.py:20
  596.3 18.9 %collective-permute-start.6 = (bf16[256,512]{0,1:T(8,128)(2,1)S(1)}, bf16[256,512]{0,1:T(8,128)(2,1)S(1)}, u32[]{:S(2)}, u32[]{:S(2)}) collective-permute-start(bf16[256,512]{0,1:T(8,128)(2,1)S(1)} %get-tuple-element.697), channel_id=1, source_target_pairs={{0,4},{2,6},{4,8},{6,10},{8,12},{10,14},{1,5},{3,7},{5,9},{7,11},{... | collective-permute-start | bytes 786440 | tf_op jit(solution)/shard_map/while/body/eval_jaxpr/ppermute | solution.py:20
  597.6 24.1 %collective-permute-start.7 = (bf16[256,512]{0,1:T(8,128)(2,1)S(1)}, bf16[256,512]{0,1:T(8,128)(2,1)S(1)}, u32[]{:S(2)}, u32[]{:S(2)}) collective-permute-start(bf16[256,512]{0,1:T(8,128)(2,1)S(1)} %get-tuple-element.697), channel_id=1, source_target_pairs={{0,2},{2,4},{4,6},{6,8},{8,10},{10,12},{12,14},{1,3},{3,5},{5,7},{... | collective-permute-start | bytes 786440 | tf_op jit(solution)/shard_map/while/body/eval_jaxpr/ppermute | solution.py:20
  600.4 22.8 %collective-permute-start = (bf16[256,512]{1,0:T(8,128)(2,1)S(1)}, bf16[256,512]{1,0:T(8,128)(2,1)S(1)}, u32[]{:S(2)}, u32[]{:S(2)}) collective-permute-start(bf16[256,512]{1,0:T(8,128)(2,1)S(1)} %get-tuple-element.695), channel_id=1, source_target_pairs={{0,8},{2,10},{4,12},{6,14},{1,9},{3,11},{5,13},{7,15},{16,24},{18,... | collective-permute-start | bytes 786440 | tf_op jit(solution)/shard_map/while/body/eval_jaxpr/ppermute | solution.py:20
  601.7 22.3 %collective-permute-start.1 = (bf16[256,512]{1,0:T(8,128)(2,1)S(1)}, bf16[256,512]{1,0:T(8,128)(2,1)S(1)}, u32[]{:S(2)}, u32[]{:S(2)}) collective-permute-start(bf16[256,512]{1,0:T(8,128)(2,1)S(1)} %get-tuple-element.695), channel_id=1, source_target_pairs={{0,6},{2,8},{4,10},{6,12},{8,14},{1,7},{3,9},{5,11},{7,13},{9,15},... | collective-permute-start | bytes 786440 | tf_op jit(solution)/shard_map/while/body/eval_jaxpr/ppermute | solution.py:20
  613.1 11.6 %collective-permute-start.2 = (bf16[256,512]{1,0:T(8,128)(2,1)S(1)}, bf16[256,512]{1,0:T(8,128)(2,1)S(1)}, u32[]{:S(2)}, u32[]{:S(2)}) collective-permute-start(bf16[256,512]{1,0:T(8,128)(2,1)S(1)} %get-tuple-element.695), channel_id=1, source_target_pairs={{0,4},{2,6},{4,8},{6,10},{8,12},{10,14},{1,5},{3,7},{5,9},{7,11},{... | collective-permute-start | bytes 786440 | tf_op jit(solution)/shard_map/while/body/eval_jaxpr/ppermute | solution.py:20
  615.2 10.3 %collective-permute-start.3 = (bf16[256,512]{1,0:T(8,128)(2,1)S(1)}, bf16[256,512]{1,0:T(8,128)(2,1)S(1)}, u32[]{:S(2)}, u32[]{:S(2)}) collective-permute-start(bf16[256,512]{1,0:T(8,128)(2,1)S(1)} %get-tuple-element.695), channel_id=1, source_target_pairs={{0,2},{2,4},{4,6},{6,8},{8,10},{10,12},{12,14},{1,3},{3,5},{5,7},{... | collective-permute-start | bytes 786440 | tf_op jit(solution)/shard_map/while/body/eval_jaxpr/ppermute | solution.py:20
  643.0 5.6 slice-start
  643.0 5.9 slice-start.1
  652.9 60.5 %copy-start = (bf16[256,1344]{0,1:T(8,128)(2,1)S(1)}, bf16[256,1344]{0,1:T(8,128)(2,1)}, u32[]{:S(2)}) copy-start(bf16[256,1344]{0,1:T(8,128)(2,1)} %bitcast_select_fusion.5) | copy-start | bytes 2064388 | tf_op jit(solution)/shard_map/while
  715.0 4.1 copy-start.2
  715.0 4.0 collective-permute-start.8
  (3 other events, 4.0 us)
Sparse Core Ops, SparseCore 0:
  9.5 90.7 all-gather.5
  102.5 87.6 all-gather.3
  193.8 23.9 all-gather.7
  249.5 106.9 reduce-scatter.5
  364.3 24.4 all-gather.7
  469.6 71.7 reduce-scatter.5
  549.5 24.4 all-gather.7
  653.0 60.2 reduce-scatter.5
where the time goes:
time: 728 us; the launch traced here: 726 us
  waiting for transfers between devices  493 us (68%)
  starting transfers between devices  89.3 us (12%)
  local copies, waits for them, and re-layouts  54.1 us (7%)
  matrix products  44.6 us (6%)
  other arithmetic  30.5 us (4%)
  between operations  13.4 us (2%)
    while x9, waiting for transfers between devices  236 us
    all_gather x1, waiting for transfers between devices, per_device(): output_cols = lax.all_gather(out_weight, 'seq', axis=2, tiled=True)[0]  92.3 us
    ppermute x27, starting transfers between devices, passed_along(): lax.ppermute(value, axis, [(source, source + steps) for source in range(i...  89.1 us
    all_gather x1, waiting for transfers between devices, per_device(): query_rows = lax.all_gather(query_weight, 'seq', axis=1, tiled=True)[0]  81.8 us
    all_gather x3, waiting for transfers between devices, advance(): full_state = lax.all_gather(state_half, 'tp', axis=1, tiled=True)  73.5 us
    while x45, local copies, waits for them, and re-layouts  28.6 us
  transfers between devices with their start and end apart: 35, of which 12 were waited for; matrix products, arithmetic and copies ran while one was open for 4% of the time, Pallas kernels for 0%

commit v1 on v0

v1 whole, which is shorter than its diff:
```python
import functools
import math

import jax
import jax.numpy as jnp
from jax import lax
from jax.experimental import pallas as pl
from jax.experimental.pallas import tpu as pltpu
from jax.sharding import PartitionSpec as P

HEADS = 16
KV = 8
HEAD_DIM = 128
WINDOW = 1024
GROUP = HEADS // KV
LAYERS = 2

norm_epsilon = 1e-06
hidden = -1e30
VMEM_LIMIT = 48 * 1024 * 1024

SWAP = ((0, 1), (1, 0))


def ring_order(count):
    return list(range(0, count, 2)) + list(range(count - 1, 0, -2))


def ring_position(index, count):
    return jnp.where(index % 2 == 0, index // 2, count - 1 - index // 2)


def ring_member(position, count):
    position = lax.rem(position + 2 * count, count)
    return jnp.where(position < count // 2, 2 * position, 2 * (count - 1 - position) + 1)


def any_spec():
    return pl.BlockSpec(memory_space=pl.ANY)


def vmem_spec():
    return pl.BlockSpec(memory_space=pltpu.VMEM)


def smem_spec():
    return pl.BlockSpec(memory_space=pltpu.SMEM)


def call(kernel, out_shape, in_specs, scratch, flops, moved, name, exps=0):
    outs = jax.tree.map(lambda _: vmem_spec(), out_shape)
    return pl.pallas_call(
        kernel,
        out_shape=out_shape,
        in_specs=in_specs,
        out_specs=outs,
        scratch_shapes=scratch,
        compiler_params=pltpu.CompilerParams(vmem_limit_bytes=VMEM_LIMIT),
        cost_estimate=pl.CostEstimate(flops=flops, bytes_accessed=moved, transcendentals=exps),
        name=name,
    )


def turned(heads, cosine, sine):
    return heads * cosine + pltpu.roll(heads, HEAD_DIM // 2, 1) * sine


def key_value_kernel(
    layer, own, other, gain, cosine, sine, key_own, key_came, value_own, value_came,
    kv_out, normed_out, weights, normed, sems,
):
    here = lax.axis_index("segment") == layer
    half = lax.axis_index("tp")
    width = own.shape[1]
    columns = key_own.shape[1]
    step = 256 if columns % 256 == 0 else columns
    parts = columns // step

    def copies(key, value):
        made = []
        for which, source in enumerate((key, value)):
            for part in range(parts):
                made.append(
                    pltpu.make_async_copy(
                        source.at[:, pl.ds(part * step, step)],
                        weights.at[which * parts + part],
                        sems.at[which * parts + part],
                    )
                )
        return made

    @pl.when(here)
    def _():
        for copy in copies(key_own, value_own):
            copy.start()

    @pl.when(jnp.logical_not(here))
    def _():
        for copy in copies(key_came, value_came):
            copy.start()

    mine = own[...].astype(jnp.float32)
    theirs = other[...].astype(jnp.float32)
    total = jnp.sum(mine * mine, axis=1, keepdims=True)
    total += jnp.sum(theirs * theirs, axis=1, keepdims=True)
    scale = lax.rsqrt(total / (2 * width) + norm_epsilon)
    normed[0] = (mine * scale * gain[pl.ds(half, 1), :]).astype(jnp.bfloat16)
    normed[1] = (theirs * scale * gain[pl.ds(1 - half, 1), :]).astype(jnp.bfloat16)
    chunks = normed_out.shape[0] // 2
    depth = normed_out.shape[2]
    for part in range(chunks):
        normed_out[half * chunks + part] = normed[0, :, part * depth : (part + 1) * depth]
        normed_out[(1 - half) * chunks + part] = normed[1, :, part * depth : (part + 1) * depth]

    waits = copies(key_own, value_own)
    for index, copy in enumerate(waits):
        copy.wait()
        result = jnp.dot(
            normed[0],
            weights[index, pl.ds(pl.multiple_of(half * width, 16), width), :],
            preferred_element_type=jnp.float32,
        )
        result += jnp.dot(
            normed[1],
            weights[index, pl.ds(pl.multiple_of((1 - half) * width, 16), width), :],
            preferred_element_type=jnp.float32,
        )
        base = index * step
        if index < parts:
            for head in range(step // HEAD_DIM):
                rows = result[:, head * HEAD_DIM : (head + 1) * HEAD_DIM]
                kv_out[:, base + head * HEAD_DIM : base + (head + 1) * HEAD_DIM] = turned(
                    rows, cosine[...], sine[...]
                ).astype(jnp.bfloat16)
        else:
            kv_out[:, base : base + step] = result.astype(jnp.bfloat16)


def key_value(layer, own, other, gain, tables, weights, count):
    rows, width = own.shape
    depth, columns = weights[0].shape
    step = 256 if columns % 256 == 0 else columns
    parts = 2 * (columns // step)
    return call(
        functools.partial(key_value_kernel, layer),
        (
            jax.ShapeDtypeStruct((rows, 2 * columns), jnp.bfloat16),
            jax.ShapeDtypeStruct((count, rows, depth // count), jnp.bfloat16),
        ),
        [vmem_spec()] * 5 + [any_spec()] * 4,
        [
            pltpu.VMEM((parts, depth, step), jnp.bfloat16),
            pltpu.VMEM((2, rows, width), jnp.bfloat16),
            pltpu.SemaphoreType.DMA((parts,)),
        ],
        4 * rows * depth * columns,
        4 * depth * columns + 4 * rows * depth,
        "key_value",
    )(own, other, gain, *tables, *weights)


def piece_copy(ref, part, target, sem):
    source = ref.at[part] if ref.shape[0] > 1 else ref.at[0]
    return pltpu.make_async_copy(source, target, sem)


def query_kernel(count, normed, cosine, sine, *refs):
    pieces, (out, weights, sems) = refs[: 2 * count], refs[2 * count :]
    core = lax.axis_index("segment")
    place = ring_position(lax.axis_index("seq"), count)
    copies = [
        piece_copy(piece, 0, weights.at[index], sems.at[index])
        for index, piece in enumerate(pieces)
    ]
    for copy in copies:
        copy.start()
    for side in range(2):
        total = None
        for step in range(count):
            index = side * count + step
            copies[index].wait()
            term = jnp.dot(
                normed[ring_member(place - step, count)],
                weights[index],
                preferred_element_type=jnp.float32,
            )
            total = term if total is None else total + term
        target = core if side == 0 else 1 - core
        for head in range(total.shape[1] // HEAD_DIM):
            cut = slice(head * HEAD_DIM, (head + 1) * HEAD_DIM)
            out[target, :, cut] = turned(total[:, cut], cosine[...], sine[...]).astype(
                jnp.bfloat16
            )


def query(normed, tables, own, came):
    count, rows, depth = normed.shape
    columns = own[0].shape[2]
    return call(
        functools.partial(query_kernel, count),
        jax.ShapeDtypeStruct((2, rows, columns), jnp.bfloat16),
        [vmem_spec()] * 3 + [any_spec()] * (2 * count),
        [
            pltpu.VMEM((2 * count, depth, columns), jnp.bfloat16),
            pltpu.SemaphoreType.DMA((2 * count,)),
        ],
        4 * count * rows * depth * columns,
        4 * count * depth * columns + 2 * count * rows * depth,
        "query",
    )(normed, *tables, *own, *came)


def attend_kernel(reach, lengths, boundary, queries, *refs):
    windows, (out, bias) = refs[: reach + 1], refs[reach + 1 :]
    batch = lax.axis_index("segment")
    seq = lax.axis_index("seq")
    rows = queries.shape[1]
    half_heads = queries.shape[2] // HEAD_DIM
    kv_columns = windows[0].shape[1] // 2
    row_ids = lax.broadcasted_iota(jnp.int32, (rows, rows), 0)
    key_ids = lax.broadcasted_iota(jnp.int32, (rows, rows), 1)
    start = boundary[batch]
    for slot in range(reach + 1):
        distance = reach - slot
        block = seq - distance
        length = jnp.where(block >= 0, lengths[batch, jnp.maximum(block, 0)], 0)
        seen = key_ids < length
        if distance == 0:
            seen &= key_ids <= row_ids
        if distance == reach:
            seen &= key_ids > row_ids + (distance * rows - WINDOW)
        seen &= (row_ids + seq * rows < start) | (key_ids + block * rows >= start)
        bias[slot] = jnp.where(seen, 0.0, hidden)
    own_length = lengths[batch, seq]
    kept = lax.broadcasted_iota(jnp.int32, (rows, 1), 0) < own_length
    factor = math.log2(math.e) * HEAD_DIM ** (-0.5)
    for head in range(2 * half_heads):
        group = head // GROUP
        cut = slice(group * HEAD_DIM, (group + 1) * HEAD_DIM)
        value_cut = slice(kv_columns + group * HEAD_DIM, kv_columns + (group + 1) * HEAD_DIM)
        half, place = head // half_heads, head % half_heads
        query_rows = queries[half, :, place * HEAD_DIM : (place + 1) * HEAD_DIM]
        scores = [
            lax.dot_general(
                query_rows,
                windows[slot][:, cut],
                (((1,), (1,)), ((), ())),
                preferred_element_type=jnp.float32,
            )
            + bias[slot]
            for slot in range(reach + 1)
        ]
        top = scores[0]
        for score in scores[1:]:
            top = jnp.maximum(top, score)
        top = jnp.max(top, axis=1, keepdims=True)
        mixed = None
        total = None
        for slot in range(reach + 1):
            term = jnp.exp2((scores[slot] - top) * factor)
            total = term if total is None else total + term
            product = jnp.dot(
                term.astype(jnp.bfloat16),
                windows[slot][:, value_cut],
                preferred_element_type=jnp.float32,
            )
            mixed = product if mixed is None else mixed + product
        total = jnp.sum(total, axis=1, keepdims=True)
        result = jnp.where(kept, mixed / total, 0.0)
        out[half, :, place * HEAD_DIM : (place + 1) * HEAD_DIM] = result.astype(jnp.bfloat16)


def attend(lengths, boundary, queries, windows):
    reach = len(windows) - 1
    rows = queries.shape[1]
    heads = 2 * queries.shape[2] // HEAD_DIM
    keys = rows * len(windows)
    return call(
        functools.partial(attend_kernel, reach),
        jax.ShapeDtypeStruct(queries.shape, jnp.bfloat16),
        [smem_spec()] * 2 + [vmem_spec()] * (reach + 2),
        [pltpu.VMEM((reach + 1, rows, rows), jnp.float32)],
        4 * heads * rows * keys * HEAD_DIM,
        2 * sum(w.size for w in windows) + 4 * queries.size,
        "attend",
        heads * rows * keys,
    )(lengths, boundary, queries, *windows)


def out_kernel(count, mixed, *refs):
    pieces, (leave, stay, weights, chunks, sems) = refs[: 2 * count], refs[2 * count :]
    core = lax.axis_index("segment")
    half = lax.axis_index("tp")
    place = ring_position(lax.axis_index("seq"), count)
    copies = [
        piece_copy(piece, 1, weights.at[index], sems.at[index])
        for index, piece in enumerate(pieces)
    ]
    for step in range(count):
        copies[step].start()
        copies[count + step].start()
    contract = (((1,), (1,)), ((), ()))
    for step in range(count):
        copies[step].wait()
        copies[count + step].wait()
        result = lax.dot_general(
            mixed[core], weights[step], contract, preferred_element_type=jnp.float32
        )
        result += lax.dot_general(
            mixed[1 - core], weights[count + step], contract, preferred_element_type=jnp.float32
        )
        chunks[ring_member(place - step, count)] = result
    parts = count // 2
    width = chunks.shape[2]
    for part in range(parts):
        cut = slice(part * width, (part + 1) * width)
        stay[:, cut] = chunks[half * parts + part]
        leave[:, cut] = chunks[(1 - half) * parts + part].astype(jnp.bfloat16)


def out_project(mixed, own, came):
    count = len(own)
    rows, columns = mixed.shape[1:]
    depth = own[0].shape[1]
    width = count // 2 * depth
    return call(
        functools.partial(out_kernel, count),
        (
            jax.ShapeDtypeStruct((rows, width), jnp.bfloat16),
            jax.ShapeDtypeStruct((rows, width), jnp.float32),
        ),
        [vmem_spec()] + [any_spec()] * (2 * count),
        [
            pltpu.VMEM((2 * count, depth, columns), jnp.bfloat16),
            pltpu.VMEM((count, rows, depth), jnp.float32),
            pltpu.SemaphoreType.DMA((2 * count,)),
        ],
        4 * count * rows * depth * columns,
        4 * count * depth * columns + 6 * rows * width,
        "out_project",
    )(mixed, *own, *came)


def after(value, *others):
    return lax.optimization_barrier((value, *others))[0]


def per_device(
    inputs, lengths, boundary, attn_gain, query_weight, key_weight, value_weight, out_weight
):
    core = lax.axis_index("segment")
    seq_index = lax.axis_index("seq")
    count = lax.axis_size("seq")
    block_len = inputs.shape[1]
    first_core = core == 0

    def across_chip(value):
        return lax.ppermute(value, "segment", SWAP)

    def across_tp(value):
        return lax.ppermute(value, "tp", SWAP)

    state = lax.dynamic_index_in_dim(inputs, core, 0, keepdims=False)
    state_other = across_tp(state)

    columns = query_weight.shape[2] // 2
    both = jnp.stack([query_weight[0], out_weight[0].T])
    mine = lax.dynamic_slice_in_dim(both, core * columns, columns, 2)
    given = lax.dynamic_slice_in_dim(both, (1 - core) * columns, columns, 2)
    came = across_chip(given)
    shards = [jnp.where(first_core, mine, came), jnp.where(first_core, came, mine)]
    key_value_weights = (
        key_weight[0],
        across_chip(key_weight[0]),
        value_weight[0],
        across_chip(value_weight[0]),
    )
    gain_came = across_chip(attn_gain)
    gains = [
        jnp.where(first_core, attn_gain, gain_came).reshape(2, -1),
        jnp.where(first_core, gain_came, attn_gain).reshape(2, -1),
    ]

    half_dim = HEAD_DIM // 2
    inverse = jnp.exp(
        -math.log(10000.0) * jnp.arange(half_dim, dtype=jnp.float32) * (2.0 / HEAD_DIM)
    )
    slots = seq_index * block_len + jnp.arange(block_len, dtype=jnp.int32)
    angles = slots.astype(jnp.float32)[:, None] * inverse[None, :]
    cosine, sine = jnp.cos(angles), jnp.sin(angles)
    tables = (
        jnp.concatenate([cosine, cosine], axis=1),
        jnp.concatenate([-sine, sine], axis=1),
    )

    order = ring_order(count)
    onward = [(order[i], order[(i + 1) % count]) for i in range(count)]
    back = [(b, a) for a, b in onward]

    def gather(shard):
        forward = [shard]
        backward = [shard]
        for _ in range(count // 2 - 1):
            forward.append(lax.ppermute(forward[-1], "seq", onward))
            backward.append(lax.ppermute(backward[-1], "seq", back))
        far_query = lax.ppermute(forward[-1][:1], "seq", onward)
        far_out = lax.ppermute(backward[-1][1:], "seq", back)
        near = forward + [None] + backward[:0:-1]
        middle = count // 2
        query_own = near[:middle] + [far_query] + near[middle + 1 :]
        out_own = near[:middle] + [far_out] + near[middle + 1 :]
        near_came = [None if piece is None else across_chip(piece) for piece in near]
        query_came = near_came[:middle] + [across_chip(far_query)] + near_came[middle + 1 :]
        out_came = near_came[:middle] + [across_chip(far_out)] + near_came[middle + 1 :]
        return query_own, query_came, out_own, out_came

    up = [(i, i + 2) for i in range(count - 2)]
    beside = [(i, i ^ 1) for i in range(count)]
    even = seq_index % 2 == 0
    reach = max(1, WINDOW // block_len)

    def window(rows):
        evens = [rows]
        odds = []
        for _ in range(reach // 2):
            evens.append(lax.ppermute(evens[-1], "seq", up))
            odds.append(
                lax.ppermute(jnp.where(even, evens[-2], evens[-1]), "seq", beside)
            )
        blocks = []
        for distance in range(reach, -1, -1):
            blocks.append(evens[distance // 2] if distance % 2 == 0 else odds[distance // 2])
        return blocks

    pieces = gather(shards[0])
    states = []
    for layer in range(LAYERS):
        kv_rows, normed = key_value(
            layer, state, state_other, gains[layer], tables, key_value_weights, count
        )
        blocks = window(kv_rows)
        query_own, query_came, out_own, out_came = pieces
        queries = query(normed, tables, query_own, query_came)
        mixed = attend(lengths, boundary, queries, blocks)
        if layer + 1 < LAYERS:
            pieces = gather(after(shards[layer + 1], *blocks[:-1]))
        leave, stay = out_project(mixed, out_own, out_came)
        arrived = across_tp(leave)
        state = (
            state.astype(jnp.float32) + stay + arrived.astype(jnp.float32)
        ).astype(jnp.bfloat16)
        states.append(state)
        if layer + 1 < LAYERS:
            state_other = across_tp(state)

    first_came = lax.ppermute(states[0], "segment", [(1, 0)])
    last_came = lax.ppermute(states[1], "segment", [(0, 1)])
    return jnp.stack(
        [
            jnp.where(first_core, states[0], last_came),
            jnp.where(first_core, first_came, states[1]),
        ]
    )[None]


def solution(mesh):
    return jax.shard_map(
        per_device,
        mesh=mesh,
        in_specs=(
            P(None, "seq", "tp"),
            P(),
            P(),
            P("segment", None),
            P("segment", "seq", "tp"),
            P("segment", None, "tp"),
            P("segment", None, "tp"),
            P("segment", "tp", "seq"),
        ),
        out_specs=P("segment", None, "seq", "tp"),
        check_vma=False,
    )
```

time: 728 us -> 279 us (0.38)
  waiting for transfers between devices: 493 us -> 118 us
  Pallas kernels: 0 us -> 49.2 us
  matrix products: 44.6 us -> 0 us
  local copies, waits for them, and re-layouts: 54.1 us -> 18.8 us
  other arithmetic: 30.5 us -> 9.55 us
  between operations: 13.4 us -> 0.56 us
  starting transfers between devices: 89.3 us -> 81.8 us
    all_gather x5 -> x0, waiting for transfers between devices: 248 us -> none  [the longest x1 92.3 us: per_device(): output_cols = lax.all_gather(out_weight, 'seq', axis=2, tiled=True)[0]]
    while x9 -> x0, waiting for transfers between devices: 236 us -> none
    ppermute x27 -> x52, waiting for transfers between devices: 8.34 us -> 118 us  [the longest x4 45.2 us: across_tp(): return lax.ppermute(value, 'tp', SWAP)]
    pallas_call x0 -> x8, Pallas kernels: none -> 49.2 us  [the longest x2 13.2 us: out_project(): call(functools.partial(out_kernel, count), (jax.ShapeDtypeStruct((rows, w...]
    dot_general x10 -> x0, matrix products: 30.1 us -> none  [the longest x2 10.8 us: mix_rows(): jnp.einsum('gjqk,kgd->qgjd', weights, value_heads, preferred_element_type...]
    while x45 -> x0, local copies, waits for them, and re-layouts: 28.6 us -> none
    sub x2 -> x0, matrix products: 14.5 us -> none  [mix_rows(): exp_terms = jnp.where(visible, jnp.exp(masked - row_max), 0.0)]
    ppermute x27 -> x52, starting transfers between devices: 89.1 us -> 81.8 us  [the longest x22 23.2 us: across_chip(): return lax.ppermute(value, 'segment', SWAP)]
  transfers between devices with their start and end apart: 35 -> 52, of which waited for: 12 -> 17; matrix products, arithmetic and copies ran while one was open for 4% -> 7% of each run, Pallas kernels for 0% -> 15%
where the time goes in v1:
time: 279 us; the launch traced here: 278 us
  waiting for transfers between devices  118 us (42%)
  starting transfers between devices  81.8 us (29%)
  Pallas kernels  49.2 us (18%)
  local copies, waits for them, and re-layouts  18.8 us (7%)
  other arithmetic  9.55 us (3%)
    ppermute x4, waiting for transfers between devices, across_tp(): return lax.ppermute(value, 'tp', SWAP)  45.2 us
    ppermute x4, waiting for transfers between devices, window(): evens.append(lax.ppermute(evens[-1], 'seq', up))  30.3 us
    ppermute x22, starting transfers between devices, across_chip(): return lax.ppermute(value, 'segment', SWAP)  23.2 us
    ppermute x4, starting transfers between devices, window(): evens.append(lax.ppermute(evens[-1], 'seq', up))  16.7 us
    ppermute x4, waiting for transfers between devices, window(): lax.ppermute(jnp.where(even, evens[-2], evens[-1]), 'seq', beside)  15.5 us
    ppermute x6, waiting for transfers between devices, gather(): forward.append(lax.ppermute(forward[-1], 'seq', onward))  14.7 us
    pallas_call x2, Pallas kernels, out_project(): call(functools.partial(out_kernel, count), (jax.ShapeDtypeStruct((rows, w...  13.2 us
    ppermute x4, starting transfers between devices, window(): lax.ppermute(jnp.where(even, evens[-2], evens[-1]), 'seq', beside)  12.4 us
  transfers between devices with their start and end apart: 52, of which 17 were waited for; matrix products, arithmetic and copies ran while one was open for 7% of the time, Pallas kernels for 15%

profile of v1, /device:TPU:1, one launch (start us, length us, event | category | flops | bytes accessed | tf_op | source)
XLA Modules:
  0.0 278.1 jit_solution(17684340490298341009)
XLA Ops:
  3.2 2.3 collective-permute-start
  5.5 1.7 collective-permute-done.4
  7.2 1.6 broadcast_select_fusion
  8.8 2.4 collective-permute-start.9
  11.4 9.8 %collective-permute-done = bf16[256,1344]{0,1:T(8,128)(2,1)} collective-permute-done((bf16[256,1344]{0,1:T(8,128)(2,1)}, bf16[256,1344]{0,1:T(8,128)(2,1)}, u32[]{:S(2)}, u32[]{:S(2)}) %collective-permute-start) | collective-permute-done | bytes 688160 | tf_op jit(solution)/shard_map/ppermute | solution.py:361
  22.2 4.7 %collective-permute-done.9.refs_7_ = bf16[2,336,512]{2,1,0:T(8,128)(2,1)} collective-permute-done((bf16[2,336,512]{2,1,0:T(8,128)(2,1)S(1)}, bf16[2,336,512]{2,1,0:T(8,128)(2,1)}, u32[]{:S(2)}, u32[]{:S(2)}) %collective-permute-start.9) | collective-permute-done | bytes 688160 | tf_op jit(solution)/shard_map/ppermute | solution.py:405
  29.3 1.5 collective-permute-start.19
  31.1 1.4 copy.13.other
  32.6 6.2 %key_value.2 = (bf16[256,1024]{1,0:T(8,128)(2,1)S(1)}, bf16[8,256,336]{2,1,0:T(8,128)(2,1)S(1)}) custom-call(bf16[256,1344]{1,0:T(8,128)(2,1)S(1)} %bitcast.17, bf16[256,1344]{1,0:T(8,128)(2,1)S(1)} %copy.13.other, f32[2,1344]{1,0:T(2,128)S(1)} %reshape.16.gain, f32[256,128]{1,0:T(8,128)S(1)} %get-tuple-element.36.cosine, ...), custom_call_target="tpu_custom_call" | custom-call | flops 1409286144 | bytes 8257536 | tf_op jit(solution)/shard_map/key_value/pallas_call | solution.py:144
  40.0 3.4 %collective-permute-start.20 = (bf16[256,1024]{1,0:T(8,128)(2,1)S(1)}, bf16[256,1024]{1,0:T(8,128)(2,1)S(1)}, u32[]{:S(2)}, u32[]{:S(2)}) collective-permute-start(bf16[256,1024]{1,0:T(8,128)(2,1)S(1)} %get-tuple-element.15.refs_4_), channel_id=1, source_target_pairs={{0,4},{2,6},{4,8},{6,10},{8,12},{10,14},{1,5},{3,7},{5,9},{7,11},{... | collective-permute-start | bytes 1572872 | tf_op jit(solution)/shard_map/ppermute | solution.py:426
  44.9 2.2 collective-permute-start.18
  47.1 7.3 %collective-permute-done.20.refs_2_ = bf16[256,1024]{1,0:T(8,128)(2,1)S(1)} collective-permute-done((bf16[256,1024]{1,0:T(8,128)(2,1)S(1)}, bf16[256,1024]{1,0:T(8,128)(2,1)S(1)}, u32[]{:S(2)}, u32[]{:S(2)}) %collective-permute-start.20) | collective-permute-done | bytes 524320 | tf_op jit(solution)/shard_map/ppermute | solution.py:426
  54.5 4.9 %collective-permute-start.21 = (bf16[256,1024]{1,0:T(8,128)(2,1)S(1)}, bf16[256,1024]{1,0:T(8,128)(2,1)}, u32[]{:S(2)}, u32[]{:S(2)}) collective-permute-start(bf16[256,1024]{1,0:T(8,128)(2,1)S(1)} %collective-permute-done.20.refs_2_), channel_id=1, source_target_pairs={{0,4},{2,6},{4,8},{6,10},{8,12},{10,14},{1,5},{3,7},{5,9},{7,11},{... | collective-permute-start | bytes 1572872 | tf_op jit(solution)/shard_map/ppermute | solution.py:426
  59.4 1.9 collective-permute-start.14
  62.3 7.0 %collective-permute-done.7.refs_3_ = bf16[2,336,512]{2,1,0:T(8,128)(2,1)S(1)} collective-permute-done((bf16[2,336,512]{2,1,0:T(8,128)(2,1)}, bf16[2,336,512]{2,1,0:T(8,128)(2,1)S(1)}, u32[]{:S(2)}, u32[]{:S(2)}) %collective-permute-start.7) | collective-permute-done | bytes 688160 | tf_op jit(solution)/shard_map/ppermute | solution.py:404
  69.3 3.6 %collective-permute-start.24 = (bf16[1,336,512]{2,1,0:T(8,128)(2,1)}, bf16[1,336,512]{2,1,0:T(8,128)(2,1)}, u32[]{:S(2)}, u32[]{:S(2)}) collective-permute-start(bf16[1,336,512]{2,1,0:T(8,128)(2,1)} %slice.17), channel_id=1, source_target_pairs={{4,0},{8,4},{12,8},{14,12},{10,14},{6,10},{2,6},{0,2},{5,1},{9,5},... | collective-permute-start | bytes 1032200 | tf_op jit(solution)/shard_map/ppermute | solution.py:407
  73.8 6.7 %collective-permute-done.21.refs_0_ = bf16[256,1024]{1,0:T(8,128)(2,1)} collective-permute-done((bf16[256,1024]{1,0:T(8,128)(2,1)S(1)}, bf16[256,1024]{1,0:T(8,128)(2,1)}, u32[]{:S(2)}, u32[]{:S(2)}) %collective-permute-start.21) | collective-permute-done | bytes 524320 | tf_op jit(solution)/shard_map/ppermute | solution.py:426
  80.5 1.6 collective-permute-start.15
  84.8 4.4 %collective-permute-start.22 = (bf16[256,1024]{1,0:T(8,128)(2,1)S(1)}, bf16[256,1024]{1,0:T(8,128)(2,1)S(1)}, u32[]{:S(2)}, u32[]{:S(2)}) collective-permute-start(bf16[256,1024]{1,0:T(8,128)(2,1)S(1)} %get-tuple-element.32), channel_id=1, source_target_pairs={{0,2},{2,0},{4,6},{6,4},{8,10},{10,8},{12,14},{14,12},{1,3},{3,1},... | collective-permute-start | bytes 1572872 | tf_op jit(solution)/shard_map/ppermute | solution.py:428
  92.0 6.1 %query.2.queries = bf16[2,256,512]{2,1,0:T(8,128)(2,1)S(1)} custom-call(bf16[8,256,336]{2,1,0:T(8,128)(2,1)} %copy-done.10, f32[256,128]{1,0:T(8,128)S(1)} %copy-done.3, f32[256,128]{1,0:T(8,128)S(1)} %copy-done.6, bf16[2,336,512]{2,1,0:T(8,128)(2,1)S(1)} %get-tuple-element.28.refs_0_, bf16[2,336,512]{2,1,0:T(8,128)(2,1)} %collective-permute-done.5.refs_1_, ...), custom_call_target="tpu_custom_call" | custom-call | flops 1409286144 | bytes 6881280 | tf_op jit(solution)/shard_map/query/pallas_call | solution.py:199
  98.2 10.1 %collective-permute-done.22.refs_1_ = bf16[256,1024]{1,0:T(8,128)(2,1)S(1)} collective-permute-done((bf16[256,1024]{1,0:T(8,128)(2,1)S(1)}, bf16[256,1024]{1,0:T(8,128)(2,1)S(1)}, u32[]{:S(2)}, u32[]{:S(2)}) %collective-permute-start.22) | collective-permute-done | bytes 524320 | tf_op jit(solution)/shard_map/ppermute | solution.py:428
  108.3 6.1 %attend.2.mixed = bf16[2,256,512]{2,1,0:T(8,128)(2,1)S(1)} custom-call(s32[2,8]{1,0:T(2,128)S(1)} %copy-done.16, s32[2]{0:T(128)S(1)} %copy-done.17, bf16[2,256,512]{2,1,0:T(8,128)(2,1)S(1)} %query.2.queries, bf16[256,1024]{1,0:T(8,128)(2,1)} %collective-permute-done.21.refs_0_, bf16[256,1024]{1,0:T(8,128)(2,1)S(1)} %collective-permute-done.22.refs_1_, ...), custom_call_target="tpu_custom_call" | custom-call | flops 1342177280 | bytes 3670016 | tf_op jit(solution)/shard_map/attend/pallas_call | solution.py:278
  114.4 6.6 %out_project.2 = (bf16[256,1344]{1,0:T(8,128)(2,1)}, f32[256,1344]{1,0:T(8,128)}) custom-call(bf16[2,256,512]{2,1,0:T(8,128)(2,1)S(1)} %attend.2.mixed, bf16[2,336,512]{2,1,0:T(8,128)(2,1)S(1)} %get-tuple-element.28.refs_0_, bf16[2,336,512]{2,1,0:T(8,128)(2,1)} %collective-permute-done.5.refs_1_, bf16[2,336,512]{2,1,0:T(8,128)(2,1)} %collective-permute-done.6.refs_2_, ...), custom_call_target="tpu_custom_call" | custom-call | flops 1409286144 | bytes 7569408 | tf_op jit(solution)/shard_map/out_project/pallas_call | solution.py:326
  126.0 12.6 %collective-permute-done.26 = bf16[256,1344]{0,1:T(8,128)(2,1)} collective-permute-done((bf16[256,1344]{0,1:T(8,128)(2,1)S(1)}, bf16[256,1344]{0,1:T(8,128)(2,1)}, u32[]{:S(2)}, u32[]{:S(2)}) %collective-permute-start.26) | collective-permute-done | bytes 688160 | tf_op jit(solution)/shard_map/ppermute | solution.py:361
  138.7 2.2 copy.15
  140.9 1.8 add_convert_fusion.1.own
  145.0 2.0 collective-permute-start.35
  150.1 9.2 %collective-permute-done.27 = bf16[256,1344]{0,1:T(8,128)(2,1)S(1)} collective-permute-done((bf16[256,1344]{0,1:T(8,128)(2,1)}, bf16[256,1344]{0,1:T(8,128)(2,1)S(1)}, u32[]{:S(2)}, u32[]{:S(2)}) %collective-permute-start.27) | collective-permute-done | bytes 688160 | tf_op jit(solution)/shard_map/ppermute | solution.py:361
  160.2 2.5 collective-permute-start.36
  164.2 5.9 %key_value.3 = (bf16[256,1024]{1,0:T(8,128)(2,1)S(1)}, bf16[8,256,336]{2,1,0:T(8,128)(2,1)S(1)}) custom-call(bf16[256,1344]{1,0:T(8,128)(2,1)S(1)} %add_convert_fusion.1.own, bf16[256,1344]{1,0:T(8,128)(2,1)S(1)} %copy.17.other, f32[2,1344]{1,0:T(2,128)S(1)} %reshape.17.gain, f32[256,128]{1,0:T(8,128)S(1)} %copy-done.4, f32[256,128]{1,0:T(8,128)S(1)} %copy-done.7, ...), custom_call_target="tpu_custom_call" | custom-call | flops 1409286144 | bytes 8257536 | tf_op jit(solution)/shard_map/key_value/pallas_call | solution.py:144
  170.1 4.3 %collective-permute-start.43 = (bf16[256,1024]{1,0:T(8,128)(2,1)S(1)}, bf16[256,1024]{1,0:T(8,128)(2,1)S(1)}, u32[]{:S(2)}, u32[]{:S(2)}) collective-permute-start(bf16[256,1024]{1,0:T(8,128)(2,1)S(1)} %get-tuple-element.20.refs_4_), channel_id=1, source_target_pairs={{0,4},{2,6},{4,8},{6,10},{8,12},{10,14},{1,5},{3,7},{5,9},{7,11},{... | collective-permute-start | bytes 1572872 | tf_op jit(solution)/shard_map/ppermute | solution.py:426
  177.1 8.3 %collective-permute-done.43.refs_2_ = bf16[256,1024]{1,0:T(8,128)(2,1)S(1)} collective-permute-done((bf16[256,1024]{1,0:T(8,128)(2,1)S(1)}, bf16[256,1024]{1,0:T(8,128)(2,1)S(1)}, u32[]{:S(2)}, u32[]{:S(2)}) %collective-permute-start.43) | collective-permute-done | bytes 524320 | tf_op jit(solution)/shard_map/ppermute | solution.py:426
  185.4 4.1 %collective-permute-start.44 = (bf16[256,1024]{1,0:T(8,128)(2,1)S(1)}, bf16[256,1024]{1,0:T(8,128)(2,1)S(1)}, u32[]{:S(2)}, u32[]{:S(2)}) collective-permute-start(bf16[256,1024]{1,0:T(8,128)(2,1)S(1)} %collective-permute-done.43.refs_2_), channel_id=1, source_target_pairs={{0,4},{2,6},{4,8},{6,10},{8,12},{10,14},{1,5},{3,7},{5,9},{7,11},{... | collective-permute-start | bytes 1572872 | tf_op jit(solution)/shard_map/ppermute | solution.py:426
  189.6 2.1 collective-permute-start.37
  192.6 7.7 %collective-permute-done.30.refs_3_ = bf16[2,336,512]{2,1,0:T(8,128)(2,1)S(1)} collective-permute-done((bf16[2,336,512]{2,1,0:T(8,128)(2,1)}, bf16[2,336,512]{2,1,0:T(8,128)(2,1)S(1)}, u32[]{:S(2)}, u32[]{:S(2)}) %collective-permute-start.30) | collective-permute-done | bytes 688160 | tf_op jit(solution)/shard_map/ppermute | solution.py:404
  200.3 3.1 %collective-permute-start.47 = (bf16[1,336,512]{2,1,0:T(8,128)(2,1)S(1)}, bf16[1,336,512]{2,1,0:T(8,128)(2,1)S(1)}, u32[]{:S(2)}, u32[]{:S(2)}) collective-permute-start(bf16[1,336,512]{2,1,0:T(8,128)(2,1)S(1)} %slice.19), channel_id=1, source_target_pairs={{4,0},{8,4},{12,8},{14,12},{10,14},{6,10},{2,6},{0,2},{5,1},{9,5},... | collective-permute-start | bytes 1032200 | tf_op jit(solution)/shard_map/ppermute | solution.py:407
  203.5 7.9 %collective-permute-done.44.refs_0_ = bf16[256,1024]{1,0:T(8,128)(2,1)S(1)} collective-permute-done((bf16[256,1024]{1,0:T(8,128)(2,1)S(1)}, bf16[256,1024]{1,0:T(8,128)(2,1)S(1)}, u32[]{:S(2)}, u32[]{:S(2)}) %collective-permute-start.44) | collective-permute-done | bytes 524320 | tf_op jit(solution)/shard_map/ppermute | solution.py:426
  211.4 1.8 collective-permute-start.38
  214.7 5.4 %collective-permute-start.45 = (bf16[256,1024]{1,0:T(8,128)(2,1)S(1)}, bf16[256,1024]{1,0:T(8,128)(2,1)S(1)}, u32[]{:S(2)}, u32[]{:S(2)}) collective-permute-start(bf16[256,1024]{1,0:T(8,128)(2,1)S(1)} %get-tuple-element.30), channel_id=1, source_target_pairs={{0,2},{2,0},{4,6},{6,4},{8,10},{10,8},{12,14},{14,12},{1,3},{3,1},... | collective-permute-start | bytes 1572872 | tf_op jit(solution)/shard_map/ppermute | solution.py:428
  222.7 3.1 %collective-permute-start.51 = (bf16[256,1344]{0,1:T(8,128)(2,1)}, bf16[256,1344]{0,1:T(8,128)(2,1)}, u32[]{:S(2)}, u32[]{:S(2)}) collective-permute-start(bf16[256,1344]{0,1:T(8,128)(2,1)} %copy.16), channel_id=1, source_target_pairs={{16,0},{17,1},{18,2},{19,3},{20,4},{21,5},{22,6},{23,7},{24,8},{25... | collective-permute-start | bytes 2064392 | tf_op jit(solution)/shard_map/ppermute | solution.py:456
  226.7 6.1 %query.3.queries = bf16[2,256,512]{2,1,0:T(8,128)(2,1)S(1)} custom-call(bf16[8,256,336]{2,1,0:T(8,128)(2,1)} %copy-done.11, f32[256,128]{1,0:T(8,128)S(1)} %copy-done.4, f32[256,128]{1,0:T(8,128)S(1)} %copy-done.7, bf16[2,336,512]{2,1,0:T(8,128)(2,1)S(1)} %get-tuple-element.19.refs_0_, bf16[2,336,512]{2,1,0:T(8,128)(2,1)} %collective-permute-done.28.refs_1_, ...), custom_call_target="tpu_custom_call" | custom-call | flops 1409286144 | bytes 6881280 | tf_op jit(solution)/shard_map/query/pallas_call | solution.py:199
  232.8 5.4 %collective-permute-done.45.refs_1_ = bf16[256,1024]{1,0:T(8,128)(2,1)S(1)} collective-permute-done((bf16[256,1024]{1,0:T(8,128)(2,1)S(1)}, bf16[256,1024]{1,0:T(8,128)(2,1)S(1)}, u32[]{:S(2)}, u32[]{:S(2)}) %collective-permute-start.45) | collective-permute-done | bytes 524320 | tf_op jit(solution)/shard_map/ppermute | solution.py:428
  238.2 5.6 %attend.3.mixed = bf16[2,256,512]{2,1,0:T(8,128)(2,1)S(1)} custom-call(s32[2,8]{1,0:T(2,128)S(1)} %copy-done.16, s32[2]{0:T(128)S(1)} %copy-done.17, bf16[2,256,512]{2,1,0:T(8,128)(2,1)S(1)} %query.3.queries, bf16[256,1024]{1,0:T(8,128)(2,1)S(1)} %collective-permute-done.44.refs_0_, bf16[256,1024]{1,0:T(8,128)(2,1)S(1)} %collective-permute-done.45.refs_1_, ...), custom_call_target="tpu_custom_call" | custom-call | flops 1342177280 | bytes 3670016 | tf_op jit(solution)/shard_map/attend/pallas_call | solution.py:278
  243.9 6.6 %out_project.3 = (bf16[256,1344]{1,0:T(8,128)(2,1)}, f32[256,1344]{1,0:T(8,128)}) custom-call(bf16[2,256,512]{2,1,0:T(8,128)(2,1)S(1)} %attend.3.mixed, bf16[2,336,512]{2,1,0:T(8,128)(2,1)S(1)} %get-tuple-element.19.refs_0_, bf16[2,336,512]{2,1,0:T(8,128)(2,1)} %collective-permute-done.28.refs_1_, bf16[2,336,512]{2,1,0:T(8,128)(2,1)} %collective-permute-done.29.refs_2_, ...), custom_call_target="tpu_custom_call" | custom-call | flops 1409286144 | bytes 7569408 | tf_op jit(solution)/shard_map/out_project/pallas_call | solution.py:326
  254.6 13.5 %collective-permute-done.49 = bf16[256,1344]{0,1:T(8,128)(2,1)S(1)} collective-permute-done((bf16[256,1344]{0,1:T(8,128)(2,1)S(1)}, bf16[256,1344]{0,1:T(8,128)(2,1)S(1)}, u32[]{:S(2)}, u32[]{:S(2)}) %collective-permute-start.49) | collective-permute-done | bytes 688160 | tf_op jit(solution)/shard_map/ppermute | solution.py:361
  268.5 2.6 select_bitcast_fusion
  272.7 3.3 %collective-permute-done.50 = bf16[256,1344]{0,1:T(8,128)(2,1)S(1)} collective-permute-done((bf16[256,1344]{0,1:T(8,128)(2,1)S(1)}, bf16[256,1344]{0,1:T(8,128)(2,1)S(1)}, u32[]{:S(2)}, u32[]{:S(2)}) %collective-permute-start.50) | collective-permute-done | bytes 688160 | tf_op jit(solution)/shard_map/ppermute | solution.py:457
  276.6 1.5 copy.24
  (153 shorter events, 44.9 us)
Async XLA Ops:
  0.0 29.3 %collective-permute-start.2 = (bf16[2688,512]{1,0:T(8,128)(2,1)}, bf16[2688,512]{1,0:T(8,128)(2,1)}, u32[]{:S(2)}, u32[]{:S(2)}) collective-permute-start(bf16[2688,512]{1,0:T(8,128)(2,1)} %bitcast.18), channel_id=1, source_target_pairs={{0,16},{16,0},{1,17},{17,1},{2,18},{18,2},{3,19},{19,3},{4,20},{20... | collective-permute-start | bytes 8257544 | tf_op jit(solution)/shard_map/ppermute | solution.py:358
  0.1 32.5 %collective-permute-start.3 = (bf16[2688,512]{1,0:T(8,128)(2,1)}, bf16[2688,512]{1,0:T(8,128)(2,1)}, u32[]{:S(2)}, u32[]{:S(2)}) collective-permute-start(bf16[2688,512]{1,0:T(8,128)(2,1)} %bitcast.21), channel_id=1, source_target_pairs={{0,16},{16,0},{1,17},{17,1},{2,18},{18,2},{3,19},{19,3},{4,20},{20... | collective-permute-start | bytes 8257544 | tf_op jit(solution)/shard_map/ppermute | solution.py:358
  1.9 9.4 %collective-permute-start.1 = (f32[1,2688]{1,0:T(1,128)S(1)}, f32[1,2688]{1,0:T(1,128)S(1)}, u32[]{:S(2)}, u32[]{:S(2)}) collective-permute-start(f32[1,2688]{1,0:T(1,128)S(1)} %copy-done.27), channel_id=1, source_target_pairs={{0,16},{16,0},{1,17},{17,1},{2,18},{18,2},{3,19},{19,3},{4,20},{20... | collective-permute-start | bytes 32264 | tf_op jit(solution)/shard_map/ppermute | solution.py:358
  3.2 18.1 %collective-permute-start = (bf16[256,1344]{0,1:T(8,128)(2,1)}, bf16[256,1344]{0,1:T(8,128)(2,1)}, u32[]{:S(2)}, u32[]{:S(2)}) collective-permute-start(bf16[256,1344]{0,1:T(8,128)(2,1)} %fusion.5), channel_id=1, source_target_pairs={{0,1},{1,0},{2,3},{3,2},{4,5},{5,4},{6,7},{7,6},{8,9},{9,8},{10,11... | collective-permute-start | bytes 2064392 | tf_op jit(solution)/shard_map/ppermute | solution.py:361
  8.8 18.1 %collective-permute-start.9 = (bf16[2,336,512]{2,1,0:T(8,128)(2,1)S(1)}, bf16[2,336,512]{2,1,0:T(8,128)(2,1)}, u32[]{:S(2)}, u32[]{:S(2)}) collective-permute-start(bf16[2,336,512]{2,1,0:T(8,128)(2,1)S(1)} %get-tuple-element.28.refs_0_), channel_id=1, source_target_pairs={{4,0},{8,4},{12,8},{14,12},{10,14},{6,10},{2,6},{0,2},{5,1},{9,5},... | collective-permute-start | bytes 2064392 | tf_op jit(solution)/shard_map/ppermute | solution.py:405
  11.2 16.8 %collective-permute-start.5 = (bf16[2,336,512]{2,1,0:T(8,128)(2,1)S(1)}, bf16[2,336,512]{2,1,0:T(8,128)(2,1)}, u32[]{:S(2)}, u32[]{:S(2)}) collective-permute-start(bf16[2,336,512]{2,1,0:T(8,128)(2,1)S(1)} %get-tuple-element.28.refs_0_), channel_id=1, source_target_pairs={{0,4},{4,8},{8,12},{12,14},{14,10},{10,6},{6,2},{2,0},{1,5},{5,9},... | collective-permute-start | bytes 2064392 | tf_op jit(solution)/shard_map/ppermute | solution.py:404
  21.2 18.8 %collective-permute-start.12 = (bf16[2,336,512]{2,1,0:T(8,128)(2,1)S(1)}, bf16[2,336,512]{2,1,0:T(8,128)(2,1)}, u32[]{:S(2)}, u32[]{:S(2)}) collective-permute-start(bf16[2,336,512]{2,1,0:T(8,128)(2,1)S(1)} %get-tuple-element.28.refs_0_), channel_id=1, source_target_pairs={{0,16},{16,0},{1,17},{17,1},{2,18},{18,2},{3,19},{19,3},{4,20},{20... | collective-permute-start | bytes 2064392 | tf_op jit(solution)/shard_map/ppermute | solution.py:358
  26.9 16.5 %collective-permute-start.10 = (bf16[2,336,512]{2,1,0:T(8,128)(2,1)}, bf16[2,336,512]{2,1,0:T(8,128)(2,1)}, u32[]{:S(2)}, u32[]{:S(2)}) collective-permute-start(bf16[2,336,512]{2,1,0:T(8,128)(2,1)} %collective-permute-done.9.refs_7_), channel_id=1, source_target_pairs={{4,0},{8,4},{12,8},{14,12},{10,14},{6,10},{2,6},{0,2},{5,1},{9,5},... | collective-permute-start | bytes 2064392 | tf_op jit(solution)/shard_map/ppermute | solution.py:405
  28.0 16.7 %collective-permute-start.6 = (bf16[2,336,512]{2,1,0:T(8,128)(2,1)}, bf16[2,336,512]{2,1,0:T(8,128)(2,1)}, u32[]{:S(2)}, u32[]{:S(2)}) collective-permute-start(bf16[2,336,512]{2,1,0:T(8,128)(2,1)} %collective-permute-done.5.refs_1_), channel_id=1, source_target_pairs={{0,4},{4,8},{8,12},{12,14},{14,10},{10,6},{6,2},{2,0},{1,5},{5,9},... | collective-permute-start | bytes 2064392 | tf_op jit(solution)/shard_map/ppermute | solution.py:404
  29.3 15.7 %collective-permute-start.19 = (bf16[2,336,512]{2,1,0:T(8,128)(2,1)}, bf16[2,336,512]{2,1,0:T(8,128)(2,1)}, u32[]{:S(2)}, u32[]{:S(2)}) collective-permute-start(bf16[2,336,512]{2,1,0:T(8,128)(2,1)} %collective-permute-done.9.refs_7_), channel_id=1, source_target_pairs={{0,16},{16,0},{1,17},{17,1},{2,18},{18,2},{3,19},{19,3},{4,20},{20... | collective-permute-start | bytes 2064392 | tf_op jit(solution)/shard_map/ppermute | solution.py:358
  32.5 26.8 %collective-permute-start.13 = (bf16[2,336,512]{2,1,0:T(8,128)(2,1)}, bf16[2,336,512]{2,1,0:T(8,128)(2,1)S(1)}, u32[]{:S(2)}, u32[]{:S(2)}) collective-permute-start(bf16[2,336,512]{2,1,0:T(8,128)(2,1)} %collective-permute-done.5.refs_1_), channel_id=1, source_target_pairs={{0,16},{16,0},{1,17},{17,1},{2,18},{18,2},{3,19},{19,3},{4,20},{20... | collective-permute-start | bytes 2064392 | tf_op jit(solution)/shard_map/ppermute | solution.py:358
  40.0 14.5 %collective-permute-start.20 = (bf16[256,1024]{1,0:T(8,128)(2,1)S(1)}, bf16[256,1024]{1,0:T(8,128)(2,1)S(1)}, u32[]{:S(2)}, u32[]{:S(2)}) collective-permute-start(bf16[256,1024]{1,0:T(8,128)(2,1)S(1)} %get-tuple-element.15.refs_4_), channel_id=1, source_target_pairs={{0,4},{2,6},{4,8},{6,10},{8,12},{10,14},{1,5},{3,7},{5,9},{7,11},{... | collective-permute-start | bytes 1572872 | tf_op jit(solution)/shard_map/ppermute | solution.py:426
  43.4 17.9 %collective-permute-start.11 = (bf16[2,336,512]{2,1,0:T(8,128)(2,1)}, bf16[2,336,512]{2,1,0:T(8,128)(2,1)S(1)}, u32[]{:S(2)}, u32[]{:S(2)}) collective-permute-start(bf16[2,336,512]{2,1,0:T(8,128)(2,1)} %collective-permute-done.10.refs_6_), channel_id=1, source_target_pairs={{4,0},{8,4},{12,8},{14,12},{10,14},{6,10},{2,6},{0,2},{5,1},{9,5},... | collective-permute-start | bytes 2064392 | tf_op jit(solution)/shard_map/ppermute | solution.py:405
  44.7 24.6 %collective-permute-start.7 = (bf16[2,336,512]{2,1,0:T(8,128)(2,1)}, bf16[2,336,512]{2,1,0:T(8,128)(2,1)S(1)}, u32[]{:S(2)}, u32[]{:S(2)}) collective-permute-start(bf16[2,336,512]{2,1,0:T(8,128)(2,1)} %collective-permute-done.6.refs_2_), channel_id=1, source_target_pairs={{0,4},{4,8},{8,12},{12,14},{14,10},{10,6},{6,2},{2,0},{1,5},{5,9},... | collective-permute-start | bytes 2064392 | tf_op jit(solution)/shard_map/ppermute | solution.py:404
  44.9 28.8 %collective-permute-start.18 = (bf16[2,336,512]{2,1,0:T(8,128)(2,1)}, bf16[2,336,512]{2,1,0:T(8,128)(2,1)S(1)}, u32[]{:S(2)}, u32[]{:S(2)}) collective-permute-start(bf16[2,336,512]{2,1,0:T(8,128)(2,1)} %collective-permute-done.10.refs_6_), channel_id=1, source_target_pairs={{0,16},{16,0},{1,17},{17,1},{2,18},{18,2},{3,19},{19,3},{4,20},{20... | collective-permute-start | bytes 2064392 | tf_op jit(solution)/shard_map/ppermute | solution.py:358
  54.5 26.0 %collective-permute-start.21 = (bf16[256,1024]{1,0:T(8,128)(2,1)S(1)}, bf16[256,1024]{1,0:T(8,128)(2,1)}, u32[]{:S(2)}, u32[]{:S(2)}) collective-permute-start(bf16[256,1024]{1,0:T(8,128)(2,1)S(1)} %collective-permute-done.20.refs_2_), channel_id=1, source_target_pairs={{0,4},{2,6},{4,8},{6,10},{8,12},{10,14},{1,5},{3,7},{5,9},{7,11},{... | collective-permute-start | bytes 1572872 | tf_op jit(solution)/shard_map/ppermute | solution.py:426
  59.4 24.1 %collective-permute-start.14 = (bf16[2,336,512]{2,1,0:T(8,128)(2,1)}, bf16[2,336,512]{2,1,0:T(8,128)(2,1)}, u32[]{:S(2)}, u32[]{:S(2)}) collective-permute-start(bf16[2,336,512]{2,1,0:T(8,128)(2,1)} %collective-permute-done.6.refs_2_), channel_id=1, source_target_pairs={{0,16},{16,0},{1,17},{17,1},{2,18},{18,2},{3,19},{19,3},{4,20},{20... | collective-permute-start | bytes 2064392 | tf_op jit(solution)/shard_map/ppermute | solution.py:358
  61.3 29.2 %collective-permute-start.17 = (bf16[2,336,512]{2,1,0:T(8,128)(2,1)S(1)}, bf16[2,336,512]{2,1,0:T(8,128)(2,1)}, u32[]{:S(2)}, u32[]{:S(2)}) collective-permute-start(bf16[2,336,512]{2,1,0:T(8,128)(2,1)S(1)} %collective-permute-done.11.refs_5_), channel_id=1, source_target_pairs={{0,16},{16,0},{1,17},{17,1},{2,18},{18,2},{3,19},{19,3},{4,20},{20... | collective-permute-start | bytes 2064392 | tf_op jit(solution)/shard_map/ppermute | solution.py:358
  69.3 15.4 %collective-permute-start.24 = (bf16[1,336,512]{2,1,0:T(8,128)(2,1)}, bf16[1,336,512]{2,1,0:T(8,128)(2,1)}, u32[]{:S(2)}, u32[]{:S(2)}) collective-permute-start(bf16[1,336,512]{2,1,0:T(8,128)(2,1)} %slice.17), channel_id=1, source_target_pairs={{4,0},{8,4},{12,8},{14,12},{10,14},{6,10},{2,6},{0,2},{5,1},{9,5},... | collective-permute-start | bytes 1032200 | tf_op jit(solution)/shard_map/ppermute | solution.py:407
  73.7 15.4 %collective-permute-start.8 = (bf16[1,336,512]{2,1,0:T(8,128)(2,1)}, bf16[1,336,512]{2,1,0:T(8,128)(2,1)}, u32[]{:S(2)}, u32[]{:S(2)}) collective-permute-start(bf16[1,336,512]{2,1,0:T(8,128)(2,1)} %slice.16), channel_id=1, source_target_pairs={{0,4},{4,8},{8,12},{12,14},{14,10},{10,6},{6,2},{2,0},{1,5},{5,9},... | collective-permute-start | bytes 1032200 | tf_op jit(solution)/shard_map/ppermute | solution.py:406
  80.5 11.5 %collective-permute-start.15 = (bf16[2,336,512]{2,1,0:T(8,128)(2,1)S(1)}, bf16[2,336,512]{2,1,0:T(8,128)(2,1)}, u32[]{:S(2)}, u32[]{:S(2)}) collective-permute-start(bf16[2,336,512]{2,1,0:T(8,128)(2,1)S(1)} %collective-permute-done.7.refs_3_), channel_id=1, source_target_pairs={{0,16},{16,0},{1,17},{17,1},{2,18},{18,2},{3,19},{19,3},{4,20},{20... | collective-permute-start | bytes 2064392 | tf_op jit(solution)/shard_map/ppermute | solution.py:358
  83.4 14.7 %collective-permute-start.23 = (bf16[256,1024]{1,0:T(8,128)(2,1)S(1)}, bf16[256,1024]{1,0:T(8,128)(2,1)S(1)}, u32[]{:S(2)}, u32[]{:S(2)}) collective-permute-start(bf16[256,1024]{1,0:T(8,128)(2,1)S(1)} %get-tuple-element.31), channel_id=1, source_target_pairs={{0,2},{2,0},{4,6},{6,4},{8,10},{10,8},{12,14},{14,12},{1,3},{3,1},... | collective-permute-start | bytes 1572872 | tf_op jit(solution)/shard_map/ppermute | solution.py:428
  84.8 23.5 %collective-permute-start.22 = (bf16[256,1024]{1,0:T(8,128)(2,1)S(1)}, bf16[256,1024]{1,0:T(8,128)(2,1)S(1)}, u32[]{:S(2)}, u32[]{:S(2)}) collective-permute-start(bf16[256,1024]{1,0:T(8,128)(2,1)S(1)} %get-tuple-element.32), channel_id=1, source_target_pairs={{0,2},{2,0},{4,6},{6,4},{8,10},{10,8},{12,14},{14,12},{1,3},{3,1},... | collective-permute-start | bytes 1572872 | tf_op jit(solution)/shard_map/ppermute | solution.py:428
  90.5 23.9 %collective-permute-start.25 = (bf16[1,336,512]{2,1,0:T(8,128)(2,1)}, bf16[1,336,512]{2,1,0:T(8,128)(2,1)S(1)}, u32[]{:S(2)}, u32[]{:S(2)}) collective-permute-start(bf16[1,336,512]{2,1,0:T(8,128)(2,1)} %collective-permute-done.24.refs_4_), channel_id=1, source_target_pairs={{0,16},{16,0},{1,17},{17,1},{2,18},{18,2},{3,19},{19,3},{4,20},{20... | collective-permute-start | bytes 1032200 | tf_op jit(solution)/shard_map/ppermute | solution.py:358
  122.4 16.3 %collective-permute-start.26 = (bf16[256,1344]{0,1:T(8,128)(2,1)S(1)}, bf16[256,1344]{0,1:T(8,128)(2,1)}, u32[]{:S(2)}, u32[]{:S(2)}) collective-permute-start(bf16[256,1344]{0,1:T(8,128)(2,1)S(1)} %copy.14), channel_id=1, source_target_pairs={{0,1},{1,0},{2,3},{3,2},{4,5},{5,4},{6,7},{7,6},{8,9},{9,8},{10,11... | collective-permute-start | bytes 2064392 | tf_op jit(solution)/shard_map/ppermute | solution.py:361
  123.6 23.4 %collective-permute-start.32 = (bf16[2,336,512]{2,1,0:T(8,128)(2,1)S(1)}, bf16[2,336,512]{2,1,0:T(8,128)(2,1)S(1)}, u32[]{:S(2)}, u32[]{:S(2)}) collective-permute-start(bf16[2,336,512]{2,1,0:T(8,128)(2,1)S(1)} %get-tuple-element.19.refs_0_), channel_id=1, source_target_pairs={{4,0},{8,4},{12,8},{14,12},{10,14},{6,10},{2,6},{0,2},{5,1},{9,5},... | collective-permute-start | bytes 2064392 | tf_op jit(solution)/shard_map/ppermute | solution.py:405
  124.9 23.4 %collective-permute-start.28 = (bf16[2,336,512]{2,1,0:T(8,128)(2,1)S(1)}, bf16[2,336,512]{2,1,0:T(8,128)(2,1)}, u32[]{:S(2)}, u32[]{:S(2)}) collective-permute-start(bf16[2,336,512]{2,1,0:T(8,128)(2,1)S(1)} %get-tuple-element.19.refs_0_), channel_id=1, source_target_pairs={{0,4},{4,8},{8,12},{12,14},{14,10},{10,6},{6,2},{2,0},{1,5},{5,9},... | collective-permute-start | bytes 2064392 | tf_op jit(solution)/shard_map/ppermute | solution.py:404
  143.8 15.5 %collective-permute-start.27 = (bf16[256,1344]{0,1:T(8,128)(2,1)}, bf16[256,1344]{0,1:T(8,128)(2,1)S(1)}, u32[]{:S(2)}, u32[]{:S(2)}) collective-permute-start(bf16[256,1344]{0,1:T(8,128)(2,1)} %copy.16), channel_id=1, source_target_pairs={{0,1},{1,0},{2,3},{3,2},{4,5},{5,4},{6,7},{7,6},{8,9},{9,8},{10,11... | collective-permute-start | bytes 2064392 | tf_op jit(solution)/shard_map/ppermute | solution.py:361
  145.0 25.1 %collective-permute-start.35 = (bf16[2,336,512]{2,1,0:T(8,128)(2,1)S(1)}, bf16[2,336,512]{2,1,0:T(8,128)(2,1)}, u32[]{:S(2)}, u32[]{:S(2)}) collective-permute-start(bf16[2,336,512]{2,1,0:T(8,128)(2,1)S(1)} %get-tuple-element.19.refs_0_), channel_id=1, source_target_pairs={{0,16},{16,0},{1,17},{17,1},{2,18},{18,2},{3,19},{19,3},{4,20},{20... | collective-permute-start | bytes 2064392 | tf_op jit(solution)/shard_map/ppermute | solution.py:358
  147.1 27.4 %collective-permute-start.33 = (bf16[2,336,512]{2,1,0:T(8,128)(2,1)S(1)}, bf16[2,336,512]{2,1,0:T(8,128)(2,1)}, u32[]{:S(2)}, u32[]{:S(2)}) collective-permute-start(bf16[2,336,512]{2,1,0:T(8,128)(2,1)S(1)} %collective-permute-done.32.refs_7_), channel_id=1, source_target_pairs={{4,0},{8,4},{12,8},{14,12},{10,14},{6,10},{2,6},{0,2},{5,1},{9,5},... | collective-permute-start | bytes 2064392 | tf_op jit(solution)/shard_map/ppermute | solution.py:405
  148.3 27.5 %collective-permute-start.29 = (bf16[2,336,512]{2,1,0:T(8,128)(2,1)}, bf16[2,336,512]{2,1,0:T(8,128)(2,1)}, u32[]{:S(2)}, u32[]{:S(2)}) collective-permute-start(bf16[2,336,512]{2,1,0:T(8,128)(2,1)} %collective-permute-done.28.refs_1_), channel_id=1, source_target_pairs={{0,4},{4,8},{8,12},{12,14},{14,10},{10,6},{6,2},{2,0},{1,5},{5,9},... | collective-permute-start | bytes 2064392 | tf_op jit(solution)/shard_map/ppermute | solution.py:404
  149.7 26.3 %collective-permute-start.42 = (bf16[2,336,512]{2,1,0:T(8,128)(2,1)S(1)}, bf16[2,336,512]{2,1,0:T(8,128)(2,1)}, u32[]{:S(2)}, u32[]{:S(2)}) collective-permute-start(bf16[2,336,512]{2,1,0:T(8,128)(2,1)S(1)} %collective-permute-done.32.refs_7_), channel_id=1, source_target_pairs={{0,16},{16,0},{1,17},{17,1},{2,18},{18,2},{3,19},{19,3},{4,20},{20... | collective-permute-start | bytes 2064392 | tf_op jit(solution)/shard_map/ppermute | solution.py:358
  160.2 29.4 %collective-permute-start.36 = (bf16[2,336,512]{2,1,0:T(8,128)(2,1)}, bf16[2,336,512]{2,1,0:T(8,128)(2,1)}, u32[]{:S(2)}, u32[]{:S(2)}) collective-permute-start(bf16[2,336,512]{2,1,0:T(8,128)(2,1)} %collective-permute-done.28.refs_1_), channel_id=1, source_target_pairs={{0,16},{16,0},{1,17},{17,1},{2,18},{18,2},{3,19},{19,3},{4,20},{20... | collective-permute-start | bytes 2064392 | tf_op jit(solution)/shard_map/ppermute | solution.py:358
  170.1 15.3 %collective-permute-start.43 = (bf16[256,1024]{1,0:T(8,128)(2,1)S(1)}, bf16[256,1024]{1,0:T(8,128)(2,1)S(1)}, u32[]{:S(2)}, u32[]{:S(2)}) collective-permute-start(bf16[256,1024]{1,0:T(8,128)(2,1)S(1)} %get-tuple-element.20.refs_4_), channel_id=1, source_target_pairs={{0,4},{2,6},{4,8},{6,10},{8,12},{10,14},{1,5},{3,7},{5,9},{7,11},{... | collective-permute-start | bytes 1572872 | tf_op jit(solution)/shard_map/ppermute | solution.py:426
  174.5 17.3 %collective-permute-start.34 = (bf16[2,336,512]{2,1,0:T(8,128)(2,1)}, bf16[2,336,512]{2,1,0:T(8,128)(2,1)S(1)}, u32[]{:S(2)}, u32[]{:S(2)}) collective-permute-start(bf16[2,336,512]{2,1,0:T(8,128)(2,1)} %collective-permute-done.33.refs_6_), channel_id=1, source_target_pairs={{4,0},{8,4},{12,8},{14,12},{10,14},{6,10},{2,6},{0,2},{5,1},{9,5},... | collective-permute-start | bytes 2064392 | tf_op jit(solution)/shard_map/ppermute | solution.py:405
  175.8 24.5 %collective-permute-start.30 = (bf16[2,336,512]{2,1,0:T(8,128)(2,1)}, bf16[2,336,512]{2,1,0:T(8,128)(2,1)S(1)}, u32[]{:S(2)}, u32[]{:S(2)}) collective-permute-start(bf16[2,336,512]{2,1,0:T(8,128)(2,1)} %collective-permute-done.29.refs_2_), channel_id=1, source_target_pairs={{0,4},{4,8},{8,12},{12,14},{14,10},{10,6},{6,2},{2,0},{1,5},{5,9},... | collective-permute-start | bytes 2064392 | tf_op jit(solution)/shard_map/ppermute | solution.py:404
  176.0 27.5 %collective-permute-start.41 = (bf16[2,336,512]{2,1,0:T(8,128)(2,1)}, bf16[2,336,512]{2,1,0:T(8,128)(2,1)S(1)}, u32[]{:S(2)}, u32[]{:S(2)}) collective-permute-start(bf16[2,336,512]{2,1,0:T(8,128)(2,1)} %collective-permute-done.33.refs_6_), channel_id=1, source_target_pairs={{0,16},{16,0},{1,17},{17,1},{2,18},{18,2},{3,19},{19,3},{4,20},{20... | collective-permute-start | bytes 2064392 | tf_op jit(solution)/shard_map/ppermute | solution.py:358
  185.4 26.0 %collective-permute-start.44 = (bf16[256,1024]{1,0:T(8,128)(2,1)S(1)}, bf16[256,1024]{1,0:T(8,128)(2,1)S(1)}, u32[]{:S(2)}, u32[]{:S(2)}) collective-permute-start(bf16[256,1024]{1,0:T(8,128)(2,1)S(1)} %collective-permute-done.43.refs_2_), channel_id=1, source_target_pairs={{0,4},{2,6},{4,8},{6,10},{8,12},{10,14},{1,5},{3,7},{5,9},{7,11},{... | collective-permute-start | bytes 1572872 | tf_op jit(solution)/shard_map/ppermute | solution.py:426
  189.6 23.7 %collective-permute-start.37 = (bf16[2,336,512]{2,1,0:T(8,128)(2,1)}, bf16[2,336,512]{2,1,0:T(8,128)(2,1)S(1)}, u32[]{:S(2)}, u32[]{:S(2)}) collective-permute-start(bf16[2,336,512]{2,1,0:T(8,128)(2,1)} %collective-permute-done.29.refs_2_), channel_id=1, source_target_pairs={{0,16},{16,0},{1,17},{17,1},{2,18},{18,2},{3,19},{19,3},{4,20},{20... | collective-permute-start | bytes 2064392 | tf_op jit(solution)/shard_map/ppermute | solution.py:358
  191.7 29.7 %collective-permute-start.40 = (bf16[2,336,512]{2,1,0:T(8,128)(2,1)S(1)}, bf16[2,336,512]{2,1,0:T(8,128)(2,1)S(1)}, u32[]{:S(2)}, u32[]{:S(2)}) collective-permute-start(bf16[2,336,512]{2,1,0:T(8,128)(2,1)S(1)} %collective-permute-done.34.refs_5_), channel_id=1, source_target_pairs={{0,16},{16,0},{1,17},{17,1},{2,18},{18,2},{3,19},{19,3},{4,20},{20... | collective-permute-start | bytes 2064392 | tf_op jit(solution)/shard_map/ppermute | solution.py:358
  200.3 14.4 %collective-permute-start.47 = (bf16[1,336,512]{2,1,0:T(8,128)(2,1)S(1)}, bf16[1,336,512]{2,1,0:T(8,128)(2,1)S(1)}, u32[]{:S(2)}, u32[]{:S(2)}) collective-permute-start(bf16[1,336,512]{2,1,0:T(8,128)(2,1)S(1)} %slice.19), channel_id=1, source_target_pairs={{4,0},{8,4},{12,8},{14,12},{10,14},{6,10},{2,6},{0,2},{5,1},{9,5},... | collective-permute-start | bytes 1032200 | tf_op jit(solution)/shard_map/ppermute | solution.py:407
  203.5 16.6 %collective-permute-start.31 = (bf16[1,336,512]{2,1,0:T(8,128)(2,1)S(1)}, bf16[1,336,512]{2,1,0:T(8,128)(2,1)S(1)}, u32[]{:S(2)}, u32[]{:S(2)}) collective-permute-start(bf16[1,336,512]{2,1,0:T(8,128)(2,1)S(1)} %slice.18), channel_id=1, source_target_pairs={{0,4},{4,8},{8,12},{12,14},{14,10},{10,6},{6,2},{2,0},{1,5},{5,9},... | collective-permute-start | bytes 1032200 | tf_op jit(solution)/shard_map/ppermute | solution.py:406
  211.4 14.4 %collective-permute-start.38 = (bf16[2,336,512]{2,1,0:T(8,128)(2,1)S(1)}, bf16[2,336,512]{2,1,0:T(8,128)(2,1)S(1)}, u32[]{:S(2)}, u32[]{:S(2)}) collective-permute-start(bf16[2,336,512]{2,1,0:T(8,128)(2,1)S(1)} %collective-permute-done.30.refs_3_), channel_id=1, source_target_pairs={{0,16},{16,0},{1,17},{17,1},{2,18},{18,2},{3,19},{19,3},{4,20},{20... | collective-permute-start | bytes 2064392 | tf_op jit(solution)/shard_map/ppermute | solution.py:358
  213.4 19.4 %collective-permute-start.46 = (bf16[256,1024]{1,0:T(8,128)(2,1)S(1)}, bf16[256,1024]{1,0:T(8,128)(2,1)S(1)}, u32[]{:S(2)}, u32[]{:S(2)}) collective-permute-start(bf16[256,1024]{1,0:T(8,128)(2,1)S(1)} %get-tuple-element.29), channel_id=1, source_target_pairs={{0,2},{2,0},{4,6},{6,4},{8,10},{10,8},{12,14},{14,12},{1,3},{3,1},... | collective-permute-start | bytes 1572872 | tf_op jit(solution)/shard_map/ppermute | solution.py:428
  214.7 23.5 %collective-permute-start.45 = (bf16[256,1024]{1,0:T(8,128)(2,1)S(1)}, bf16[256,1024]{1,0:T(8,128)(2,1)S(1)}, u32[]{:S(2)}, u32[]{:S(2)}) collective-permute-start(bf16[256,1024]{1,0:T(8,128)(2,1)S(1)} %get-tuple-element.30), channel_id=1, source_target_pairs={{0,2},{2,0},{4,6},{6,4},{8,10},{10,8},{12,14},{14,12},{1,3},{3,1},... | collective-permute-start | bytes 1572872 | tf_op jit(solution)/shard_map/ppermute | solution.py:428
  221.4 22.4 %collective-permute-start.48 = (bf16[1,336,512]{2,1,0:T(8,128)(2,1)S(1)}, bf16[1,336,512]{2,1,0:T(8,128)(2,1)S(1)}, u32[]{:S(2)}, u32[]{:S(2)}) collective-permute-start(bf16[1,336,512]{2,1,0:T(8,128)(2,1)S(1)} %collective-permute-done.47.refs_4_), channel_id=1, source_target_pairs={{0,16},{16,0},{1,17},{17,1},{2,18},{18,2},{3,19},{19,3},{4,20},{20... | collective-permute-start | bytes 1032200 | tf_op jit(solution)/shard_map/ppermute | solution.py:358
  222.7 30.4 %collective-permute-start.51 = (bf16[256,1344]{0,1:T(8,128)(2,1)}, bf16[256,1344]{0,1:T(8,128)(2,1)}, u32[]{:S(2)}, u32[]{:S(2)}) collective-permute-start(bf16[256,1344]{0,1:T(8,128)(2,1)} %copy.16), channel_id=1, source_target_pairs={{16,0},{17,1},{18,2},{19,3},{20,4},{21,5},{22,6},{23,7},{24,8},{25... | collective-permute-start | bytes 2064392 | tf_op jit(solution)/shard_map/ppermute | solution.py:456
  251.9 16.2 %collective-permute-start.49 = (bf16[256,1344]{0,1:T(8,128)(2,1)S(1)}, bf16[256,1344]{0,1:T(8,128)(2,1)S(1)}, u32[]{:S(2)}, u32[]{:S(2)}) collective-permute-start(bf16[256,1344]{0,1:T(8,128)(2,1)S(1)} %copy.18), channel_id=1, source_target_pairs={{0,1},{1,0},{2,3},{3,2},{4,5},{5,4},{6,7},{7,6},{8,9},{9,8},{10,11... | collective-permute-start | bytes 2064392 | tf_op jit(solution)/shard_map/ppermute | solution.py:361
  (32 other events, 384.0 us)

commit v2 on v1

v2 whole, which is shorter than its diff:
```python
import functools
import math

import jax
import jax.numpy as jnp
from jax import lax
from jax.experimental import pallas as pl
from jax.experimental.pallas import tpu as pltpu
from jax.sharding import PartitionSpec as P

HEADS = 16
KV = 8
HEAD_DIM = 128
WINDOW = 1024
GROUP = HEADS // KV
LAYERS = 2

norm_epsilon = 1e-06
hidden = -1e30
VMEM_LIMIT = 16 * 1024 * 1024

SWAP = ((0, 1), (1, 0))


def ring_order(count):
    return list(range(0, count, 2)) + list(range(count - 1, 0, -2))


def ring_position(index, count):
    return jnp.where(index % 2 == 0, index // 2, count - 1 - index // 2)


def ring_member(position, count):
    position = lax.rem(position + 2 * count, count)
    return jnp.where(position < count // 2, 2 * position, 2 * (count - 1 - position) + 1)


def hbm_spec():
    return pl.BlockSpec(memory_space=pltpu.HBM)


def vmem_spec():
    return pl.BlockSpec(memory_space=pltpu.VMEM)


def smem_spec():
    return pl.BlockSpec(memory_space=pltpu.SMEM)


def call(kernel, out_shape, in_specs, scratch, flops, moved, name, exps=0):
    outs = jax.tree.map(lambda _: vmem_spec(), out_shape)
    return pl.pallas_call(
        kernel,
        out_shape=out_shape,
        in_specs=in_specs,
        out_specs=outs,
        scratch_shapes=scratch,
        compiler_params=pltpu.CompilerParams(vmem_limit_bytes=VMEM_LIMIT),
        cost_estimate=pl.CostEstimate(flops=flops, bytes_accessed=moved, transcendentals=exps),
        name=name,
    )


def turned(heads, cosine, sine):
    return heads * cosine + pltpu.roll(heads, HEAD_DIM // 2, 1) * sine


def norm_rows(own, other, gain, half):
    width, rows = own.shape
    total = jnp.zeros((1, rows), jnp.float32)
    for source in (own, other):
        wide = source[...].astype(jnp.float32)
        total += jnp.sum(wide * wide, axis=0, keepdims=True)
    scale = lax.rsqrt(total / (2 * width) + norm_epsilon).T
    return [
        (source[...].T.astype(jnp.float32) * scale * gain[pl.ds(which, 1), :]).astype(
            jnp.bfloat16
        )
        for source, which in ((own, half), (other, 1 - half))
    ]


def key_value_kernel(own, other, gain, tables, key, value, kv_out, normed, angles, sem):
    half = lax.axis_index("tp")
    width = own.shape[0]
    step = key.shape[1] // 2
    table_copy = pltpu.make_async_copy(tables, angles, sem)
    table_copy.start()
    normed[0], normed[1] = norm_rows(own, other, gain, half)
    table_copy.wait()
    for index in range(4):
        weight = (key, value)[index // 2]
        cut = slice(index % 2 * step, (index % 2 + 1) * step)
        result = jnp.dot(
            normed[0],
            weight[pl.ds(pl.multiple_of(half * width, 16), width), cut],
            preferred_element_type=jnp.float32,
        )
        result += jnp.dot(
            normed[1],
            weight[pl.ds(pl.multiple_of((1 - half) * width, 16), width), cut],
            preferred_element_type=jnp.float32,
        )
        if index < 2:
            for head in range(step // HEAD_DIM):
                cut = slice(head * HEAD_DIM, (head + 1) * HEAD_DIM)
                kv_out[index, :, cut] = turned(result[:, cut], angles[0], angles[1]).astype(
                    jnp.bfloat16
                )
        else:
            kv_out[index] = result.astype(jnp.bfloat16).T


def key_value(own, other, gain, tables, weights):
    width, rows = own.shape
    depth, columns = weights[0].shape
    step = columns // 2
    return call(
        key_value_kernel,
        jax.ShapeDtypeStruct((4, rows, step), jnp.bfloat16),
        [vmem_spec()] * 3 + [hbm_spec()] + [vmem_spec()] * 2,
        [
            pltpu.VMEM((2, rows, width), jnp.bfloat16),
            pltpu.VMEM(tables.shape, jnp.float32),
            pltpu.SemaphoreType.DMA(()),
        ],
        4 * rows * depth * columns,
        4 * depth * columns + 4 * rows * depth,
        "key_value",
    )(own, other, gain, tables, *weights)


def query_kernel(count, own, other, gain, tables, *refs):
    pieces, (out, normed, angles, sem) = refs[: 2 * count], refs[2 * count :]
    table_copy = pltpu.make_async_copy(tables, angles, sem)
    table_copy.start()
    core = lax.axis_index("segment")
    half = lax.axis_index("tp")
    place = ring_position(lax.axis_index("seq"), count)
    chunks, depth = count // 2, normed.shape[2]
    for rows, which in zip(norm_rows(own, other, gain, half), (half, 1 - half)):
        for part in range(chunks):
            normed[which * chunks + part] = rows[:, part * depth : (part + 1) * depth]
    table_copy.wait()
    for side in range(2):
        total = None
        for step in range(count):
            term = jnp.dot(
                normed[ring_member(place - step, count)],
                pieces[side * count + step][0],
                preferred_element_type=jnp.float32,
            )
            total = term if total is None else total + term
        target = core if side == 0 else 1 - core
        for head in range(total.shape[1] // HEAD_DIM):
            cut = slice(head * HEAD_DIM, (head + 1) * HEAD_DIM)
            rows = turned(total[:, cut], angles[0], angles[1]).astype(jnp.bfloat16)
            out[target, cut, :] = rows.T


def query(state, other, gain, tables, own, came):
    count = len(own)
    width, rows = state.shape
    depth, columns = own[0].shape[1:]
    return call(
        functools.partial(query_kernel, count),
        jax.ShapeDtypeStruct((2, columns, rows), jnp.bfloat16),
        [vmem_spec()] * 3 + [hbm_spec()] + [vmem_spec()] * (2 * count),
        [
            pltpu.VMEM((count, rows, depth), jnp.bfloat16),
            pltpu.VMEM(tables.shape, jnp.float32),
            pltpu.SemaphoreType.DMA(()),
        ],
        4 * count * rows * depth * columns,
        4 * count * depth * columns + 2 * count * rows * depth,
        "query",
    )(state, other, gain, tables, *own, *came)


def head_cuts(head, half_heads, groups):
    group = head // GROUP
    side, within = group // groups, group % groups
    cut = slice(within * HEAD_DIM, (within + 1) * HEAD_DIM)
    half, place = head // half_heads, head % half_heads
    return half, slice(place * HEAD_DIM, (place + 1) * HEAD_DIM), side, cut


def score_bias(distance, reach, rows, lengths, boundary):
    batch = lax.axis_index("segment")
    seq = lax.axis_index("seq")
    key_ids = lax.broadcasted_iota(jnp.int32, (rows, rows), 0)
    query_ids = lax.broadcasted_iota(jnp.int32, (rows, rows), 1)
    start = boundary[batch]
    block = seq - distance
    length = jnp.where(block >= 0, lengths[batch, jnp.maximum(block, 0)], 0)
    seen = key_ids < length
    if distance == 0:
        seen &= key_ids <= query_ids
    if distance == reach:
        seen &= key_ids > query_ids + (distance * rows - WINDOW)
    seen &= (query_ids + seq * rows < start) | (key_ids + block * rows >= start)
    return jnp.where(seen, 0.0, hidden)


score_factor = math.log2(math.e) * HEAD_DIM ** (-0.5)


def attend_kernel(distances, reach, lengths, boundary, queries, *refs):
    count = len(distances)
    windows, (out, tops, totals, bias) = refs[:count], refs[count:]
    rows = queries.shape[2]
    half_heads = queries.shape[1] // HEAD_DIM
    groups = windows[0].shape[2] // HEAD_DIM
    for slot, distance in enumerate(distances):
        bias[slot] = score_bias(distance, reach, rows, lengths, boundary)
    for head in range(2 * half_heads):
        half, place, side, cut = head_cuts(head, half_heads, groups)
        scores = [
            jnp.dot(
                window[side, :, cut], queries[half, place, :], preferred_element_type=jnp.float32
            )
            + bias[slot]
            for slot, window in enumerate(windows)
        ]
        top = functools.reduce(jnp.maximum, scores)
        top = jnp.max(top, axis=0, keepdims=True)
        mixed = None
        total = None
        for score, window in zip(scores, windows):
            term = jnp.exp2((score - top) * score_factor)
            total = term if total is None else total + term
            product = jnp.dot(
                window[2 + side, cut, :],
                term.astype(jnp.bfloat16),
                preferred_element_type=jnp.float32,
            )
            mixed = product if mixed is None else mixed + product
        out[half, place, :] = mixed
        tops[pl.ds(head, 1), :] = top
        totals[pl.ds(head, 1), :] = jnp.sum(total, axis=0, keepdims=True)


def attend(lengths, boundary, queries, windows, distances, reach):
    rows = queries.shape[2]
    heads = 2 * queries.shape[1] // HEAD_DIM
    span = rows * len(windows)
    return call(
        functools.partial(attend_kernel, distances, reach),
        (
            jax.ShapeDtypeStruct(queries.shape, jnp.float32),
            jax.ShapeDtypeStruct((heads, rows), jnp.float32),
            jax.ShapeDtypeStruct((heads, rows), jnp.float32),
        ),
        [smem_spec()] * 2 + [vmem_spec()] * (1 + len(windows)),
        [pltpu.VMEM((len(windows), rows, rows), jnp.float32)],
        4 * heads * rows * span * HEAD_DIM,
        2 * sum(w.size for w in windows) + 6 * queries.size,
        "attend",
        heads * rows * span,
    )(lengths, boundary, queries, *windows)


def out_kernel(
    count, distance, reach, lengths, boundary, queries, window, sums, tops, totals, state, *refs
):
    pieces, (leave, stay, mixed, chunks) = refs[: 2 * count], refs[2 * count :]
    core = lax.axis_index("segment")
    half = lax.axis_index("tp")
    seq = lax.axis_index("seq")
    place = ring_position(seq, count)
    rows = queries.shape[2]
    half_heads = queries.shape[1] // HEAD_DIM
    groups = window.shape[2] // HEAD_DIM
    bias = score_bias(distance, reach, rows, lengths, boundary)
    kept = lax.broadcasted_iota(jnp.int32, (1, rows), 1) < lengths[core, seq]
    for head in range(2 * half_heads):
        side_half, spot, side, cut = head_cuts(head, half_heads, groups)
        score = bias + jnp.dot(
            window[side, :, cut], queries[side_half, spot, :], preferred_element_type=jnp.float32
        )
        before = tops[pl.ds(head, 1), :]
        top = jnp.maximum(before, jnp.max(score, axis=0, keepdims=True))
        fade = jnp.exp2((before - top) * score_factor)
        term = jnp.exp2((score - top) * score_factor)
        total = totals[pl.ds(head, 1), :] * fade + jnp.sum(term, axis=0, keepdims=True)
        product = jnp.dot(
            window[2 + side, cut, :], term.astype(jnp.bfloat16), preferred_element_type=jnp.float32
        )
        result = (sums[side_half, spot, :] * fade + product) / total
        mixed[side_half, spot, :] = jnp.where(kept, result, 0.0).astype(jnp.bfloat16)
    for step in range(count):
        far = pieces[step].shape[0] - 1
        result = jnp.dot(pieces[step][far], mixed[core], preferred_element_type=jnp.float32)
        result += jnp.dot(
            pieces[count + step][far], mixed[1 - core], preferred_element_type=jnp.float32
        )
        chunks[ring_member(place - step, count)] = result
    parts = count // 2
    depth = chunks.shape[1]
    for part in range(parts):
        cut = slice(part * depth, (part + 1) * depth)
        leave[cut, :] = chunks[(1 - half) * parts + part].astype(jnp.bfloat16)
        stay[cut, :] = state[cut, :].astype(jnp.float32) + chunks[half * parts + part]


def out_project(lengths, boundary, queries, window, distance, reach, partial, state, own, came):
    count = len(own)
    columns, rows = queries.shape[1:]
    depth = own[0].shape[1]
    return call(
        functools.partial(out_kernel, count, distance, reach),
        (
            jax.ShapeDtypeStruct(state.shape, jnp.bfloat16),
            jax.ShapeDtypeStruct(state.shape, jnp.float32),
        ),
        [smem_spec()] * 2 + [vmem_spec()] * (6 + 2 * count),
        [
            pltpu.VMEM(queries.shape, jnp.bfloat16),
            pltpu.VMEM((count, depth, rows), jnp.float32),
        ],
        4 * count * rows * depth * columns + 8 * rows * rows * columns,
        4 * count * depth * columns + 8 * state.size,
        "out_project",
    )(lengths, boundary, queries, window, *partial, state, *own, *came)


def closed(*values):
    return lax.optimization_barrier(values)


class Ring:
    def __init__(self, shard, count):
        order = ring_order(count)
        self.onward = [(order[i], order[(i + 1) % count]) for i in range(count)]
        self.back = [(b, a) for a, b in self.onward]
        self.count = count
        self.forward = [shard]
        self.backward = [shard]
        self.far = None

    def step(self):
        if len(self.forward) < self.count // 2:
            self.forward.append(lax.ppermute(self.forward[-1], "seq", self.onward))
            self.backward.append(lax.ppermute(self.backward[-1], "seq", self.back))
        elif self.far is None:
            self.far = (
                lax.ppermute(self.forward[-1][:1], "seq", self.onward),
                lax.ppermute(self.backward[-1][1:], "seq", self.back),
            )

    def close(self, *values):
        if self.far is None:
            self.forward[-1], self.backward[-1], *rest = closed(
                self.forward[-1], self.backward[-1], *values
            )
        else:
            far_query, far_out, *rest = closed(*self.far, *values)
            self.far = (far_query, far_out)
        return rest

    def pieces(self):
        while self.far is None:
            self.step()
        far_query, far_out = self.far
        before, behind = self.forward, self.backward[:0:-1]
        return (before + [far_query] + behind, before + [far_out] + behind)


def per_device(
    inputs, lengths, boundary, attn_gain, query_weight, key_weight, value_weight, out_weight
):
    core = lax.axis_index("segment")
    seq_index = lax.axis_index("seq")
    count = lax.axis_size("seq")
    block_len = inputs.shape[1]
    first_core = core == 0

    def across_chip(value):
        return lax.ppermute(value, "segment", SWAP)

    def across_tp(value):
        return lax.ppermute(value, "tp", SWAP)

    def both_cores(pieces):
        own_query, own_out = pieces
        middle = count // 2
        came = [across_chip(piece) for piece in own_query]
        came_out = came[:middle] + [across_chip(own_out[middle])] + came[middle + 1 :]
        return own_query, came, own_out, came_out

    state = lax.dynamic_index_in_dim(jnp.swapaxes(inputs, 1, 2), core, 0, keepdims=False)
    state_other = across_tp(state)

    columns = query_weight.shape[2] // 2
    both = jnp.stack([query_weight[0], out_weight[0].T])
    mine = lax.dynamic_slice_in_dim(both, core * columns, columns, 2)
    given = lax.dynamic_slice_in_dim(both, (1 - core) * columns, columns, 2)
    came = across_chip(given)
    came, key_shard, value_shard, gain_shard = closed(
        came, key_weight[0], value_weight[0], attn_gain
    )
    shards = [jnp.where(first_core, mine, came), jnp.where(first_core, came, mine)]
    key_came, value_came = across_chip(key_shard), across_chip(value_shard)
    key_value_weights = [
        (jnp.where(first_core, key_shard, key_came), jnp.where(first_core, value_shard, value_came)),
        (jnp.where(first_core, key_came, key_shard), jnp.where(first_core, value_came, value_shard)),
    ]
    gain_came = across_chip(gain_shard)
    gains = [
        jnp.where(first_core, attn_gain, gain_came).reshape(2, -1),
        jnp.where(first_core, gain_came, attn_gain).reshape(2, -1),
    ]

    half_dim = HEAD_DIM // 2
    inverse = jnp.exp(
        -math.log(10000.0) * jnp.arange(half_dim, dtype=jnp.float32) * (2.0 / HEAD_DIM)
    )
    slots = seq_index * block_len + jnp.arange(block_len, dtype=jnp.int32)
    angles = slots.astype(jnp.float32)[:, None] * inverse[None, :]
    cosine, sine = jnp.cos(angles), jnp.sin(angles)
    tables = jnp.stack(
        [
            jnp.concatenate([cosine, cosine], axis=1),
            jnp.concatenate([-sine, sine], axis=1),
        ]
    )

    up = [(i, (i + 2) % count) for i in range(count)]
    beside = [(i, i ^ 1) for i in range(count)]
    even = seq_index % 2 == 0
    reach = max(1, WINDOW // block_len)

    def shifted(value):
        return lax.ppermute(value, "seq", up)

    def swapped(near, far):
        return lax.ppermute(jnp.where(even, near, far), "seq", beside)

    ring = Ring(shards[0], count)
    ring.step()
    states = []
    for layer in range(LAYERS):
        ring.step()
        kv_rows = key_value(
            state, state_other, gains[layer], tables, key_value_weights[layer]
        )
        evens, odds = [kv_rows], []
        for _ in range(reach // 2):
            evens.append(shifted(evens[-1]))
            if len(evens) > 2:
                odds.append(swapped(evens[-3], evens[-2]))
                evens[-1], odds[-1] = ring.close(evens[-1], odds[-1])
            else:
                (evens[-1],) = ring.close(evens[-1])
            ring.step()
        odds.append(swapped(evens[-2], evens[-1]))
        query_own, query_came, out_own, out_came = both_cores(ring.pieces())
        queries = query(state, state_other, gains[layer], tables, query_own, query_came)
        late = odds.pop()
        blocks = {2 * place: block for place, block in enumerate(evens)}
        blocks.update({2 * place + 1: block for place, block in enumerate(odds)})
        partial = attend(
            lengths, boundary, queries, list(blocks.values()), tuple(blocks), reach
        )
        if layer + 1 < LAYERS:
            late, shard, *partial = closed(late, shards[layer + 1], *partial)
            ring = Ring(shard, count)
            ring.step()
        leave, stay = out_project(
            lengths, boundary, queries, late, reach - 1, reach, partial, state, out_own, out_came
        )
        arrived = across_tp(leave)
        if layer + 1 < LAYERS:
            arrived, *key_value_weights[layer + 1] = ring.close(
                arrived, *key_value_weights[layer + 1]
            )
            ring.step()
        state = (stay + arrived.astype(jnp.float32)).astype(jnp.bfloat16)
        states.append(state)
        if layer + 1 < LAYERS:
            state_other = across_tp(state)
            (state_other,) = ring.close(state_other)

    first_came = lax.ppermute(states[0], "segment", [(1, 0)])
    last_came = lax.ppermute(states[1], "segment", [(0, 1)])
    both = jnp.stack(
        [
            jnp.where(first_core, states[0], last_came),
            jnp.where(first_core, first_came, states[1]),
        ]
    )
    return jnp.swapaxes(both, 1, 2)[None]


def solution(mesh):
    return jax.shard_map(
        per_device,
        mesh=mesh,
        in_specs=(
            P(None, "seq", "tp"),
            P(),
            P(),
            P("segment", None),
            P("segment", "seq", "tp"),
            P("segment", None, "tp"),
            P("segment", None, "tp"),
            P("segment", "tp", "seq"),
        ),
        out_specs=P("segment", None, "seq", "tp"),
        check_vma=False,
    )
```

time: 279 us -> 255 us (0.914)
  starting transfers between devices: 81.8 us -> 48.1 us
  waiting for transfers between devices: 118 us -> 140 us
  local copies, waits for them, and re-layouts: 18.8 us -> 9.03 us
  Pallas kernels: 49.2 us -> 41.1 us
  other arithmetic: 9.55 us -> 15.5 us
    ppermute x24, starting transfers between devices: 48 us -> 17 us  [the longest x6 5.82 us: step(): self.forward.append(lax.ppermute(self.forward[-1], 'seq', self.onward))]
    ppermute x24, waiting for transfers between devices: 65.2 us -> 88.5 us  [the longest x4 26 us: shifted(): return lax.ppermute(value, 'seq', up)]
    pallas_call x8, Pallas kernels: 49.2 us -> 41.1 us  [the longest x2 11.9 us: out_project(): call(functools.partial(out_kernel, count, distance, reach), (jax.ShapeDty...]
    select_n x2 -> x6, other arithmetic: 1.42 us -> 9.41 us  [the longest x1 3.99 us: per_device(): jnp.where(first_core, key_came, key_shard)]
    ppermute x6 -> x0, local copies, waits for them, and re-layouts: 7.23 us -> none  [the longest x4 5.45 us: across_tp(): return lax.ppermute(value, 'tp', SWAP)]
    unnamed x56 -> x42, local copies, waits for them, and re-layouts: 2.94 us -> 5.92 us
  transfers between devices with their start and end apart: 52 -> 52, of which waited for: 17 -> 20; matrix products, arithmetic and copies ran while one was open for 7% -> 6% of each run, Pallas kernels for 15% -> 14%
where the time goes in v2:
time: 255 us; the launch traced here: 254 us
  waiting for transfers between devices  140 us (55%)
  starting transfers between devices  48.1 us (19%)
  Pallas kernels  41.1 us (16%)
  other arithmetic  15.5 us (6%)
  local copies, waits for them, and re-layouts  9.03 us (4%)
    ppermute x4, waiting for transfers between devices, across_tp(): return lax.ppermute(value, 'tp', SWAP)  42.8 us
    ppermute x4, waiting for transfers between devices, shifted(): return lax.ppermute(value, 'seq', up)  26 us
    ppermute x22, starting transfers between devices, across_chip(): return lax.ppermute(value, 'segment', SWAP)  22.5 us
    ppermute x4, waiting for transfers between devices, swapped(): return lax.ppermute(jnp.where(even, near, far), 'seq', beside)  22.1 us
    ppermute x2, waiting for transfers between devices, step(): lax.ppermute(self.forward[-1][:1], 'seq', self.onward)  14.1 us
    ppermute x2, waiting for transfers between devices, step(): lax.ppermute(self.backward[-1][1:], 'seq', self.back)  12.8 us
    pallas_call x2, Pallas kernels, out_project(): call(functools.partial(out_kernel, count, distance, reach), (jax.ShapeDty...  11.9 us
    ppermute x6, waiting for transfers between devices, step(): self.forward.append(lax.ppermute(self.forward[-1], 'seq', self.onward))  11.7 us
  transfers between devices with their start and end apart: 52, of which 20 were waited for; matrix products, arithmetic and copies ran while one was open for 6% of the time, Pallas kernels for 14%

profile of v2, /device:TPU:1, one launch (start us, length us, event | category | flops | bytes accessed | tf_op | source)
XLA Modules:
  0.0 254.4 jit_solution(915024422118446546)
XLA Ops:
  0.0 1.3 fusion.1
  1.4 2.2 collective-permute-done.1
  4.2 2.3 broadcast_select_fusion.4
  6.5 2.4 collective-permute-start.3
  11.2 1.5 collective-permute-done.2
  12.7 2.3 collective-permute-start
  15.2 9.3 %collective-permute-done.3.refs_1_ = bf16[2,336,512]{2,1,0:T(8,128)(2,1)} collective-permute-done((bf16[2,336,512]{2,1,0:T(8,128)(2,1)S(1)}, bf16[2,336,512]{2,1,0:T(8,128)(2,1)}, u32[]{:S(2)}, u32[]{:S(2)}) %collective-permute-start.3) | collective-permute-done | bytes 688160 | tf_op jit(solution)/shard_map/ppermute | solution.py:343
  24.5 1.2 collective-permute-start.4
  25.9 3.1 %broadcast_select_fusion = (bf16[2688,512]{1,0:T(8,128)(2,1)S(1)}, bf16[2688,512]{1,0:T(8,128)(2,1)S(1)}) fusion(bf16[2688,512]{1,0:T(8,128)(2,1)} %collective-permute-done.8, bf16[2688,512]{1,0:T(8,128)(2,1)} %bitcast.24, pred[]{:T(512)S(6)} %eq.8), kind=kLoop, calls=%fused_computation | loop fusion | flops 2752512 | bytes 11010049 | tf_op jit(solution)/shard_map/jit(_where)/select_n | solution.py:406
  29.4 4.0 %broadcast_select_fusion.1 = (bf16[2688,512]{1,0:T(8,128)(2,1)}, bf16[2688,512]{1,0:T(8,128)(2,1)S(1)}) fusion(bf16[2688,512]{1,0:T(8,128)(2,1)} %collective-permute-done.7, bf16[2688,512]{1,0:T(8,128)(2,1)S(1)} %bitcast.26, pred[]{:T(512)S(6)} %eq.8), kind=kLoop, calls=%fused_computation.1 | loop fusion | flops 2752512 | bytes 11010049 | tf_op jit(solution)/shard_map/jit(_where)/select_n | solution.py:406
  33.4 4.8 %key_value.2.refs_0_ = bf16[4,256,256]{2,1,0:T(8,128)(2,1)} custom-call(bf16[1344,256]{1,0:T(8,128)(2,1)} %dynamic-slice_bitcast_fusion.own.state, bf16[1344,256]{1,0:T(8,128)(2,1)} %collective-permute-done.other, f32[2,1344]{1,0:T(2,128)S(1)} %reshape.16.gain, f32[2,256,128]{2,1,0:T(8,128)S(1)} %pad_maximum_fusion.tables, ...), custom_call_target="tpu_custom_call" | custom-call | flops 1409286144 | bytes 8257536 | tf_op jit(solution)/shard_map/key_value/pallas_call | solution.py:118
  38.1 1.3 collective-permute-start.9
  39.4 1.5 collective-permute-done.4.refs_2_
  41.5 13.3 %collective-permute-done.9.refs_1_ = bf16[4,256,256]{2,1,0:T(8,128)(2,1)} collective-permute-done((bf16[4,256,256]{2,1,0:T(8,128)(2,1)}, bf16[4,256,256]{2,1,0:T(8,128)(2,1)}, u32[]{:S(2)}, u32[]{:S(2)}) %collective-permute-start.9) | collective-permute-done | bytes 524320 | tf_op jit(solution)/shard_map/ppermute | solution.py:434
  55.8 1.5 collective-permute-start.13
  58.2 2.4 collective-permute-start.15
  60.6 20.1 %collective-permute-done.13.refs_3_ = bf16[4,256,256]{2,1,0:T(8,128)(2,1)S(1)} collective-permute-done((bf16[4,256,256]{2,1,0:T(8,128)(2,1)S(1)}, bf16[4,256,256]{2,1,0:T(8,128)(2,1)S(1)}, u32[]{:S(2)}, u32[]{:S(2)}) %collective-permute-start.13) | collective-permute-done | bytes 524320 | tf_op jit(solution)/shard_map/ppermute | solution.py:437
  80.7 3.3 %collective-permute-start.16 = (bf16[2,336,512]{2,1,0:T(8,128)(2,1)}, bf16[2,336,512]{2,1,0:T(8,128)(2,1)S(1)}, u32[]{:S(2)}, u32[]{:S(2)}) collective-permute-start(bf16[2,336,512]{2,1,0:T(8,128)(2,1)} %collective-permute-done.3.refs_1_), channel_id=1, source_target_pairs={{0,16},{16,0},{1,17},{17,1},{2,18},{18,2},{3,19},{19,3},{4,20},{20... | collective-permute-start | bytes 2064392 | tf_op jit(solution)/shard_map/ppermute | solution.py:379
  84.5 1.3 collective-permute-done.11.refs_5_
  85.8 1.6 collective-permute-start.21
  88.2 1.6 collective-permute-start.24
  89.8 7.4 %collective-permute-done.14.refs_4_ = bf16[1,336,512]{2,1,0:T(8,128)(2,1)S(1)} collective-permute-done((bf16[1,336,512]{2,1,0:T(8,128)(2,1)S(1)}, bf16[1,336,512]{2,1,0:T(8,128)(2,1)S(1)}, u32[]{:S(2)}, u32[]{:S(2)}) %collective-permute-start.14) | collective-permute-done | bytes 344096 | tf_op jit(solution)/shard_map/ppermute | solution.py:347
  99.3 5.9 %query.2.queries = bf16[2,512,256]{2,1,0:T(8,128)(2,1)S(1)} custom-call(bf16[1344,256]{1,0:T(8,128)(2,1)} %dynamic-slice_bitcast_fusion.own.state, bf16[1344,256]{1,0:T(8,128)(2,1)} %collective-permute-done.other, f32[2,1344]{1,0:T(2,128)S(1)} %reshape.16.gain, f32[2,256,128]{2,1,0:T(8,128)S(1)} %pad_maximum_fusion.tables, ...), custom_call_target="tpu_custom_call" | custom-call | flops 1409286144 | bytes 6881280 | tf_op jit(solution)/shard_map/query/pallas_call | solution.py:165
  105.2 5.6 %attend.2 = (f32[2,512,256]{2,1,0:T(8,128)S(1)}, f32[8,256]{1,0:T(8,128)S(1)}, f32[8,256]{1,0:T(8,128)S(1)}) custom-call(s32[2,8]{1,0:T(2,128)S(1)} %copy-done.15, s32[2]{0:T(128)S(1)} %copy-done.16, bf16[2,512,256]{2,1,0:T(8,128)(2,1)S(1)} %query.2.queries, bf16[4,256,256]{2,1,0:T(8,128)(2,1)} %key_value.2.refs_0_, ...), custom_call_target="tpu_custom_call" | custom-call | flops 1073741824 | bytes 3670016 | tf_op jit(solution)/shard_map/attend/pallas_call | solution.py:247
  110.8 1.9 collective-permute-done.23.window
  112.8 6.1 %out_project.2 = (bf16[1344,256]{1,0:T(8,128)(2,1)S(1)}, f32[1344,256]{1,0:T(8,128)S(1)}) custom-call(s32[2,8]{1,0:T(2,128)S(1)} %copy-done.15, s32[2]{0:T(128)S(1)} %copy-done.16, bf16[2,512,256]{2,1,0:T(8,128)(2,1)S(1)} %query.2.queries, bf16[4,256,256]{2,1,0:T(8,128)(2,1)S(1)} %collective-permute-done.23.window, ...), custom_call_target="tpu_custom_call" | custom-call | flops 1677721600 | bytes 8257536 | tf_op jit(solution)/shard_map/out_project/pallas_call | solution.py:310
  118.8 1.3 collective-permute-start.28
  120.1 1.5 collective-permute-start.27
  121.6 13.5 %collective-permute-done.28 = bf16[1344,256]{1,0:T(8,128)(2,1)S(1)} collective-permute-done((bf16[1344,256]{1,0:T(8,128)(2,1)S(1)}, bf16[1344,256]{1,0:T(8,128)(2,1)S(1)}, u32[]{:S(2)}, u32[]{:S(2)}) %collective-permute-start.28) | collective-permute-done | bytes 688160 | tf_op jit(solution)/shard_map/ppermute | solution.py:382
  138.3 12.9 %collective-permute-done.31.other = bf16[1344,256]{1,0:T(8,128)(2,1)S(1)} collective-permute-done((bf16[1344,256]{1,0:T(8,128)(2,1)S(1)}, bf16[1344,256]{1,0:T(8,128)(2,1)S(1)}, u32[]{:S(2)}, u32[]{:S(2)}) %collective-permute-start.31) | collective-permute-done | bytes 688160 | tf_op jit(solution)/shard_map/ppermute | solution.py:382
  153.6 1.8 copy-done.2
  157.4 2.6 %key_value.3.refs_0_ = bf16[4,256,256]{2,1,0:T(8,128)(2,1)S(1)} custom-call(bf16[1344,256]{1,0:T(8,128)(2,1)S(1)} %add_convert_fusion.1.own.state, bf16[1344,256]{1,0:T(8,128)(2,1)S(1)} %copy-done.10, f32[2,1344]{1,0:T(2,128)S(1)} %reshape.17.gain, f32[2,256,128]{2,1,0:T(8,128)S(1)} %copy-done.4, bf16[2688,512]{1,0:T(8,128)(2,1)S(1)} %copy-done.2, ...), custom_call_target="tpu_custom_call" | custom-call | flops 1409286144 | bytes 8257536 | tf_op jit(solution)/shard_map/key_value/pallas_call | solution.py:118
  160.0 1.2 collective-permute-start.34
  161.2 4.0 %collective-permute-start.39 = (bf16[2,336,512]{2,1,0:T(8,128)(2,1)S(1)}, bf16[2,336,512]{2,1,0:T(8,128)(2,1)S(1)}, u32[]{:S(2)}, u32[]{:S(2)}) collective-permute-start(bf16[2,336,512]{2,1,0:T(8,128)(2,1)S(1)} %copy-done.6), channel_id=1, source_target_pairs={{0,16},{16,0},{1,17},{17,1},{2,18},{18,2},{3,19},{19,3},{4,20},{20... | collective-permute-start | bytes 2064392 | tf_op jit(solution)/shard_map/ppermute | solution.py:379
  165.4 12.7 %collective-permute-done.34.refs_1_ = bf16[4,256,256]{2,1,0:T(8,128)(2,1)S(1)} collective-permute-done((bf16[4,256,256]{2,1,0:T(8,128)(2,1)S(1)}, bf16[4,256,256]{2,1,0:T(8,128)(2,1)S(1)}, u32[]{:S(2)}, u32[]{:S(2)}) %collective-permute-start.34) | collective-permute-done | bytes 524320 | tf_op jit(solution)/shard_map/ppermute | solution.py:434
  178.1 4.8 %collective-permute-start.46 = (bf16[2,336,512]{2,1,0:T(8,128)(2,1)S(1)}, bf16[2,336,512]{2,1,0:T(8,128)(2,1)S(1)}, u32[]{:S(2)}, u32[]{:S(2)}) collective-permute-start(bf16[2,336,512]{2,1,0:T(8,128)(2,1)S(1)} %copy-done.14), channel_id=1, source_target_pairs={{0,16},{16,0},{1,17},{17,1},{2,18},{18,2},{3,19},{19,3},{4,20},{20... | collective-permute-start | bytes 2064392 | tf_op jit(solution)/shard_map/ppermute | solution.py:379
  184.0 1.5 collective-permute-start.38
  186.9 6.7 %collective-permute-done.35.refs_4_ = bf16[1,336,512]{2,1,0:T(8,128)(2,1)S(1)} collective-permute-done((bf16[1,336,512]{2,1,0:T(8,128)(2,1)S(1)}, bf16[1,336,512]{2,1,0:T(8,128)(2,1)S(1)}, u32[]{:S(2)}, u32[]{:S(2)}) %collective-permute-start.35) | collective-permute-done | bytes 344096 | tf_op jit(solution)/shard_map/ppermute | solution.py:347
  194.8 12.8 %collective-permute-done.36.refs_4_ = bf16[1,336,512]{2,1,0:T(8,128)(2,1)S(1)} collective-permute-done((bf16[1,336,512]{2,1,0:T(8,128)(2,1)S(1)}, bf16[1,336,512]{2,1,0:T(8,128)(2,1)S(1)}, u32[]{:S(2)}, u32[]{:S(2)}) %collective-permute-start.36) | collective-permute-done | bytes 344096 | tf_op jit(solution)/shard_map/ppermute | solution.py:348
  209.3 1.2 collective-permute-done.45.refs_14_
  212.0 2.3 collective-permute-start.51
  214.4 5.4 %query.3.queries = bf16[2,512,256]{2,1,0:T(8,128)(2,1)S(1)} custom-call(bf16[1344,256]{1,0:T(8,128)(2,1)S(1)} %add_convert_fusion.1.own.state, bf16[1344,256]{1,0:T(8,128)(2,1)S(1)} %copy-done.10, f32[2,1344]{1,0:T(2,128)S(1)} %reshape.17.gain, f32[2,256,128]{2,1,0:T(8,128)S(1)} %copy-done.4, bf16[2,336,512]{2,1,0:T(8,128)(2,1)S(1)} %copy-done.6, ...), custom_call_target="tpu_custom_call" | custom-call | flops 1409286144 | bytes 6881280 | tf_op jit(solution)/shard_map/query/pallas_call | solution.py:165
  219.8 5.0 %attend.3 = (f32[2,512,256]{2,1,0:T(8,128)S(1)}, f32[8,256]{1,0:T(8,128)S(1)}, f32[8,256]{1,0:T(8,128)S(1)}) custom-call(s32[2,8]{1,0:T(2,128)S(1)} %copy-done.15, s32[2]{0:T(128)S(1)} %copy-done.16, bf16[2,512,256]{2,1,0:T(8,128)(2,1)S(1)} %query.3.queries, bf16[4,256,256]{2,1,0:T(8,128)(2,1)S(1)} %key_value.3.refs_0_, ...), custom_call_target="tpu_custom_call" | custom-call | flops 1073741824 | bytes 3670016 | tf_op jit(solution)/shard_map/attend/pallas_call | solution.py:247
  224.8 5.8 %out_project.3 = (bf16[1344,256]{1,0:T(8,128)(2,1)S(1)}, f32[1344,256]{1,0:T(8,128)S(1)}) custom-call(s32[2,8]{1,0:T(2,128)S(1)} %copy-done.15, s32[2]{0:T(128)S(1)} %copy-done.16, bf16[2,512,256]{2,1,0:T(8,128)(2,1)S(1)} %query.3.queries, bf16[4,256,256]{2,1,0:T(8,128)(2,1)S(1)} %collective-permute-done.47.window, ...), custom_call_target="tpu_custom_call" | custom-call | flops 1677721600 | bytes 8257536 | tf_op jit(solution)/shard_map/out_project/pallas_call | solution.py:310
  231.6 16.5 %collective-permute-done.49 = bf16[1344,256]{1,0:T(8,128)(2,1)S(1)} collective-permute-done((bf16[1344,256]{1,0:T(8,128)(2,1)S(1)}, bf16[1344,256]{1,0:T(8,128)(2,1)S(1)}, u32[]{:S(2)}, u32[]{:S(2)}) %collective-permute-start.49) | collective-permute-done | bytes 688160 | tf_op jit(solution)/shard_map/ppermute | solution.py:382
  248.4 1.3 collective-permute-start.50
  249.7 2.7 %collective-permute-done.50 = bf16[1344,256]{1,0:T(8,128)(2,1)S(1)} collective-permute-done((bf16[1344,256]{1,0:T(8,128)(2,1)S(1)}, bf16[1344,256]{1,0:T(8,128)(2,1)S(1)}, u32[]{:S(2)}, u32[]{:S(2)}) %collective-permute-start.50) | collective-permute-done | bytes 688160 | tf_op jit(solution)/shard_map/ppermute | solution.py:485
  252.6 1.2 maximum_bitcast_fusion
  (131 shorter events, 26.1 us)
Async XLA Ops:
  3.6 22.3 %collective-permute-start.8 = (bf16[2688,512]{1,0:T(8,128)(2,1)}, bf16[2688,512]{1,0:T(8,128)(2,1)}, u32[]{:S(2)}, u32[]{:S(2)}) collective-permute-start(bf16[2688,512]{1,0:T(8,128)(2,1)} %bitcast.23), channel_id=1, source_target_pairs={{0,16},{16,0},{1,17},{17,1},{2,18},{18,2},{3,19},{19,3},{4,20},{20... | collective-permute-start | bytes 8257544 | tf_op jit(solution)/shard_map/ppermute | solution.py:379
  3.8 25.3 %collective-permute-start.7 = (bf16[2688,512]{1,0:T(8,128)(2,1)}, bf16[2688,512]{1,0:T(8,128)(2,1)}, u32[]{:S(2)}, u32[]{:S(2)}) collective-permute-start(bf16[2688,512]{1,0:T(8,128)(2,1)} %bitcast.25), channel_id=1, source_target_pairs={{0,16},{16,0},{1,17},{17,1},{2,18},{18,2},{3,19},{19,3},{4,20},{20... | collective-permute-start | bytes 8257544 | tf_op jit(solution)/shard_map/ppermute | solution.py:379
  6.5 18.0 %collective-permute-start.3 = (bf16[2,336,512]{2,1,0:T(8,128)(2,1)S(1)}, bf16[2,336,512]{2,1,0:T(8,128)(2,1)}, u32[]{:S(2)}, u32[]{:S(2)}) collective-permute-start(bf16[2,336,512]{2,1,0:T(8,128)(2,1)S(1)} %get-tuple-element.96.refs_0_), channel_id=1, source_target_pairs={{0,4},{4,8},{8,12},{12,14},{14,10},{10,6},{6,2},{2,0},{1,5},{5,9},... | collective-permute-start | bytes 2064392 | tf_op jit(solution)/shard_map/ppermute | solution.py:343
  8.9 16.8 %collective-permute-start.5 = (bf16[2,336,512]{2,1,0:T(8,128)(2,1)S(1)}, bf16[2,336,512]{2,1,0:T(8,128)(2,1)}, u32[]{:S(2)}, u32[]{:S(2)}) collective-permute-start(bf16[2,336,512]{2,1,0:T(8,128)(2,1)S(1)} %get-tuple-element.96.refs_0_), channel_id=1, source_target_pairs={{4,0},{8,4},{12,8},{14,12},{10,14},{6,10},{2,6},{0,2},{5,1},{9,5},... | collective-permute-start | bytes 2064392 | tf_op jit(solution)/shard_map/ppermute | solution.py:344
  12.7 20.7 %collective-permute-start = (bf16[1344,256]{1,0:T(8,128)(2,1)}, bf16[1344,256]{1,0:T(8,128)(2,1)}, u32[]{:S(2)}, u32[]{:S(2)}) collective-permute-start(bf16[1344,256]{1,0:T(8,128)(2,1)} %dynamic-slice_bitcast_fusion.own.state), channel_id=1, source_target_pairs={{0,1},{1,0},{2,3},{3,2},{4,5},{5,4},{6,7},{7,6},{8,9},{9,8},{10,11... | collective-permute-start | bytes 2064392 | tf_op jit(solution)/shard_map/ppermute | solution.py:382
  24.5 16.4 %collective-permute-start.4 = (bf16[2,336,512]{2,1,0:T(8,128)(2,1)}, bf16[2,336,512]{2,1,0:T(8,128)(2,1)}, u32[]{:S(2)}, u32[]{:S(2)}) collective-permute-start(bf16[2,336,512]{2,1,0:T(8,128)(2,1)} %collective-permute-done.3.refs_1_), channel_id=1, source_target_pairs={{0,4},{4,8},{8,12},{12,14},{14,10},{10,6},{6,2},{2,0},{1,5},{5,9},... | collective-permute-start | bytes 2064392 | tf_op jit(solution)/shard_map/ppermute | solution.py:343
  25.7 15.8 %collective-permute-start.6 = (bf16[2,336,512]{2,1,0:T(8,128)(2,1)}, bf16[2,336,512]{2,1,0:T(8,128)(2,1)}, u32[]{:S(2)}, u32[]{:S(2)}) collective-permute-start(bf16[2,336,512]{2,1,0:T(8,128)(2,1)} %collective-permute-done.5.refs_7_), channel_id=1, source_target_pairs={{4,0},{8,4},{12,8},{14,12},{10,14},{6,10},{2,6},{0,2},{5,1},{9,5},... | collective-permute-start | bytes 2064392 | tf_op jit(solution)/shard_map/ppermute | solution.py:344
  38.1 16.6 %collective-permute-start.9 = (bf16[4,256,256]{2,1,0:T(8,128)(2,1)}, bf16[4,256,256]{2,1,0:T(8,128)(2,1)}, u32[]{:S(2)}, u32[]{:S(2)}) collective-permute-start(bf16[4,256,256]{2,1,0:T(8,128)(2,1)} %key_value.2.refs_0_), channel_id=1, source_target_pairs={{0,4},{2,6},{4,8},{6,10},{8,12},{10,14},{12,0},{14,2},{1,5},{3,7},... | collective-permute-start | bytes 1572872 | tf_op jit(solution)/shard_map/ppermute | solution.py:434
  54.7 29.3 %collective-permute-start.10 = (bf16[2,336,512]{2,1,0:T(8,128)(2,1)}, bf16[2,336,512]{2,1,0:T(8,128)(2,1)S(1)}, u32[]{:S(2)}, u32[]{:S(2)}) collective-permute-start(bf16[2,336,512]{2,1,0:T(8,128)(2,1)} %collective-permute-done.4.refs_2_), channel_id=1, source_target_pairs={{0,4},{4,8},{8,12},{12,14},{14,10},{10,6},{6,2},{2,0},{1,5},{5,9},... | collective-permute-start | bytes 2064392 | tf_op jit(solution)/shard_map/ppermute | solution.py:343
  55.8 24.9 %collective-permute-start.13 = (bf16[4,256,256]{2,1,0:T(8,128)(2,1)S(1)}, bf16[4,256,256]{2,1,0:T(8,128)(2,1)S(1)}, u32[]{:S(2)}, u32[]{:S(2)}) collective-permute-start(bf16[4,256,256]{2,1,0:T(8,128)(2,1)S(1)} %broadcast_select_fusion.9), channel_id=1, source_target_pairs={{0,2},{2,0},{4,6},{6,4},{8,10},{10,8},{12,14},{14,12},{1,3},{3,1},... | collective-permute-start | bytes 1572872 | tf_op jit(solution)/shard_map/ppermute | solution.py:437
  57.3 26.7 %collective-permute-start.12 = (bf16[4,256,256]{2,1,0:T(8,128)(2,1)}, bf16[4,256,256]{2,1,0:T(8,128)(2,1)S(1)}, u32[]{:S(2)}, u32[]{:S(2)}) collective-permute-start(bf16[4,256,256]{2,1,0:T(8,128)(2,1)} %collective-permute-done.9.refs_1_), channel_id=1, source_target_pairs={{0,4},{2,6},{4,8},{6,10},{8,12},{10,14},{12,0},{14,2},{1,5},{3,7},... | collective-permute-start | bytes 1572872 | tf_op jit(solution)/shard_map/ppermute | solution.py:434
  58.1 27.7 %collective-permute-start.11 = (bf16[2,336,512]{2,1,0:T(8,128)(2,1)}, bf16[2,336,512]{2,1,0:T(8,128)(2,1)S(1)}, u32[]{:S(2)}, u32[]{:S(2)}) collective-permute-start(bf16[2,336,512]{2,1,0:T(8,128)(2,1)} %collective-permute-done.6.refs_6_), channel_id=1, source_target_pairs={{4,0},{8,4},{12,8},{14,12},{10,14},{6,10},{2,6},{0,2},{5,1},{9,5},... | collective-permute-start | bytes 2064392 | tf_op jit(solution)/shard_map/ppermute | solution.py:344
  58.2 29.3 %collective-permute-start.15 = (bf16[2,336,512]{2,1,0:T(8,128)(2,1)S(1)}, bf16[2,336,512]{2,1,0:T(8,128)(2,1)S(1)}, u32[]{:S(2)}, u32[]{:S(2)}) collective-permute-start(bf16[2,336,512]{2,1,0:T(8,128)(2,1)S(1)} %copy-done.8), channel_id=1, source_target_pairs={{0,16},{16,0},{1,17},{17,1},{2,18},{18,2},{3,19},{19,3},{4,20},{20... | collective-permute-start | bytes 2064392 | tf_op jit(solution)/shard_map/ppermute | solution.py:379
  80.7 6.8 %collective-permute-start.16 = (bf16[2,336,512]{2,1,0:T(8,128)(2,1)}, bf16[2,336,512]{2,1,0:T(8,128)(2,1)S(1)}, u32[]{:S(2)}, u32[]{:S(2)}) collective-permute-start(bf16[2,336,512]{2,1,0:T(8,128)(2,1)} %collective-permute-done.3.refs_1_), channel_id=1, source_target_pairs={{0,16},{16,0},{1,17},{17,1},{2,18},{18,2},{3,19},{19,3},{4,20},{20... | collective-permute-start | bytes 2064392 | tf_op jit(solution)/shard_map/ppermute | solution.py:379
  84.0 3.8 %collective-permute-start.22 = (bf16[2,336,512]{2,1,0:T(8,128)(2,1)}, bf16[2,336,512]{2,1,0:T(8,128)(2,1)S(1)}, u32[]{:S(2)}, u32[]{:S(2)}) collective-permute-start(bf16[2,336,512]{2,1,0:T(8,128)(2,1)} %collective-permute-done.5.refs_7_), channel_id=1, source_target_pairs={{0,16},{16,0},{1,17},{17,1},{2,18},{18,2},{3,19},{19,3},{4,20},{20... | collective-permute-start | bytes 2064392 | tf_op jit(solution)/shard_map/ppermute | solution.py:379
  84.0 4.1 %collective-permute-start.17 = (bf16[2,336,512]{2,1,0:T(8,128)(2,1)}, bf16[2,336,512]{2,1,0:T(8,128)(2,1)S(1)}, u32[]{:S(2)}, u32[]{:S(2)}) collective-permute-start(bf16[2,336,512]{2,1,0:T(8,128)(2,1)} %collective-permute-done.4.refs_2_), channel_id=1, source_target_pairs={{0,16},{16,0},{1,17},{17,1},{2,18},{18,2},{3,19},{19,3},{4,20},{20... | collective-permute-start | bytes 2064392 | tf_op jit(solution)/shard_map/ppermute | solution.py:379
  85.8 13.3 %collective-permute-start.21 = (bf16[2,336,512]{2,1,0:T(8,128)(2,1)}, bf16[2,336,512]{2,1,0:T(8,128)(2,1)S(1)}, u32[]{:S(2)}, u32[]{:S(2)}) collective-permute-start(bf16[2,336,512]{2,1,0:T(8,128)(2,1)} %collective-permute-done.6.refs_6_), channel_id=1, source_target_pairs={{0,16},{16,0},{1,17},{17,1},{2,18},{18,2},{3,19},{19,3},{4,20},{20... | collective-permute-start | bytes 2064392 | tf_op jit(solution)/shard_map/ppermute | solution.py:379
  87.5 9.7 %collective-permute-start.14 = (bf16[1,336,512]{2,1,0:T(8,128)(2,1)S(1)}, bf16[1,336,512]{2,1,0:T(8,128)(2,1)S(1)}, u32[]{:S(2)}, u32[]{:S(2)}) collective-permute-start(bf16[1,336,512]{2,1,0:T(8,128)(2,1)S(1)} %slice.12), channel_id=1, source_target_pairs={{0,4},{4,8},{8,12},{12,14},{14,10},{10,6},{6,2},{2,0},{1,5},{5,9},... | collective-permute-start | bytes 1032200 | tf_op jit(solution)/shard_map/ppermute | solution.py:347
  87.5 11.8 %collective-permute-start.18 = (bf16[2,336,512]{2,1,0:T(8,128)(2,1)S(1)}, bf16[2,336,512]{2,1,0:T(8,128)(2,1)S(1)}, u32[]{:S(2)}, u32[]{:S(2)}) collective-permute-start(bf16[2,336,512]{2,1,0:T(8,128)(2,1)S(1)} %collective-permute-done.10.refs_3_), channel_id=1, source_target_pairs={{0,16},{16,0},{1,17},{17,1},{2,18},{18,2},{3,19},{19,3},{4,20},{20... | collective-permute-start | bytes 2064392 | tf_op jit(solution)/shard_map/ppermute | solution.py:379
  87.8 11.5 %collective-permute-start.20 = (bf16[2,336,512]{2,1,0:T(8,128)(2,1)S(1)}, bf16[2,336,512]{2,1,0:T(8,128)(2,1)S(1)}, u32[]{:S(2)}, u32[]{:S(2)}) collective-permute-start(bf16[2,336,512]{2,1,0:T(8,128)(2,1)S(1)} %collective-permute-done.11.refs_5_), channel_id=1, source_target_pairs={{0,16},{16,0},{1,17},{17,1},{2,18},{18,2},{3,19},{19,3},{4,20},{20... | collective-permute-start | bytes 2064392 | tf_op jit(solution)/shard_map/ppermute | solution.py:379
  88.2 11.1 %collective-permute-start.24 = (bf16[1,336,512]{2,1,0:T(8,128)(2,1)S(1)}, bf16[1,336,512]{2,1,0:T(8,128)(2,1)S(1)}, u32[]{:S(2)}, u32[]{:S(2)}) collective-permute-start(bf16[1,336,512]{2,1,0:T(8,128)(2,1)S(1)} %slice.13), channel_id=1, source_target_pairs={{4,0},{8,4},{12,8},{14,12},{10,14},{6,10},{2,6},{0,2},{5,1},{9,5},... | collective-permute-start | bytes 1032200 | tf_op jit(solution)/shard_map/ppermute | solution.py:348
  99.1 13.6 %collective-permute-start.23 = (bf16[4,256,256]{2,1,0:T(8,128)(2,1)S(1)}, bf16[4,256,256]{2,1,0:T(8,128)(2,1)S(1)}, u32[]{:S(2)}, u32[]{:S(2)}) collective-permute-start(bf16[4,256,256]{2,1,0:T(8,128)(2,1)S(1)} %broadcast_select_fusion.8), channel_id=1, source_target_pairs={{0,2},{2,0},{4,6},{6,4},{8,10},{10,8},{12,14},{14,12},{1,3},{3,1},... | collective-permute-start | bytes 1572872 | tf_op jit(solution)/shard_map/ppermute | solution.py:437
  99.2 13.5 %collective-permute-start.25 = (bf16[1,336,512]{2,1,0:T(8,128)(2,1)S(1)}, bf16[1,336,512]{2,1,0:T(8,128)(2,1)S(1)}, u32[]{:S(2)}, u32[]{:S(2)}) collective-permute-start(bf16[1,336,512]{2,1,0:T(8,128)(2,1)S(1)} %collective-permute-done.24.refs_4_), channel_id=1, source_target_pairs={{0,16},{16,0},{1,17},{17,1},{2,18},{18,2},{3,19},{19,3},{4,20},{20... | collective-permute-start | bytes 1032200 | tf_op jit(solution)/shard_map/ppermute | solution.py:379
  118.8 16.2 %collective-permute-start.28 = (bf16[1344,256]{1,0:T(8,128)(2,1)S(1)}, bf16[1344,256]{1,0:T(8,128)(2,1)S(1)}, u32[]{:S(2)}, u32[]{:S(2)}) collective-permute-start(bf16[1344,256]{1,0:T(8,128)(2,1)S(1)} %get-tuple-element.66), channel_id=1, source_target_pairs={{0,1},{1,0},{2,3},{3,2},{4,5},{5,4},{6,7},{7,6},{8,9},{9,8},{10,11... | collective-permute-start | bytes 2064392 | tf_op jit(solution)/shard_map/ppermute | solution.py:382
  120.1 15.8 %collective-permute-start.26 = (bf16[2,336,512]{2,1,0:T(8,128)(2,1)S(1)}, bf16[2,336,512]{2,1,0:T(8,128)(2,1)S(1)}, u32[]{:S(2)}, u32[]{:S(2)}) collective-permute-start(bf16[2,336,512]{2,1,0:T(8,128)(2,1)S(1)} %copy-done.5), channel_id=1, source_target_pairs={{0,4},{4,8},{8,12},{12,14},{14,10},{10,6},{6,2},{2,0},{1,5},{5,9},... | collective-permute-start | bytes 2064392 | tf_op jit(solution)/shard_map/ppermute | solution.py:343
  120.1 15.9 %collective-permute-start.27 = (bf16[2,336,512]{2,1,0:T(8,128)(2,1)S(1)}, bf16[2,336,512]{2,1,0:T(8,128)(2,1)S(1)}, u32[]{:S(2)}, u32[]{:S(2)}) collective-permute-start(bf16[2,336,512]{2,1,0:T(8,128)(2,1)S(1)} %copy-done.5), channel_id=1, source_target_pairs={{4,0},{8,4},{12,8},{14,12},{10,14},{6,10},{2,6},{0,2},{5,1},{9,5},... | collective-permute-start | bytes 2064392 | tf_op jit(solution)/shard_map/ppermute | solution.py:344
  136.2 15.0 %collective-permute-start.31 = (bf16[1344,256]{1,0:T(8,128)(2,1)S(1)}, bf16[1344,256]{1,0:T(8,128)(2,1)S(1)}, u32[]{:S(2)}, u32[]{:S(2)}) collective-permute-start(bf16[1344,256]{1,0:T(8,128)(2,1)S(1)} %add_convert_fusion.1.own.state), channel_id=1, source_target_pairs={{0,1},{1,0},{2,3},{3,2},{4,5},{5,4},{6,7},{7,6},{8,9},{9,8},{10,11... | collective-permute-start | bytes 2064392 | tf_op jit(solution)/shard_map/ppermute | solution.py:382
  136.8 15.2 %collective-permute-start.29 = (bf16[2,336,512]{2,1,0:T(8,128)(2,1)S(1)}, bf16[2,336,512]{2,1,0:T(8,128)(2,1)}, u32[]{:S(2)}, u32[]{:S(2)}) collective-permute-start(bf16[2,336,512]{2,1,0:T(8,128)(2,1)S(1)} %collective-permute-done.26.refs_1_), channel_id=1, source_target_pairs={{0,4},{4,8},{8,12},{12,14},{14,10},{10,6},{6,2},{2,0},{1,5},{5,9},... | collective-permute-start | bytes 2064392 | tf_op jit(solution)/shard_map/ppermute | solution.py:343
  137.8 14.2 %collective-permute-start.30 = (bf16[2,336,512]{2,1,0:T(8,128)(2,1)S(1)}, bf16[2,336,512]{2,1,0:T(8,128)(2,1)}, u32[]{:S(2)}, u32[]{:S(2)}) collective-permute-start(bf16[2,336,512]{2,1,0:T(8,128)(2,1)S(1)} %collective-permute-done.27.refs_7_), channel_id=1, source_target_pairs={{4,0},{8,4},{12,8},{14,12},{10,14},{6,10},{2,6},{0,2},{5,1},{9,5},... | collective-permute-start | bytes 2064392 | tf_op jit(solution)/shard_map/ppermute | solution.py:344
  152.0 30.8 %collective-permute-start.32 = (bf16[2,336,512]{2,1,0:T(8,128)(2,1)}, bf16[2,336,512]{2,1,0:T(8,128)(2,1)}, u32[]{:S(2)}, u32[]{:S(2)}) collective-permute-start(bf16[2,336,512]{2,1,0:T(8,128)(2,1)} %collective-permute-done.29.refs_2_), channel_id=1, source_target_pairs={{0,4},{4,8},{8,12},{12,14},{14,10},{10,6},{6,2},{2,0},{1,5},{5,9},... | collective-permute-start | bytes 2064392 | tf_op jit(solution)/shard_map/ppermute | solution.py:343
  153.2 29.6 %collective-permute-start.33 = (bf16[2,336,512]{2,1,0:T(8,128)(2,1)}, bf16[2,336,512]{2,1,0:T(8,128)(2,1)}, u32[]{:S(2)}, u32[]{:S(2)}) collective-permute-start(bf16[2,336,512]{2,1,0:T(8,128)(2,1)} %collective-permute-done.30.refs_6_), channel_id=1, source_target_pairs={{4,0},{8,4},{12,8},{14,12},{10,14},{6,10},{2,6},{0,2},{5,1},{9,5},... | collective-permute-start | bytes 2064392 | tf_op jit(solution)/shard_map/ppermute | solution.py:344
  160.0 18.0 %collective-permute-start.34 = (bf16[4,256,256]{2,1,0:T(8,128)(2,1)S(1)}, bf16[4,256,256]{2,1,0:T(8,128)(2,1)S(1)}, u32[]{:S(2)}, u32[]{:S(2)}) collective-permute-start(bf16[4,256,256]{2,1,0:T(8,128)(2,1)S(1)} %key_value.3.refs_0_), channel_id=1, source_target_pairs={{0,4},{2,6},{4,8},{6,10},{8,12},{10,14},{12,0},{14,2},{1,5},{3,7},... | collective-permute-start | bytes 1572872 | tf_op jit(solution)/shard_map/ppermute | solution.py:434
  161.2 24.2 %collective-permute-start.39 = (bf16[2,336,512]{2,1,0:T(8,128)(2,1)S(1)}, bf16[2,336,512]{2,1,0:T(8,128)(2,1)S(1)}, u32[]{:S(2)}, u32[]{:S(2)}) collective-permute-start(bf16[2,336,512]{2,1,0:T(8,128)(2,1)S(1)} %copy-done.6), channel_id=1, source_target_pairs={{0,16},{16,0},{1,17},{17,1},{2,18},{18,2},{3,19},{19,3},{4,20},{20... | collective-permute-start | bytes 2064392 | tf_op jit(solution)/shard_map/ppermute | solution.py:379
  165.3 21.5 %collective-permute-start.40 = (bf16[2,336,512]{2,1,0:T(8,128)(2,1)S(1)}, bf16[2,336,512]{2,1,0:T(8,128)(2,1)S(1)}, u32[]{:S(2)}, u32[]{:S(2)}) collective-permute-start(bf16[2,336,512]{2,1,0:T(8,128)(2,1)S(1)} %copy-done.12), channel_id=1, source_target_pairs={{0,16},{16,0},{1,17},{17,1},{2,18},{18,2},{3,19},{19,3},{4,20},{20... | collective-permute-start | bytes 2064392 | tf_op jit(solution)/shard_map/ppermute | solution.py:379
  178.1 31.0 %collective-permute-start.46 = (bf16[2,336,512]{2,1,0:T(8,128)(2,1)S(1)}, bf16[2,336,512]{2,1,0:T(8,128)(2,1)S(1)}, u32[]{:S(2)}, u32[]{:S(2)}) collective-permute-start(bf16[2,336,512]{2,1,0:T(8,128)(2,1)S(1)} %copy-done.14), channel_id=1, source_target_pairs={{0,16},{16,0},{1,17},{17,1},{2,18},{18,2},{3,19},{19,3},{4,20},{20... | collective-permute-start | bytes 2064392 | tf_op jit(solution)/shard_map/ppermute | solution.py:379
  183.8 9.7 %collective-permute-start.35 = (bf16[1,336,512]{2,1,0:T(8,128)(2,1)S(1)}, bf16[1,336,512]{2,1,0:T(8,128)(2,1)S(1)}, u32[]{:S(2)}, u32[]{:S(2)}) collective-permute-start(bf16[1,336,512]{2,1,0:T(8,128)(2,1)S(1)} %slice.14), channel_id=1, source_target_pairs={{0,4},{4,8},{8,12},{12,14},{14,10},{10,6},{6,2},{2,0},{1,5},{5,9},... | collective-permute-start | bytes 1032200 | tf_op jit(solution)/shard_map/ppermute | solution.py:347
  184.0 24.6 %collective-permute-start.38 = (bf16[4,256,256]{2,1,0:T(8,128)(2,1)S(1)}, bf16[4,256,256]{2,1,0:T(8,128)(2,1)S(1)}, u32[]{:S(2)}, u32[]{:S(2)}) collective-permute-start(bf16[4,256,256]{2,1,0:T(8,128)(2,1)S(1)} %broadcast_select_fusion.7), channel_id=1, source_target_pairs={{0,2},{2,0},{4,6},{6,4},{8,10},{10,8},{12,14},{14,12},{1,3},{3,1},... | collective-permute-start | bytes 1572872 | tf_op jit(solution)/shard_map/ppermute | solution.py:437
  185.5 23.1 %collective-permute-start.37 = (bf16[4,256,256]{2,1,0:T(8,128)(2,1)S(1)}, bf16[4,256,256]{2,1,0:T(8,128)(2,1)S(1)}, u32[]{:S(2)}, u32[]{:S(2)}) collective-permute-start(bf16[4,256,256]{2,1,0:T(8,128)(2,1)S(1)} %collective-permute-done.34.refs_1_), channel_id=1, source_target_pairs={{0,4},{2,6},{4,8},{6,10},{8,12},{10,14},{12,0},{14,2},{1,5},{3,7},... | collective-permute-start | bytes 1572872 | tf_op jit(solution)/shard_map/ppermute | solution.py:434
  186.8 20.7 %collective-permute-start.36 = (bf16[1,336,512]{2,1,0:T(8,128)(2,1)S(1)}, bf16[1,336,512]{2,1,0:T(8,128)(2,1)S(1)}, u32[]{:S(2)}, u32[]{:S(2)}) collective-permute-start(bf16[1,336,512]{2,1,0:T(8,128)(2,1)S(1)} %slice.15), channel_id=1, source_target_pairs={{4,0},{8,4},{12,8},{14,12},{10,14},{6,10},{2,6},{0,2},{5,1},{9,5},... | collective-permute-start | bytes 1032200 | tf_op jit(solution)/shard_map/ppermute | solution.py:348
  193.6 15.6 %collective-permute-start.41 = (bf16[2,336,512]{2,1,0:T(8,128)(2,1)}, bf16[2,336,512]{2,1,0:T(8,128)(2,1)S(1)}, u32[]{:S(2)}, u32[]{:S(2)}) collective-permute-start(bf16[2,336,512]{2,1,0:T(8,128)(2,1)} %collective-permute-done.29.refs_2_), channel_id=1, source_target_pairs={{0,16},{16,0},{1,17},{17,1},{2,18},{18,2},{3,19},{19,3},{4,20},{20... | collective-permute-start | bytes 2064392 | tf_op jit(solution)/shard_map/ppermute | solution.py:379
  208.6 3.5 %collective-permute-start.42 = (bf16[2,336,512]{2,1,0:T(8,128)(2,1)}, bf16[2,336,512]{2,1,0:T(8,128)(2,1)S(1)}, u32[]{:S(2)}, u32[]{:S(2)}) collective-permute-start(bf16[2,336,512]{2,1,0:T(8,128)(2,1)} %collective-permute-done.32.refs_3_), channel_id=1, source_target_pairs={{0,16},{16,0},{1,17},{17,1},{2,18},{18,2},{3,19},{19,3},{4,20},{20... | collective-permute-start | bytes 2064392 | tf_op jit(solution)/shard_map/ppermute | solution.py:379
  208.6 5.8 %collective-permute-start.44 = (bf16[2,336,512]{2,1,0:T(8,128)(2,1)}, bf16[2,336,512]{2,1,0:T(8,128)(2,1)S(1)}, u32[]{:S(2)}, u32[]{:S(2)}) collective-permute-start(bf16[2,336,512]{2,1,0:T(8,128)(2,1)} %collective-permute-done.33.refs_5_), channel_id=1, source_target_pairs={{0,16},{16,0},{1,17},{17,1},{2,18},{18,2},{3,19},{19,3},{4,20},{20... | collective-permute-start | bytes 2064392 | tf_op jit(solution)/shard_map/ppermute | solution.py:379
  209.1 5.3 %collective-permute-start.43 = (bf16[1,336,512]{2,1,0:T(8,128)(2,1)S(1)}, bf16[1,336,512]{2,1,0:T(8,128)(2,1)S(1)}, u32[]{:S(2)}, u32[]{:S(2)}) collective-permute-start(bf16[1,336,512]{2,1,0:T(8,128)(2,1)S(1)} %collective-permute-done.35.refs_4_), channel_id=1, source_target_pairs={{0,16},{16,0},{1,17},{17,1},{2,18},{18,2},{3,19},{19,3},{4,20},{20... | collective-permute-start | bytes 1032200 | tf_op jit(solution)/shard_map/ppermute | solution.py:379
  209.2 15.6 %collective-permute-start.47 = (bf16[4,256,256]{2,1,0:T(8,128)(2,1)S(1)}, bf16[4,256,256]{2,1,0:T(8,128)(2,1)S(1)}, u32[]{:S(2)}, u32[]{:S(2)}) collective-permute-start(bf16[4,256,256]{2,1,0:T(8,128)(2,1)S(1)} %broadcast_select_fusion.6), channel_id=1, source_target_pairs={{0,2},{2,0},{4,6},{6,4},{8,10},{10,8},{12,14},{14,12},{1,3},{3,1},... | collective-permute-start | bytes 1572872 | tf_op jit(solution)/shard_map/ppermute | solution.py:437
  210.5 14.2 %collective-permute-start.48 = (bf16[1,336,512]{2,1,0:T(8,128)(2,1)S(1)}, bf16[1,336,512]{2,1,0:T(8,128)(2,1)S(1)}, u32[]{:S(2)}, u32[]{:S(2)}) collective-permute-start(bf16[1,336,512]{2,1,0:T(8,128)(2,1)S(1)} %collective-permute-done.36.refs_4_), channel_id=1, source_target_pairs={{0,16},{16,0},{1,17},{17,1},{2,18},{18,2},{3,19},{19,3},{4,20},{20... | collective-permute-start | bytes 1032200 | tf_op jit(solution)/shard_map/ppermute | solution.py:379
  212.0 19.6 %collective-permute-start.51 = (bf16[1344,256]{1,0:T(8,128)(2,1)S(1)}, bf16[1344,256]{1,0:T(8,128)(2,1)S(1)}, u32[]{:S(2)}, u32[]{:S(2)}) collective-permute-start(bf16[1344,256]{1,0:T(8,128)(2,1)S(1)} %add_convert_fusion.1.own.state), channel_id=1, source_target_pairs={{16,0},{17,1},{18,2},{19,3},{20,4},{21,5},{22,6},{23,7},{24,8},{25... | collective-permute-start | bytes 2064392 | tf_op jit(solution)/shard_map/ppermute | solution.py:484
  230.6 17.5 %collective-permute-start.49 = (bf16[1344,256]{1,0:T(8,128)(2,1)S(1)}, bf16[1344,256]{1,0:T(8,128)(2,1)S(1)}, u32[]{:S(2)}, u32[]{:S(2)}) collective-permute-start(bf16[1344,256]{1,0:T(8,128)(2,1)S(1)} %get-tuple-element.86), channel_id=1, source_target_pairs={{0,1},{1,0},{2,3},{3,2},{4,5},{5,4},{6,7},{7,6},{8,9},{9,8},{10,11... | collective-permute-start | bytes 2064392 | tf_op jit(solution)/shard_map/ppermute | solution.py:382
  248.4 4.0 %collective-permute-start.50 = (bf16[1344,256]{1,0:T(8,128)(2,1)S(1)}, bf16[1344,256]{1,0:T(8,128)(2,1)S(1)}, u32[]{:S(2)}, u32[]{:S(2)}) collective-permute-start(bf16[1344,256]{1,0:T(8,128)(2,1)S(1)} %get-tuple-element.90), channel_id=1, source_target_pairs={{0,16},{1,17},{2,18},{3,19},{4,20},{5,21},{6,22},{7,23},{8,24},{9,... | collective-permute-start | bytes 2064392 | tf_op jit(solution)/shard_map/ppermute | solution.py:485
  (25 other events, 207.9 us)

commit v3 on v2

--- a/solution.py
+++ b/solution.py
@@ -451,7 +451,10 @@
                 odds.append(swapped(evens[-3], evens[-2]))
                 evens[-1], odds[-1] = ring.close(evens[-1], odds[-1])
             else:
-                (evens[-1],) = ring.close(evens[-1])
+                if layer:
+                    evens[-1], first_came = ring.close(evens[-1], first_came)
+                else:
+                    (evens[-1],) = ring.close(evens[-1])
             ring.step()
         odds.append(swapped(evens[-2], evens[-1]))
         query_own, query_came, out_own, out_came = both_cores(ring.pieces())
@@ -469,24 +472,33 @@
         leave, stay = out_project(
             lengths, boundary, queries, late, reach - 1, reach, partial, state, out_own, out_came
         )
-        arrived = across_tp(leave)
         if layer + 1 < LAYERS:
+            arrived = across_tp(leave)
             arrived, *key_value_weights[layer + 1] = ring.close(
                 arrived, *key_value_weights[layer + 1]
             )
             ring.step()
-        state = (stay + arrived.astype(jnp.float32)).astype(jnp.bfloat16)
-        states.append(state)
-        if layer + 1 < LAYERS:
+            state = (stay + arrived.astype(jnp.float32)).astype(jnp.bfloat16)
+            states.append(state)
+            first_came = lax.ppermute(state, "segment", [(1, 0)])
             state_other = across_tp(state)
             (state_other,) = ring.close(state_other)
 
-    first_came = lax.ppermute(states[0], "segment", [(1, 0)])
-    last_came = lax.ppermute(states[1], "segment", [(0, 1)])
+    pairs = [[(2 * source + half, 3 - half) for half in range(2)] for source in range(2)]
+    arrived = [lax.ppermute(leave, ("segment", "tp"), pair) for pair in pairs]
+    stay_came = lax.ppermute(stay, "segment", [(0, 1)])
     both = jnp.stack(
         [
-            jnp.where(first_core, states[0], last_came),
-            jnp.where(first_core, first_came, states[1]),
+            jnp.where(
+                first_core,
+                states[0],
+                (stay_came + arrived[0].astype(jnp.float32)).astype(jnp.bfloat16),
+            ),
+            jnp.where(
+                first_core,
+                first_came,
+                (stay + arrived[1].astype(jnp.float32)).astype(jnp.bfloat16),
+            ),
         ]
     )
     return jnp.swapaxes(both, 1, 2)[None]

time: 255 us -> 248 us (0.973)
  waiting for transfers between devices: 140 us -> 131 us
  starting transfers between devices: 48.1 us -> 55.4 us
  Pallas kernels: 41.1 us -> 38.1 us
    ppermute x4 -> x3, waiting for transfers between devices: 42.8 us -> 20.9 us  [across_tp(): return lax.ppermute(value, 'tp', SWAP)]
    ppermute x2 -> x4, waiting for transfers between devices: 2.74 us -> 14.7 us  [the longest x2 14.7 us: per_device(): arrived = [lax.ppermute(leave, ('segment', 'tp'), pair) for pair in pairs]]
    ppermute x2 -> x4, starting transfers between devices: 3.6 us -> 10.8 us  [the longest x1 5.42 us: per_device(): first_came = lax.ppermute(state, 'segment', [(1, 0)])]
    unnamed x42 -> x36, local copies, waits for them, and re-layouts: 5.92 us -> 6.25 us
  transfers between devices with their start and end apart: 52 -> 53, of which waited for: 20 -> 21; matrix products, arithmetic and copies ran while one was open for 6% -> 6% of each run, Pallas kernels for 14% -> 11%
where the time goes in v3:
time: 248 us
  waiting for transfers between devices  131 us (53%)
  starting transfers between devices  55.4 us (22%)
  Pallas kernels  38.1 us (15%)
  other arithmetic  16.5 us (7%)
  local copies, waits for them, and re-layouts  6.56 us (3%)
    ppermute x4, waiting for transfers between devices, shifted(): return lax.ppermute(value, 'seq', up)  25.1 us
    ppermute x22, starting transfers between devices, across_chip(): return lax.ppermute(value, 'segment', SWAP)  23.4 us
    ppermute x4, waiting for transfers between devices, swapped(): return lax.ppermute(jnp.where(even, near, far), 'seq', beside)  22.5 us
    ppermute x3, waiting for transfers between devices, across_tp(): return lax.ppermute(value, 'tp', SWAP)  20.9 us
    ppermute x2, waiting for transfers between devices, step(): lax.ppermute(self.forward[-1][:1], 'seq', self.onward)  14.8 us
    ppermute x2, waiting for transfers between devices, per_device(): arrived = [lax.ppermute(leave, ('segment', 'tp'), pair) for pair in pairs]  14.7 us
    ppermute x6, waiting for transfers between devices, step(): self.forward.append(lax.ppermute(self.forward[-1], 'seq', self.onward))  11.5 us
    ppermute x2, waiting for transfers between devices, step(): lax.ppermute(self.backward[-1][1:], 'seq', self.back)  11.3 us
  transfers between devices with their start and end apart: 53, of which 21 were waited for; matrix products, arithmetic and copies ran while one was open for 6% of the time, Pallas kernels for 11%

profile of v3, /device:TPU:1, one launch (start us, length us, event | category | flops | bytes accessed | tf_op | source)
XLA Modules:
  0.0 247.6 jit_solution(3864931198850977288)
XLA Ops:
  0.0 1.3 fusion.5
  1.4 2.1 collective-permute-done.1
  4.3 1.7 broadcast_select_fusion.4
  6.0 2.5 %collective-permute-start.3 = (bf16[2,336,512]{2,1,0:T(8,128)(2,1)S(1)}, bf16[2,336,512]{2,1,0:T(8,128)(2,1)}, u32[]{:S(2)}, u32[]{:S(2)}) collective-permute-start(bf16[2,336,512]{2,1,0:T(8,128)(2,1)S(1)} %get-tuple-element.96.refs_0_), channel_id=1, source_target_pairs={{0,4},{4,8},{8,12},{12,14},{14,10},{10,6},{6,2},{2,0},{1,5},{5,9},... | collective-permute-start | bytes 2064392 | tf_op jit(solution)/shard_map/ppermute | solution.py:343
  10.0 2.5 %collective-permute-done.2 = f32[1,2688]{1,0:T(1,128)S(1)} collective-permute-done((f32[1,2688]{1,0:T(1,128)S(1)}, f32[1,2688]{1,0:T(1,128)S(1)}, u32[]{:S(2)}, u32[]{:S(2)}) %collective-permute-start.2) | collective-permute-done | bytes 10784 | tf_op jit(solution)/shard_map/ppermute | solution.py:379
  12.5 2.3 collective-permute-start
  15.0 9.1 %collective-permute-done.3.refs_1_ = bf16[2,336,512]{2,1,0:T(8,128)(2,1)} collective-permute-done((bf16[2,336,512]{2,1,0:T(8,128)(2,1)S(1)}, bf16[2,336,512]{2,1,0:T(8,128)(2,1)}, u32[]{:S(2)}, u32[]{:S(2)}) %collective-permute-start.3) | collective-permute-done | bytes 688160 | tf_op jit(solution)/shard_map/ppermute | solution.py:343
  25.6 4.6 %broadcast_select_fusion = (bf16[2688,512]{1,0:T(8,128)(2,1)}, bf16[2688,512]{1,0:T(8,128)(2,1)S(1)}) fusion(bf16[2688,512]{1,0:T(8,128)(2,1)} %collective-permute-done.8, bf16[2688,512]{1,0:T(8,128)(2,1)} %bitcast.24, pred[]{:T(512)S(6)} %eq.8), kind=kLoop, calls=%fused_computation | loop fusion | flops 2752512 | bytes 11010049 | tf_op jit(solution)/shard_map/jit(_where)/select_n | solution.py:406
  30.2 4.0 %broadcast_select_fusion.1 = (bf16[2688,512]{1,0:T(8,128)(2,1)}, bf16[2688,512]{1,0:T(8,128)(2,1)S(1)}) fusion(bf16[2688,512]{1,0:T(8,128)(2,1)} %collective-permute-done.7, bf16[2688,512]{1,0:T(8,128)(2,1)S(1)} %bitcast.26, pred[]{:T(512)S(6)} %eq.8), kind=kLoop, calls=%fused_computation.1 | loop fusion | flops 2752512 | bytes 11010049 | tf_op jit(solution)/shard_map/jit(_where)/select_n | solution.py:406
  34.2 3.5 %key_value.2.refs_0_ = bf16[4,256,256]{2,1,0:T(8,128)(2,1)} custom-call(bf16[1344,256]{1,0:T(8,128)(2,1)S(1)} %dynamic-slice_bitcast_fusion.own.state, bf16[1344,256]{1,0:T(8,128)(2,1)S(1)} %collective-permute-done.other, f32[2,1344]{1,0:T(2,128)S(1)} %reshape.16.gain, f32[2,256,128]{2,1,0:T(8,128)S(1)} %pad_maximum_fusion.tables, ...), custom_call_target="tpu_custom_call" | custom-call | flops 1409286144 | bytes 8257536 | tf_op jit(solution)/shard_map/key_value/pallas_call | solution.py:118
  39.0 1.5 collective-permute-done.4.refs_2_
  41.1 13.3 %collective-permute-done.9.refs_1_ = bf16[4,256,256]{2,1,0:T(8,128)(2,1)} collective-permute-done((bf16[4,256,256]{2,1,0:T(8,128)(2,1)}, bf16[4,256,256]{2,1,0:T(8,128)(2,1)}, u32[]{:S(2)}, u32[]{:S(2)}) %collective-permute-start.9) | collective-permute-done | bytes 524320 | tf_op jit(solution)/shard_map/ppermute | solution.py:434
  55.5 1.5 collective-permute-start.13
  57.8 2.4 collective-permute-start.15
  60.2 20.1 %collective-permute-done.13.refs_3_ = bf16[4,256,256]{2,1,0:T(8,128)(2,1)S(1)} collective-permute-done((bf16[4,256,256]{2,1,0:T(8,128)(2,1)S(1)}, bf16[4,256,256]{2,1,0:T(8,128)(2,1)S(1)}, u32[]{:S(2)}, u32[]{:S(2)}) %collective-permute-start.13) | collective-permute-done | bytes 524320 | tf_op jit(solution)/shard_map/ppermute | solution.py:437
  80.3 3.3 %collective-permute-start.16 = (bf16[2,336,512]{2,1,0:T(8,128)(2,1)}, bf16[2,336,512]{2,1,0:T(8,128)(2,1)S(1)}, u32[]{:S(2)}, u32[]{:S(2)}) collective-permute-start(bf16[2,336,512]{2,1,0:T(8,128)(2,1)} %collective-permute-done.3.refs_1_), channel_id=1, source_target_pairs={{0,16},{16,0},{1,17},{17,1},{2,18},{18,2},{3,19},{19,3},{4,20},{20... | collective-permute-start | bytes 2064392 | tf_op jit(solution)/shard_map/ppermute | solution.py:379
  84.1 1.3 collective-permute-done.11.refs_5_
  85.4 1.6 collective-permute-start.21
  87.8 1.6 collective-permute-start.24
  89.4 7.4 %collective-permute-done.14.refs_4_ = bf16[1,336,512]{2,1,0:T(8,128)(2,1)S(1)} collective-permute-done((bf16[1,336,512]{2,1,0:T(8,128)(2,1)S(1)}, bf16[1,336,512]{2,1,0:T(8,128)(2,1)S(1)}, u32[]{:S(2)}, u32[]{:S(2)}) %collective-permute-start.14) | collective-permute-done | bytes 344096 | tf_op jit(solution)/shard_map/ppermute | solution.py:347
  99.0 5.4 %query.2.queries = bf16[2,512,256]{2,1,0:T(8,128)(2,1)S(1)} custom-call(bf16[1344,256]{1,0:T(8,128)(2,1)S(1)} %dynamic-slice_bitcast_fusion.own.state, bf16[1344,256]{1,0:T(8,128)(2,1)S(1)} %copy-done.5, f32[2,1344]{1,0:T(2,128)S(1)} %reshape.16.gain, f32[2,256,128]{2,1,0:T(8,128)S(1)} %pad_maximum_fusion.tables, ...), custom_call_target="tpu_custom_call" | custom-call | flops 1409286144 | bytes 6881280 | tf_op jit(solution)/shard_map/query/pallas_call | solution.py:165
  104.4 5.5 %attend.2 = (f32[2,512,256]{2,1,0:T(8,128)S(1)}, f32[8,256]{1,0:T(8,128)S(1)}, f32[8,256]{1,0:T(8,128)S(1)}) custom-call(s32[2,8]{1,0:T(2,128)S(1)} %copy-done.12, s32[2]{0:T(128)S(1)} %copy-done.13, bf16[2,512,256]{2,1,0:T(8,128)(2,1)S(1)} %query.2.queries, bf16[4,256,256]{2,1,0:T(8,128)(2,1)} %key_value.2.refs_0_, ...), custom_call_target="tpu_custom_call" | custom-call | flops 1073741824 | bytes 3670016 | tf_op jit(solution)/shard_map/attend/pallas_call | solution.py:247
  110.0 2.4 collective-permute-done.23.window
  112.4 5.8 %out_project.2 = (bf16[1344,256]{1,0:T(8,128)(2,1)S(1)}, f32[1344,256]{1,0:T(8,128)S(1)}) custom-call(s32[2,8]{1,0:T(2,128)S(1)} %copy-done.12, s32[2]{0:T(128)S(1)} %copy-done.13, bf16[2,512,256]{2,1,0:T(8,128)(2,1)S(1)} %query.2.queries, bf16[4,256,256]{2,1,0:T(8,128)(2,1)S(1)} %collective-permute-done.23.window, ...), custom_call_target="tpu_custom_call" | custom-call | flops 1677721600 | bytes 8257536 | tf_op jit(solution)/shard_map/out_project/pallas_call | solution.py:310
  118.2 1.3 collective-permute-start.28
  119.5 1.5 collective-permute-start.27
  120.9 13.5 %collective-permute-done.28 = bf16[1344,256]{1,0:T(8,128)(2,1)S(1)} collective-permute-done((bf16[1344,256]{1,0:T(8,128)(2,1)S(1)}, bf16[1344,256]{1,0:T(8,128)(2,1)S(1)}, u32[]{:S(2)}, u32[]{:S(2)}) %collective-permute-start.28) | collective-permute-done | bytes 688160 | tf_op jit(solution)/shard_map/ppermute | solution.py:382
  137.6 5.4 %collective-permute-start.35 = (bf16[1344,256]{1,0:T(8,128)(2,1)S(1)}, bf16[1344,256]{1,0:T(8,128)(2,1)}, u32[]{:S(2)}, u32[]{:S(2)}) collective-permute-start(bf16[1344,256]{1,0:T(8,128)(2,1)S(1)} %add_convert_fusion.2.own.state), channel_id=1, source_target_pairs={{16,0},{17,1},{18,2},{19,3},{20,4},{21,5},{22,6},{23,7},{24,8},{25... | collective-permute-start | bytes 2064392 | tf_op jit(solution)/shard_map/ppermute | solution.py:483
  143.1 7.5 %collective-permute-done.31.other = bf16[1344,256]{1,0:T(8,128)(2,1)S(1)} collective-permute-done((bf16[1344,256]{1,0:T(8,128)(2,1)S(1)}, bf16[1344,256]{1,0:T(8,128)(2,1)S(1)}, u32[]{:S(2)}, u32[]{:S(2)}) %collective-permute-start.31) | collective-permute-done | bytes 688160 | tf_op jit(solution)/shard_map/ppermute | solution.py:382
  152.9 1.8 copy-done.2
  154.7 1.8 copy-done.3
  157.6 2.6 %key_value.3.refs_0_ = bf16[4,256,256]{2,1,0:T(8,128)(2,1)S(1)} custom-call(bf16[1344,256]{1,0:T(8,128)(2,1)S(1)} %add_convert_fusion.2.own.state, bf16[1344,256]{1,0:T(8,128)(2,1)S(1)} %copy-done.7, f32[2,1344]{1,0:T(2,128)S(1)} %reshape.17.gain, f32[2,256,128]{2,1,0:T(8,128)S(1)} %pad_maximum_fusion.tables, bf16[2688,512]{1,0:T(8,128)(2,1)S(1)} %copy-done.3, ...), custom_call_target="tpu_custom_call" | custom-call | flops 1409286144 | bytes 8257536 | tf_op jit(solution)/shard_map/key_value/pallas_call | solution.py:118
  161.4 4.0 %collective-permute-start.40 = (bf16[2,336,512]{2,1,0:T(8,128)(2,1)S(1)}, bf16[2,336,512]{2,1,0:T(8,128)(2,1)S(1)}, u32[]{:S(2)}, u32[]{:S(2)}) collective-permute-start(bf16[2,336,512]{2,1,0:T(8,128)(2,1)S(1)} %get-tuple-element.66.refs_0_), channel_id=1, source_target_pairs={{0,16},{16,0},{1,17},{17,1},{2,18},{18,2},{3,19},{19,3},{4,20},{20... | collective-permute-start | bytes 2064392 | tf_op jit(solution)/shard_map/ppermute | solution.py:379
  165.5 11.8 %collective-permute-done.34.refs_1_ = bf16[4,256,256]{2,1,0:T(8,128)(2,1)S(1)} collective-permute-done((bf16[4,256,256]{2,1,0:T(8,128)(2,1)S(1)}, bf16[4,256,256]{2,1,0:T(8,128)(2,1)S(1)}, u32[]{:S(2)}, u32[]{:S(2)}) %collective-permute-start.34) | collective-permute-done | bytes 524320 | tf_op jit(solution)/shard_map/ppermute | solution.py:434
  177.4 4.8 %collective-permute-start.47 = (bf16[2,336,512]{2,1,0:T(8,128)(2,1)S(1)}, bf16[2,336,512]{2,1,0:T(8,128)(2,1)S(1)}, u32[]{:S(2)}, u32[]{:S(2)}) collective-permute-start(bf16[2,336,512]{2,1,0:T(8,128)(2,1)S(1)} %copy-done.11), channel_id=1, source_target_pairs={{0,16},{16,0},{1,17},{17,1},{2,18},{18,2},{3,19},{19,3},{4,20},{20... | collective-permute-start | bytes 2064392 | tf_op jit(solution)/shard_map/ppermute | solution.py:379
  182.3 1.5 collective-permute-start.39
  184.5 7.4 %collective-permute-done.36.refs_4_ = bf16[1,336,512]{2,1,0:T(8,128)(2,1)S(1)} collective-permute-done((bf16[1,336,512]{2,1,0:T(8,128)(2,1)S(1)}, bf16[1,336,512]{2,1,0:T(8,128)(2,1)S(1)}, u32[]{:S(2)}, u32[]{:S(2)}) %collective-permute-start.36) | collective-permute-done | bytes 344096 | tf_op jit(solution)/shard_map/ppermute | solution.py:347
  193.1 11.3 %collective-permute-done.37.refs_4_ = bf16[1,336,512]{2,1,0:T(8,128)(2,1)S(1)} collective-permute-done((bf16[1,336,512]{2,1,0:T(8,128)(2,1)S(1)}, bf16[1,336,512]{2,1,0:T(8,128)(2,1)S(1)}, u32[]{:S(2)}, u32[]{:S(2)}) %collective-permute-start.37) | collective-permute-done | bytes 344096 | tf_op jit(solution)/shard_map/ppermute | solution.py:348
  204.5 1.7 collective-permute-start.46
  206.9 2.1 collective-permute-done.46.refs_14_
  210.4 5.0 %query.3.queries = bf16[2,512,256]{2,1,0:T(8,128)(2,1)S(1)} custom-call(bf16[1344,256]{1,0:T(8,128)(2,1)S(1)} %add_convert_fusion.2.own.state, bf16[1344,256]{1,0:T(8,128)(2,1)S(1)} %copy-done.7, f32[2,1344]{1,0:T(2,128)S(1)} %reshape.17.gain, f32[2,256,128]{2,1,0:T(8,128)S(1)} %pad_maximum_fusion.tables, ...), custom_call_target="tpu_custom_call" | custom-call | flops 1409286144 | bytes 6881280 | tf_op jit(solution)/shard_map/query/pallas_call | solution.py:165
  215.4 4.9 %attend.3 = (f32[2,512,256]{2,1,0:T(8,128)S(1)}, f32[8,256]{1,0:T(8,128)S(1)}, f32[8,256]{1,0:T(8,128)S(1)}) custom-call(s32[2,8]{1,0:T(2,128)S(1)} %copy-done.12, s32[2]{0:T(128)S(1)} %copy-done.13, bf16[2,512,256]{2,1,0:T(8,128)(2,1)S(1)} %query.3.queries, bf16[4,256,256]{2,1,0:T(8,128)(2,1)S(1)} %key_value.3.refs_0_, ...), custom_call_target="tpu_custom_call" | custom-call | flops 1073741824 | bytes 3670016 | tf_op jit(solution)/shard_map/attend/pallas_call | solution.py:247
  220.3 5.4 %out_project.3 = (bf16[1344,256]{1,0:T(8,128)(2,1)S(1)}, f32[1344,256]{1,0:T(8,128)S(1)}) custom-call(s32[2,8]{1,0:T(2,128)S(1)} %copy-done.12, s32[2]{0:T(128)S(1)} %copy-done.13, bf16[2,512,256]{2,1,0:T(8,128)(2,1)S(1)} %query.3.queries, bf16[4,256,256]{2,1,0:T(8,128)(2,1)S(1)} %collective-permute-done.48.window, ...), custom_call_target="tpu_custom_call" | custom-call | flops 1677721600 | bytes 8257536 | tf_op jit(solution)/shard_map/out_project/pallas_call | solution.py:310
  225.7 1.3 collective-permute-start.50
  227.0 2.8 %collective-permute-start.52 = (bf16[1344,256]{1,0:T(8,128)(2,1)S(1)}, bf16[1344,256]{1,0:T(8,128)(2,1)S(1)}, u32[]{:S(2)}, u32[]{:S(2)}) collective-permute-start(bf16[1344,256]{1,0:T(8,128)(2,1)S(1)} %get-tuple-element.87), channel_id=1, source_target_pairs={{16,17},{17,16},{18,19},{19,18},{20,21},{21,20},{22,23},{23,22},{2... | collective-permute-start | bytes 2064392 | tf_op jit(solution)/shard_map/ppermute | solution.py:488
  229.9 1.3 collective-permute-start.51
  231.2 11.4 %collective-permute-done.52 = bf16[1344,256]{1,0:T(8,128)(2,1)S(1)} collective-permute-done((bf16[1344,256]{1,0:T(8,128)(2,1)S(1)}, bf16[1344,256]{1,0:T(8,128)(2,1)S(1)}, u32[]{:S(2)}, u32[]{:S(2)}) %collective-permute-start.52) | collective-permute-done | bytes 688160 | tf_op jit(solution)/shard_map/ppermute | solution.py:488
  242.8 3.2 %collective-permute-done.51 = bf16[1344,256]{1,0:T(8,128)(2,1)S(1)} collective-permute-done((bf16[1344,256]{1,0:T(8,128)(2,1)S(1)}, bf16[1344,256]{1,0:T(8,128)(2,1)S(1)}, u32[]{:S(2)}, u32[]{:S(2)}) %collective-permute-start.51) | collective-permute-done | bytes 688160 | tf_op jit(solution)/shard_map/ppermute | solution.py:488
  (127 shorter events, 25.0 us)
Async XLA Ops:
  3.5 22.1 %collective-permute-start.8 = (bf16[2688,512]{1,0:T(8,128)(2,1)}, bf16[2688,512]{1,0:T(8,128)(2,1)}, u32[]{:S(2)}, u32[]{:S(2)}) collective-permute-start(bf16[2688,512]{1,0:T(8,128)(2,1)} %bitcast.23), channel_id=1, source_target_pairs={{0,16},{16,0},{1,17},{17,1},{2,18},{18,2},{3,19},{19,3},{4,20},{20... | collective-permute-start | bytes 8257544 | tf_op jit(solution)/shard_map/ppermute | solution.py:379
  3.6 26.5 %collective-permute-start.7 = (bf16[2688,512]{1,0:T(8,128)(2,1)}, bf16[2688,512]{1,0:T(8,128)(2,1)}, u32[]{:S(2)}, u32[]{:S(2)}) collective-permute-start(bf16[2688,512]{1,0:T(8,128)(2,1)} %bitcast.25), channel_id=1, source_target_pairs={{0,16},{16,0},{1,17},{17,1},{2,18},{18,2},{3,19},{19,3},{4,20},{20... | collective-permute-start | bytes 8257544 | tf_op jit(solution)/shard_map/ppermute | solution.py:379
  6.0 18.0 %collective-permute-start.3 = (bf16[2,336,512]{2,1,0:T(8,128)(2,1)S(1)}, bf16[2,336,512]{2,1,0:T(8,128)(2,1)}, u32[]{:S(2)}, u32[]{:S(2)}) collective-permute-start(bf16[2,336,512]{2,1,0:T(8,128)(2,1)S(1)} %get-tuple-element.96.refs_0_), channel_id=1, source_target_pairs={{0,4},{4,8},{8,12},{12,14},{14,10},{10,6},{6,2},{2,0},{1,5},{5,9},... | collective-permute-start | bytes 2064392 | tf_op jit(solution)/shard_map/ppermute | solution.py:343
  8.5 16.8 %collective-permute-start.5 = (bf16[2,336,512]{2,1,0:T(8,128)(2,1)S(1)}, bf16[2,336,512]{2,1,0:T(8,128)(2,1)}, u32[]{:S(2)}, u32[]{:S(2)}) collective-permute-start(bf16[2,336,512]{2,1,0:T(8,128)(2,1)S(1)} %get-tuple-element.96.refs_0_), channel_id=1, source_target_pairs={{4,0},{8,4},{12,8},{14,12},{10,14},{6,10},{2,6},{0,2},{5,1},{9,5},... | collective-permute-start | bytes 2064392 | tf_op jit(solution)/shard_map/ppermute | solution.py:344
  12.5 21.7 %collective-permute-start = (bf16[1344,256]{1,0:T(8,128)(2,1)S(1)}, bf16[1344,256]{1,0:T(8,128)(2,1)S(1)}, u32[]{:S(2)}, u32[]{:S(2)}) collective-permute-start(bf16[1344,256]{1,0:T(8,128)(2,1)S(1)} %dynamic-slice_bitcast_fusion.own.state), channel_id=1, source_target_pairs={{0,1},{1,0},{2,3},{3,2},{4,5},{5,4},{6,7},{7,6},{8,9},{9,8},{10,11... | collective-permute-start | bytes 2064392 | tf_op jit(solution)/shard_map/ppermute | solution.py:382
  24.1 16.4 %collective-permute-start.4 = (bf16[2,336,512]{2,1,0:T(8,128)(2,1)}, bf16[2,336,512]{2,1,0:T(8,128)(2,1)}, u32[]{:S(2)}, u32[]{:S(2)}) collective-permute-start(bf16[2,336,512]{2,1,0:T(8,128)(2,1)} %collective-permute-done.3.refs_1_), channel_id=1, source_target_pairs={{0,4},{4,8},{8,12},{12,14},{14,10},{10,6},{6,2},{2,0},{1,5},{5,9},... | collective-permute-start | bytes 2064392 | tf_op jit(solution)/shard_map/ppermute | solution.py:343
  25.3 15.8 %collective-permute-start.6 = (bf16[2,336,512]{2,1,0:T(8,128)(2,1)}, bf16[2,336,512]{2,1,0:T(8,128)(2,1)}, u32[]{:S(2)}, u32[]{:S(2)}) collective-permute-start(bf16[2,336,512]{2,1,0:T(8,128)(2,1)} %collective-permute-done.5.refs_7_), channel_id=1, source_target_pairs={{4,0},{8,4},{12,8},{14,12},{10,14},{6,10},{2,6},{0,2},{5,1},{9,5},... | collective-permute-start | bytes 2064392 | tf_op jit(solution)/shard_map/ppermute | solution.py:344
  37.7 16.6 %collective-permute-start.9 = (bf16[4,256,256]{2,1,0:T(8,128)(2,1)}, bf16[4,256,256]{2,1,0:T(8,128)(2,1)}, u32[]{:S(2)}, u32[]{:S(2)}) collective-permute-start(bf16[4,256,256]{2,1,0:T(8,128)(2,1)} %key_value.2.refs_0_), channel_id=1, source_target_pairs={{0,4},{2,6},{4,8},{6,10},{8,12},{10,14},{12,0},{14,2},{1,5},{3,7},... | collective-permute-start | bytes 1572872 | tf_op jit(solution)/shard_map/ppermute | solution.py:434
  54.3 29.3 %collective-permute-start.10 = (bf16[2,336,512]{2,1,0:T(8,128)(2,1)}, bf16[2,336,512]{2,1,0:T(8,128)(2,1)S(1)}, u32[]{:S(2)}, u32[]{:S(2)}) collective-permute-start(bf16[2,336,512]{2,1,0:T(8,128)(2,1)} %collective-permute-done.4.refs_2_), channel_id=1, source_target_pairs={{0,4},{4,8},{8,12},{12,14},{14,10},{10,6},{6,2},{2,0},{1,5},{5,9},... | collective-permute-start | bytes 2064392 | tf_op jit(solution)/shard_map/ppermute | solution.py:343
  55.5 24.9 %collective-permute-start.13 = (bf16[4,256,256]{2,1,0:T(8,128)(2,1)S(1)}, bf16[4,256,256]{2,1,0:T(8,128)(2,1)S(1)}, u32[]{:S(2)}, u32[]{:S(2)}) collective-permute-start(bf16[4,256,256]{2,1,0:T(8,128)(2,1)S(1)} %broadcast_select_fusion.9), channel_id=1, source_target_pairs={{0,2},{2,0},{4,6},{6,4},{8,10},{10,8},{12,14},{14,12},{1,3},{3,1},... | collective-permute-start | bytes 1572872 | tf_op jit(solution)/shard_map/ppermute | solution.py:437
  57.0 26.7 %collective-permute-start.12 = (bf16[4,256,256]{2,1,0:T(8,128)(2,1)}, bf16[4,256,256]{2,1,0:T(8,128)(2,1)S(1)}, u32[]{:S(2)}, u32[]{:S(2)}) collective-permute-start(bf16[4,256,256]{2,1,0:T(8,128)(2,1)} %collective-permute-done.9.refs_1_), channel_id=1, source_target_pairs={{0,4},{2,6},{4,8},{6,10},{8,12},{10,14},{12,0},{14,2},{1,5},{3,7},... | collective-permute-start | bytes 1572872 | tf_op jit(solution)/shard_map/ppermute | solution.py:434
  57.8 27.7 %collective-permute-start.11 = (bf16[2,336,512]{2,1,0:T(8,128)(2,1)}, bf16[2,336,512]{2,1,0:T(8,128)(2,1)S(1)}, u32[]{:S(2)}, u32[]{:S(2)}) collective-permute-start(bf16[2,336,512]{2,1,0:T(8,128)(2,1)} %collective-permute-done.6.refs_6_), channel_id=1, source_target_pairs={{4,0},{8,4},{12,8},{14,12},{10,14},{6,10},{2,6},{0,2},{5,1},{9,5},... | collective-permute-start | bytes 2064392 | tf_op jit(solution)/shard_map/ppermute | solution.py:344
  57.8 29.3 %collective-permute-start.15 = (bf16[2,336,512]{2,1,0:T(8,128)(2,1)S(1)}, bf16[2,336,512]{2,1,0:T(8,128)(2,1)S(1)}, u32[]{:S(2)}, u32[]{:S(2)}) collective-permute-start(bf16[2,336,512]{2,1,0:T(8,128)(2,1)S(1)} %get-tuple-element.96.refs_0_), channel_id=1, source_target_pairs={{0,16},{16,0},{1,17},{17,1},{2,18},{18,2},{3,19},{19,3},{4,20},{20... | collective-permute-start | bytes 2064392 | tf_op jit(solution)/shard_map/ppermute | solution.py:379
  80.3 6.8 %collective-permute-start.16 = (bf16[2,336,512]{2,1,0:T(8,128)(2,1)}, bf16[2,336,512]{2,1,0:T(8,128)(2,1)S(1)}, u32[]{:S(2)}, u32[]{:S(2)}) collective-permute-start(bf16[2,336,512]{2,1,0:T(8,128)(2,1)} %collective-permute-done.3.refs_1_), channel_id=1, source_target_pairs={{0,16},{16,0},{1,17},{17,1},{2,18},{18,2},{3,19},{19,3},{4,20},{20... | collective-permute-start | bytes 2064392 | tf_op jit(solution)/shard_map/ppermute | solution.py:379
  83.6 3.8 %collective-permute-start.22 = (bf16[2,336,512]{2,1,0:T(8,128)(2,1)}, bf16[2,336,512]{2,1,0:T(8,128)(2,1)S(1)}, u32[]{:S(2)}, u32[]{:S(2)}) collective-permute-start(bf16[2,336,512]{2,1,0:T(8,128)(2,1)} %collective-permute-done.5.refs_7_), channel_id=1, source_target_pairs={{0,16},{16,0},{1,17},{17,1},{2,18},{18,2},{3,19},{19,3},{4,20},{20... | collective-permute-start | bytes 2064392 | tf_op jit(solution)/shard_map/ppermute | solution.py:379
  83.6 4.1 %collective-permute-start.17 = (bf16[2,336,512]{2,1,0:T(8,128)(2,1)}, bf16[2,336,512]{2,1,0:T(8,128)(2,1)S(1)}, u32[]{:S(2)}, u32[]{:S(2)}) collective-permute-start(bf16[2,336,512]{2,1,0:T(8,128)(2,1)} %collective-permute-done.4.refs_2_), channel_id=1, source_target_pairs={{0,16},{16,0},{1,17},{17,1},{2,18},{18,2},{3,19},{19,3},{4,20},{20... | collective-permute-start | bytes 2064392 | tf_op jit(solution)/shard_map/ppermute | solution.py:379
  85.4 13.3 %collective-permute-start.21 = (bf16[2,336,512]{2,1,0:T(8,128)(2,1)}, bf16[2,336,512]{2,1,0:T(8,128)(2,1)S(1)}, u32[]{:S(2)}, u32[]{:S(2)}) collective-permute-start(bf16[2,336,512]{2,1,0:T(8,128)(2,1)} %collective-permute-done.6.refs_6_), channel_id=1, source_target_pairs={{0,16},{16,0},{1,17},{17,1},{2,18},{18,2},{3,19},{19,3},{4,20},{20... | collective-permute-start | bytes 2064392 | tf_op jit(solution)/shard_map/ppermute | solution.py:379
  87.1 9.7 %collective-permute-start.14 = (bf16[1,336,512]{2,1,0:T(8,128)(2,1)S(1)}, bf16[1,336,512]{2,1,0:T(8,128)(2,1)S(1)}, u32[]{:S(2)}, u32[]{:S(2)}) collective-permute-start(bf16[1,336,512]{2,1,0:T(8,128)(2,1)S(1)} %slice.12), channel_id=1, source_target_pairs={{0,4},{4,8},{8,12},{12,14},{14,10},{10,6},{6,2},{2,0},{1,5},{5,9},... | collective-permute-start | bytes 1032200 | tf_op jit(solution)/shard_map/ppermute | solution.py:347
  87.2 11.8 %collective-permute-start.18 = (bf16[2,336,512]{2,1,0:T(8,128)(2,1)S(1)}, bf16[2,336,512]{2,1,0:T(8,128)(2,1)S(1)}, u32[]{:S(2)}, u32[]{:S(2)}) collective-permute-start(bf16[2,336,512]{2,1,0:T(8,128)(2,1)S(1)} %collective-permute-done.10.refs_3_), channel_id=1, source_target_pairs={{0,16},{16,0},{1,17},{17,1},{2,18},{18,2},{3,19},{19,3},{4,20},{20... | collective-permute-start | bytes 2064392 | tf_op jit(solution)/shard_map/ppermute | solution.py:379
  87.4 11.5 %collective-permute-start.20 = (bf16[2,336,512]{2,1,0:T(8,128)(2,1)S(1)}, bf16[2,336,512]{2,1,0:T(8,128)(2,1)S(1)}, u32[]{:S(2)}, u32[]{:S(2)}) collective-permute-start(bf16[2,336,512]{2,1,0:T(8,128)(2,1)S(1)} %collective-permute-done.11.refs_5_), channel_id=1, source_target_pairs={{0,16},{16,0},{1,17},{17,1},{2,18},{18,2},{3,19},{19,3},{4,20},{20... | collective-permute-start | bytes 2064392 | tf_op jit(solution)/shard_map/ppermute | solution.py:379
  87.8 11.1 %collective-permute-start.24 = (bf16[1,336,512]{2,1,0:T(8,128)(2,1)S(1)}, bf16[1,336,512]{2,1,0:T(8,128)(2,1)S(1)}, u32[]{:S(2)}, u32[]{:S(2)}) collective-permute-start(bf16[1,336,512]{2,1,0:T(8,128)(2,1)S(1)} %slice.13), channel_id=1, source_target_pairs={{4,0},{8,4},{12,8},{14,12},{10,14},{6,10},{2,6},{0,2},{5,1},{9,5},... | collective-permute-start | bytes 1032200 | tf_op jit(solution)/shard_map/ppermute | solution.py:348
  98.8 13.6 %collective-permute-start.23 = (bf16[4,256,256]{2,1,0:T(8,128)(2,1)S(1)}, bf16[4,256,256]{2,1,0:T(8,128)(2,1)S(1)}, u32[]{:S(2)}, u32[]{:S(2)}) collective-permute-start(bf16[4,256,256]{2,1,0:T(8,128)(2,1)S(1)} %broadcast_select_fusion.8), channel_id=1, source_target_pairs={{0,2},{2,0},{4,6},{6,4},{8,10},{10,8},{12,14},{14,12},{1,3},{3,1},... | collective-permute-start | bytes 1572872 | tf_op jit(solution)/shard_map/ppermute | solution.py:437
  98.9 13.5 %collective-permute-start.25 = (bf16[1,336,512]{2,1,0:T(8,128)(2,1)S(1)}, bf16[1,336,512]{2,1,0:T(8,128)(2,1)S(1)}, u32[]{:S(2)}, u32[]{:S(2)}) collective-permute-start(bf16[1,336,512]{2,1,0:T(8,128)(2,1)S(1)} %collective-permute-done.24.refs_4_), channel_id=1, source_target_pairs={{0,16},{16,0},{1,17},{17,1},{2,18},{18,2},{3,19},{19,3},{4,20},{20... | collective-permute-start | bytes 1032200 | tf_op jit(solution)/shard_map/ppermute | solution.py:379
  118.2 16.2 %collective-permute-start.28 = (bf16[1344,256]{1,0:T(8,128)(2,1)S(1)}, bf16[1344,256]{1,0:T(8,128)(2,1)S(1)}, u32[]{:S(2)}, u32[]{:S(2)}) collective-permute-start(bf16[1344,256]{1,0:T(8,128)(2,1)S(1)} %get-tuple-element.67), channel_id=1, source_target_pairs={{0,1},{1,0},{2,3},{3,2},{4,5},{5,4},{6,7},{7,6},{8,9},{9,8},{10,11... | collective-permute-start | bytes 2064392 | tf_op jit(solution)/shard_map/ppermute | solution.py:382
  119.5 15.9 %collective-permute-start.26 = (bf16[2,336,512]{2,1,0:T(8,128)(2,1)S(1)}, bf16[2,336,512]{2,1,0:T(8,128)(2,1)S(1)}, u32[]{:S(2)}, u32[]{:S(2)}) collective-permute-start(bf16[2,336,512]{2,1,0:T(8,128)(2,1)S(1)} %get-tuple-element.66.refs_0_), channel_id=1, source_target_pairs={{0,4},{4,8},{8,12},{12,14},{14,10},{10,6},{6,2},{2,0},{1,5},{5,9},... | collective-permute-start | bytes 2064392 | tf_op jit(solution)/shard_map/ppermute | solution.py:343
  119.5 15.9 %collective-permute-start.27 = (bf16[2,336,512]{2,1,0:T(8,128)(2,1)S(1)}, bf16[2,336,512]{2,1,0:T(8,128)(2,1)S(1)}, u32[]{:S(2)}, u32[]{:S(2)}) collective-permute-start(bf16[2,336,512]{2,1,0:T(8,128)(2,1)S(1)} %get-tuple-element.66.refs_0_), channel_id=1, source_target_pairs={{4,0},{8,4},{12,8},{14,12},{10,14},{6,10},{2,6},{0,2},{5,1},{9,5},... | collective-permute-start | bytes 2064392 | tf_op jit(solution)/shard_map/ppermute | solution.py:344
  135.5 15.0 %collective-permute-start.31 = (bf16[1344,256]{1,0:T(8,128)(2,1)S(1)}, bf16[1344,256]{1,0:T(8,128)(2,1)S(1)}, u32[]{:S(2)}, u32[]{:S(2)}) collective-permute-start(bf16[1344,256]{1,0:T(8,128)(2,1)S(1)} %add_convert_fusion.2.own.state), channel_id=1, source_target_pairs={{0,1},{1,0},{2,3},{3,2},{4,5},{5,4},{6,7},{7,6},{8,9},{9,8},{10,11... | collective-permute-start | bytes 2064392 | tf_op jit(solution)/shard_map/ppermute | solution.py:382
  136.2 15.2 %collective-permute-start.29 = (bf16[2,336,512]{2,1,0:T(8,128)(2,1)S(1)}, bf16[2,336,512]{2,1,0:T(8,128)(2,1)}, u32[]{:S(2)}, u32[]{:S(2)}) collective-permute-start(bf16[2,336,512]{2,1,0:T(8,128)(2,1)S(1)} %collective-permute-done.26.refs_1_), channel_id=1, source_target_pairs={{0,4},{4,8},{8,12},{12,14},{14,10},{10,6},{6,2},{2,0},{1,5},{5,9},... | collective-permute-start | bytes 2064392 | tf_op jit(solution)/shard_map/ppermute | solution.py:343
  137.2 14.2 %collective-permute-start.30 = (bf16[2,336,512]{2,1,0:T(8,128)(2,1)S(1)}, bf16[2,336,512]{2,1,0:T(8,128)(2,1)}, u32[]{:S(2)}, u32[]{:S(2)}) collective-permute-start(bf16[2,336,512]{2,1,0:T(8,128)(2,1)S(1)} %collective-permute-done.27.refs_7_), channel_id=1, source_target_pairs={{4,0},{8,4},{12,8},{14,12},{10,14},{6,10},{2,6},{0,2},{5,1},{9,5},... | collective-permute-start | bytes 2064392 | tf_op jit(solution)/shard_map/ppermute | solution.py:344
  137.6 27.8 %collective-permute-start.35 = (bf16[1344,256]{1,0:T(8,128)(2,1)S(1)}, bf16[1344,256]{1,0:T(8,128)(2,1)}, u32[]{:S(2)}, u32[]{:S(2)}) collective-permute-start(bf16[1344,256]{1,0:T(8,128)(2,1)S(1)} %add_convert_fusion.2.own.state), channel_id=1, source_target_pairs={{16,0},{17,1},{18,2},{19,3},{20,4},{21,5},{22,6},{23,7},{24,8},{25... | collective-permute-start | bytes 2064392 | tf_op jit(solution)/shard_map/ppermute | solution.py:483
  151.4 30.8 %collective-permute-start.32 = (bf16[2,336,512]{2,1,0:T(8,128)(2,1)}, bf16[2,336,512]{2,1,0:T(8,128)(2,1)S(1)}, u32[]{:S(2)}, u32[]{:S(2)}) collective-permute-start(bf16[2,336,512]{2,1,0:T(8,128)(2,1)} %collective-permute-done.29.refs_2_), channel_id=1, source_target_pairs={{0,4},{4,8},{8,12},{12,14},{14,10},{10,6},{6,2},{2,0},{1,5},{5,9},... | collective-permute-start | bytes 2064392 | tf_op jit(solution)/shard_map/ppermute | solution.py:343
  152.5 29.6 %collective-permute-start.33 = (bf16[2,336,512]{2,1,0:T(8,128)(2,1)}, bf16[2,336,512]{2,1,0:T(8,128)(2,1)S(1)}, u32[]{:S(2)}, u32[]{:S(2)}) collective-permute-start(bf16[2,336,512]{2,1,0:T(8,128)(2,1)} %collective-permute-done.30.refs_6_), channel_id=1, source_target_pairs={{4,0},{8,4},{12,8},{14,12},{10,14},{6,10},{2,6},{0,2},{5,1},{9,5},... | collective-permute-start | bytes 2064392 | tf_op jit(solution)/shard_map/ppermute | solution.py:344
  160.2 17.2 %collective-permute-start.34 = (bf16[4,256,256]{2,1,0:T(8,128)(2,1)S(1)}, bf16[4,256,256]{2,1,0:T(8,128)(2,1)S(1)}, u32[]{:S(2)}, u32[]{:S(2)}) collective-permute-start(bf16[4,256,256]{2,1,0:T(8,128)(2,1)S(1)} %key_value.3.refs_0_), channel_id=1, source_target_pairs={{0,4},{2,6},{4,8},{6,10},{8,12},{10,14},{12,0},{14,2},{1,5},{3,7},... | collective-permute-start | bytes 1572872 | tf_op jit(solution)/shard_map/ppermute | solution.py:434
  161.4 22.4 %collective-permute-start.40 = (bf16[2,336,512]{2,1,0:T(8,128)(2,1)S(1)}, bf16[2,336,512]{2,1,0:T(8,128)(2,1)S(1)}, u32[]{:S(2)}, u32[]{:S(2)}) collective-permute-start(bf16[2,336,512]{2,1,0:T(8,128)(2,1)S(1)} %get-tuple-element.66.refs_0_), channel_id=1, source_target_pairs={{0,16},{16,0},{1,17},{17,1},{2,18},{18,2},{3,19},{19,3},{4,20},{20... | collective-permute-start | bytes 2064392 | tf_op jit(solution)/shard_map/ppermute | solution.py:379
  165.5 18.7 %collective-permute-start.41 = (bf16[2,336,512]{2,1,0:T(8,128)(2,1)S(1)}, bf16[2,336,512]{2,1,0:T(8,128)(2,1)S(1)}, u32[]{:S(2)}, u32[]{:S(2)}) collective-permute-start(bf16[2,336,512]{2,1,0:T(8,128)(2,1)S(1)} %copy-done.9), channel_id=1, source_target_pairs={{0,16},{16,0},{1,17},{17,1},{2,18},{18,2},{3,19},{19,3},{4,20},{20... | collective-permute-start | bytes 2064392 | tf_op jit(solution)/shard_map/ppermute | solution.py:379
  177.4 29.3 %collective-permute-start.47 = (bf16[2,336,512]{2,1,0:T(8,128)(2,1)S(1)}, bf16[2,336,512]{2,1,0:T(8,128)(2,1)S(1)}, u32[]{:S(2)}, u32[]{:S(2)}) collective-permute-start(bf16[2,336,512]{2,1,0:T(8,128)(2,1)S(1)} %copy-done.11), channel_id=1, source_target_pairs={{0,16},{16,0},{1,17},{17,1},{2,18},{18,2},{3,19},{19,3},{4,20},{20... | collective-permute-start | bytes 2064392 | tf_op jit(solution)/shard_map/ppermute | solution.py:379
  182.2 9.7 %collective-permute-start.36 = (bf16[1,336,512]{2,1,0:T(8,128)(2,1)S(1)}, bf16[1,336,512]{2,1,0:T(8,128)(2,1)S(1)}, u32[]{:S(2)}, u32[]{:S(2)}) collective-permute-start(bf16[1,336,512]{2,1,0:T(8,128)(2,1)S(1)} %slice.14), channel_id=1, source_target_pairs={{0,4},{4,8},{8,12},{12,14},{14,10},{10,6},{6,2},{2,0},{1,5},{5,9},... | collective-permute-start | bytes 1032200 | tf_op jit(solution)/shard_map/ppermute | solution.py:347
  182.3 23.9 %collective-permute-start.39 = (bf16[4,256,256]{2,1,0:T(8,128)(2,1)S(1)}, bf16[4,256,256]{2,1,0:T(8,128)(2,1)S(1)}, u32[]{:S(2)}, u32[]{:S(2)}) collective-permute-start(bf16[4,256,256]{2,1,0:T(8,128)(2,1)S(1)} %broadcast_select_fusion.7), channel_id=1, source_target_pairs={{0,2},{2,0},{4,6},{6,4},{8,10},{10,8},{12,14},{14,12},{1,3},{3,1},... | collective-permute-start | bytes 1572872 | tf_op jit(solution)/shard_map/ppermute | solution.py:437
  183.8 22.3 %collective-permute-start.38 = (bf16[4,256,256]{2,1,0:T(8,128)(2,1)S(1)}, bf16[4,256,256]{2,1,0:T(8,128)(2,1)S(1)}, u32[]{:S(2)}, u32[]{:S(2)}) collective-permute-start(bf16[4,256,256]{2,1,0:T(8,128)(2,1)S(1)} %collective-permute-done.34.refs_1_), channel_id=1, source_target_pairs={{0,4},{2,6},{4,8},{6,10},{8,12},{10,14},{12,0},{14,2},{1,5},{3,7},... | collective-permute-start | bytes 1572872 | tf_op jit(solution)/shard_map/ppermute | solution.py:434
  184.2 20.3 %collective-permute-start.37 = (bf16[1,336,512]{2,1,0:T(8,128)(2,1)S(1)}, bf16[1,336,512]{2,1,0:T(8,128)(2,1)S(1)}, u32[]{:S(2)}, u32[]{:S(2)}) collective-permute-start(bf16[1,336,512]{2,1,0:T(8,128)(2,1)S(1)} %slice.15), channel_id=1, source_target_pairs={{4,0},{8,4},{12,8},{14,12},{10,14},{6,10},{2,6},{0,2},{5,1},{9,5},... | collective-permute-start | bytes 1032200 | tf_op jit(solution)/shard_map/ppermute | solution.py:348
  191.9 14.9 %collective-permute-start.42 = (bf16[2,336,512]{2,1,0:T(8,128)(2,1)}, bf16[2,336,512]{2,1,0:T(8,128)(2,1)S(1)}, u32[]{:S(2)}, u32[]{:S(2)}) collective-permute-start(bf16[2,336,512]{2,1,0:T(8,128)(2,1)} %collective-permute-done.29.refs_2_), channel_id=1, source_target_pairs={{0,16},{16,0},{1,17},{17,1},{2,18},{18,2},{3,19},{19,3},{4,20},{20... | collective-permute-start | bytes 2064392 | tf_op jit(solution)/shard_map/ppermute | solution.py:379
  204.5 4.6 %collective-permute-start.46 = (bf16[2,336,512]{2,1,0:T(8,128)(2,1)}, bf16[2,336,512]{2,1,0:T(8,128)(2,1)S(1)}, u32[]{:S(2)}, u32[]{:S(2)}) collective-permute-start(bf16[2,336,512]{2,1,0:T(8,128)(2,1)} %collective-permute-done.30.refs_6_), channel_id=1, source_target_pairs={{0,16},{16,0},{1,17},{17,1},{2,18},{18,2},{3,19},{19,3},{4,20},{20... | collective-permute-start | bytes 2064392 | tf_op jit(solution)/shard_map/ppermute | solution.py:379
  206.2 3.7 %collective-permute-start.45 = (bf16[2,336,512]{2,1,0:T(8,128)(2,1)S(1)}, bf16[2,336,512]{2,1,0:T(8,128)(2,1)S(1)}, u32[]{:S(2)}, u32[]{:S(2)}) collective-permute-start(bf16[2,336,512]{2,1,0:T(8,128)(2,1)S(1)} %collective-permute-done.33.refs_5_), channel_id=1, source_target_pairs={{0,16},{16,0},{1,17},{17,1},{2,18},{18,2},{3,19},{19,3},{4,20},{20... | collective-permute-start | bytes 2064392 | tf_op jit(solution)/shard_map/ppermute | solution.py:379
  206.8 13.5 %collective-permute-start.48 = (bf16[4,256,256]{2,1,0:T(8,128)(2,1)S(1)}, bf16[4,256,256]{2,1,0:T(8,128)(2,1)S(1)}, u32[]{:S(2)}, u32[]{:S(2)}) collective-permute-start(bf16[4,256,256]{2,1,0:T(8,128)(2,1)S(1)} %broadcast_select_fusion.6), channel_id=1, source_target_pairs={{0,2},{2,0},{4,6},{6,4},{8,10},{10,8},{12,14},{14,12},{1,3},{3,1},... | collective-permute-start | bytes 1572872 | tf_op jit(solution)/shard_map/ppermute | solution.py:437
  209.1 11.2 %collective-permute-start.49 = (bf16[1,336,512]{2,1,0:T(8,128)(2,1)S(1)}, bf16[1,336,512]{2,1,0:T(8,128)(2,1)S(1)}, u32[]{:S(2)}, u32[]{:S(2)}) collective-permute-start(bf16[1,336,512]{2,1,0:T(8,128)(2,1)S(1)} %collective-permute-done.37.refs_4_), channel_id=1, source_target_pairs={{0,16},{16,0},{1,17},{17,1},{2,18},{18,2},{3,19},{19,3},{4,20},{20... | collective-permute-start | bytes 1032200 | tf_op jit(solution)/shard_map/ppermute | solution.py:379
  225.7 20.4 %collective-permute-start.50 = (f32[1344,256]{1,0:T(8,128)S(1)}, f32[1344,256]{1,0:T(8,128)S(1)}, u32[]{:S(2)}, u32[]{:S(2)}) collective-permute-start(f32[1344,256]{1,0:T(8,128)S(1)} %get-tuple-element.86), channel_id=1, source_target_pairs={{0,16},{1,17},{2,18},{3,19},{4,20},{5,21},{6,22},{7,23},{8,24},{9,... | collective-permute-start | bytes 4128776 | tf_op jit(solution)/shard_map/ppermute | solution.py:489
  227.0 15.6 %collective-permute-start.52 = (bf16[1344,256]{1,0:T(8,128)(2,1)S(1)}, bf16[1344,256]{1,0:T(8,128)(2,1)S(1)}, u32[]{:S(2)}, u32[]{:S(2)}) collective-permute-start(bf16[1344,256]{1,0:T(8,128)(2,1)S(1)} %get-tuple-element.87), channel_id=1, source_target_pairs={{16,17},{17,16},{18,19},{19,18},{20,21},{21,20},{22,23},{23,22},{2... | collective-permute-start | bytes 2064392 | tf_op jit(solution)/shard_map/ppermute | solution.py:488
  229.9 16.2 %collective-permute-start.51 = (bf16[1344,256]{1,0:T(8,128)(2,1)S(1)}, bf16[1344,256]{1,0:T(8,128)(2,1)S(1)}, u32[]{:S(2)}, u32[]{:S(2)}) collective-permute-start(bf16[1344,256]{1,0:T(8,128)(2,1)S(1)} %get-tuple-element.87), channel_id=1, source_target_pairs={{0,17},{1,16},{2,19},{3,18},{4,21},{5,20},{6,23},{7,22},{8,25},{9,... | collective-permute-start | bytes 2064392 | tf_op jit(solution)/shard_map/ppermute | solution.py:488
  (23 other events, 132.6 us)

commit v4 on v3

--- a/solution.py
+++ b/solution.py
@@ -18,6 +18,8 @@
 norm_epsilon = 1e-06
 hidden = -1e30
 VMEM_LIMIT = 16 * 1024 * 1024
+
+COST = 0
 
 SWAP = ((0, 1), (1, 0))
 
@@ -56,7 +58,9 @@
         out_specs=outs,
         scratch_shapes=scratch,
         compiler_params=pltpu.CompilerParams(vmem_limit_bytes=VMEM_LIMIT),
-        cost_estimate=pl.CostEstimate(flops=flops, bytes_accessed=moved, transcendentals=exps),
+        cost_estimate=pl.CostEstimate(
+            flops=COST * flops, bytes_accessed=COST * moved, transcendentals=COST * exps
+        ),
         name=name,
     )
 
@@ -450,12 +454,12 @@
             if len(evens) > 2:
                 odds.append(swapped(evens[-3], evens[-2]))
                 evens[-1], odds[-1] = ring.close(evens[-1], odds[-1])
+                ring.step()
+            elif layer:
+                evens[-1], first_came = ring.close(evens[-1], first_came)
             else:
-                if layer:
-                    evens[-1], first_came = ring.close(evens[-1], first_came)
-                else:
-                    (evens[-1],) = ring.close(evens[-1])
-            ring.step()
+                (evens[-1],) = ring.close(evens[-1])
+                ring.step()
         odds.append(swapped(evens[-2], evens[-1]))
         query_own, query_came, out_own, out_came = both_cores(ring.pieces())
         queries = query(state, state_other, gains[layer], tables, query_own, query_came)

time: 248 us -> 245 us (0.988)
  waiting for transfers between devices: 131 us -> 128 us
  local copies, waits for them, and re-layouts: 6.56 us -> 9.39 us
    ppermute x2, waiting for transfers between devices: 11.3 us -> 0.01 us  [step(): lax.ppermute(self.backward[-1][1:], 'seq', self.back)]
    ppermute x4, waiting for transfers between devices: 25.1 us -> 30.8 us  [shifted(): return lax.ppermute(value, 'seq', up)]
    ppermute x22, starting transfers between devices: 23.4 us -> 26.8 us  [across_chip(): return lax.ppermute(value, 'segment', SWAP)]
    ppermute x22, waiting for transfers between devices: 7.76 us -> 10.7 us  [across_chip(): return lax.ppermute(value, 'segment', SWAP)]
    unnamed x36 -> x40, local copies, waits for them, and re-layouts: 6.25 us -> 8.1 us
  transfers between devices with their start and end apart: 53 -> 53, of which waited for: 21 -> 22; matrix products, arithmetic and copies ran while one was open for 6% -> 5% of each run, Pallas kernels for 11% -> 11%
where the time goes in v4:
time: 245 us
  waiting for transfers between devices  128 us (52%)
  starting transfers between devices  55.2 us (23%)
  Pallas kernels  37.1 us (15%)
  other arithmetic  14.6 us (6%)
  local copies, waits for them, and re-layouts  9.39 us (4%)
    ppermute x4, waiting for transfers between devices, shifted(): return lax.ppermute(value, 'seq', up)  30.8 us
    ppermute x22, starting transfers between devices, across_chip(): return lax.ppermute(value, 'segment', SWAP)  26.8 us
    ppermute x4, waiting for transfers between devices, swapped(): return lax.ppermute(jnp.where(even, near, far), 'seq', beside)  24.7 us
    ppermute x3, waiting for transfers between devices, across_tp(): return lax.ppermute(value, 'tp', SWAP)  23.4 us
    ppermute x2, waiting for transfers between devices, per_device(): arrived = [lax.ppermute(leave, ('segment', 'tp'), pair) for pair in pairs]  14.9 us
    ppermute x2, waiting for transfers between devices, step(): lax.ppermute(self.forward[-1][:1], 'seq', self.onward)  12.7 us
    pallas_call x2, Pallas kernels, out_project(): call(functools.partial(out_kernel, count, distance, reach), (jax.ShapeDty...  11.4 us
    ppermute x22, waiting for transfers between devices, across_chip(): return lax.ppermute(value, 'segment', SWAP)  10.7 us
  transfers between devices with their start and end apart: 53, of which 22 were waited for; matrix products, arithmetic and copies ran while one was open for 5% of the time, Pallas kernels for 11%

profile of v4, /device:TPU:1, one launch (start us, length us, event | category | flops | bytes accessed | tf_op | source)
XLA Modules:
  0.0 244.8 jit_solution(13146091147231993253)
XLA Ops:
  0.0 1.3 fusion.5
  1.4 2.1 collective-permute-done.1
  4.3 1.7 broadcast_select_fusion.4
  6.0 2.5 %collective-permute-start.3 = (bf16[2,336,512]{2,1,0:T(8,128)(2,1)S(1)}, bf16[2,336,512]{2,1,0:T(8,128)(2,1)}, u32[]{:S(2)}, u32[]{:S(2)}) collective-permute-start(bf16[2,336,512]{2,1,0:T(8,128)(2,1)S(1)} %get-tuple-element.96.refs_0_), channel_id=1, source_target_pairs={{0,4},{4,8},{8,12},{12,14},{14,10},{10,6},{6,2},{2,0},{1,5},{5,9},... | collective-permute-start | bytes 2064392 | tf_op jit(solution)/shard_map/ppermute | solution.py:347
  10.0 2.5 %collective-permute-done.2 = f32[1,2688]{1,0:T(1,128)S(1)} collective-permute-done((f32[1,2688]{1,0:T(1,128)S(1)}, f32[1,2688]{1,0:T(1,128)S(1)}, u32[]{:S(2)}, u32[]{:S(2)}) %collective-permute-start.2) | collective-permute-done | bytes 10784 | tf_op jit(solution)/shard_map/ppermute | solution.py:383
  12.5 2.3 collective-permute-start
  15.0 9.1 %collective-permute-done.3.refs_1_ = bf16[2,336,512]{2,1,0:T(8,128)(2,1)} collective-permute-done((bf16[2,336,512]{2,1,0:T(8,128)(2,1)S(1)}, bf16[2,336,512]{2,1,0:T(8,128)(2,1)}, u32[]{:S(2)}, u32[]{:S(2)}) %collective-permute-start.3) | collective-permute-done | bytes 688160 | tf_op jit(solution)/shard_map/ppermute | solution.py:347
  25.6 4.6 %broadcast_select_fusion = (bf16[2688,512]{1,0:T(8,128)(2,1)}, bf16[2688,512]{1,0:T(8,128)(2,1)S(1)}) fusion(bf16[2688,512]{1,0:T(8,128)(2,1)} %collective-permute-done.8, bf16[2688,512]{1,0:T(8,128)(2,1)} %bitcast.24, pred[]{:T(512)S(6)} %eq.8), kind=kLoop, calls=%fused_computation | loop fusion | flops 2752512 | bytes 11010049 | tf_op jit(solution)/shard_map/jit(_where)/select_n | solution.py:410
  30.2 4.0 %broadcast_select_fusion.1 = (bf16[2688,512]{1,0:T(8,128)(2,1)}, bf16[2688,512]{1,0:T(8,128)(2,1)S(1)}) fusion(bf16[2688,512]{1,0:T(8,128)(2,1)} %collective-permute-done.7, bf16[2688,512]{1,0:T(8,128)(2,1)S(1)} %bitcast.26, pred[]{:T(512)S(6)} %eq.8), kind=kLoop, calls=%fused_computation.1 | loop fusion | flops 2752512 | bytes 11010049 | tf_op jit(solution)/shard_map/jit(_where)/select_n | solution.py:410
  36.2 2.7 %key_value.2.refs_0_ = bf16[4,256,256]{2,1,0:T(8,128)(2,1)S(1)} custom-call(bf16[1344,256]{1,0:T(8,128)(2,1)S(1)} %dynamic-slice_bitcast_fusion.own.state, bf16[1344,256]{1,0:T(8,128)(2,1)S(1)} %copy-done.5, f32[2,1344]{1,0:T(2,128)S(1)} %reshape.16.gain, f32[2,256,128]{2,1,0:T(8,128)S(1)} %pad_maximum_fusion.tables, ...), custom_call_target="tpu_custom_call" | custom-call | tf_op jit(solution)/shard_map/key_value/pallas_call | solution.py:122
  38.9 1.2 collective-permute-start.9
  41.1 13.7 %collective-permute-done.9.refs_1_ = bf16[4,256,256]{2,1,0:T(8,128)(2,1)S(1)} collective-permute-done((bf16[4,256,256]{2,1,0:T(8,128)(2,1)S(1)}, bf16[4,256,256]{2,1,0:T(8,128)(2,1)S(1)}, u32[]{:S(2)}, u32[]{:S(2)}) %collective-permute-start.9) | collective-permute-done | bytes 524320 | tf_op jit(solution)/shard_map/ppermute | solution.py:438
  54.8 1.5 collective-permute-start.13
  56.5 2.6 %collective-permute-start.15 = (bf16[2,336,512]{2,1,0:T(8,128)(2,1)S(1)}, bf16[2,336,512]{2,1,0:T(8,128)(2,1)S(1)}, u32[]{:S(2)}, u32[]{:S(2)}) collective-permute-start(bf16[2,336,512]{2,1,0:T(8,128)(2,1)S(1)} %get-tuple-element.96.refs_0_), channel_id=1, source_target_pairs={{0,16},{16,0},{1,17},{17,1},{2,18},{18,2},{3,19},{19,3},{4,20},{20... | collective-permute-start | bytes 2064392 | tf_op jit(solution)/shard_map/ppermute | solution.py:383
  59.1 22.2 %collective-permute-done.13.refs_3_ = bf16[4,256,256]{2,1,0:T(8,128)(2,1)S(1)} collective-permute-done((bf16[4,256,256]{2,1,0:T(8,128)(2,1)S(1)}, bf16[4,256,256]{2,1,0:T(8,128)(2,1)S(1)}, u32[]{:S(2)}, u32[]{:S(2)}) %collective-permute-start.13) | collective-permute-done | bytes 524320 | tf_op jit(solution)/shard_map/ppermute | solution.py:441
  81.2 2.8 %collective-permute-start.16 = (bf16[2,336,512]{2,1,0:T(8,128)(2,1)}, bf16[2,336,512]{2,1,0:T(8,128)(2,1)S(1)}, u32[]{:S(2)}, u32[]{:S(2)}) collective-permute-start(bf16[2,336,512]{2,1,0:T(8,128)(2,1)} %collective-permute-done.3.refs_1_), channel_id=1, source_target_pairs={{0,16},{16,0},{1,17},{17,1},{2,18},{18,2},{3,19},{19,3},{4,20},{20... | collective-permute-start | bytes 2064392 | tf_op jit(solution)/shard_map/ppermute | solution.py:383
  87.0 2.0 collective-permute-done.17.refs_10_
  89.0 1.9 collective-permute-done.21.refs_14_
  90.9 5.3 %collective-permute-done.14.refs_4_ = bf16[1,336,512]{2,1,0:T(8,128)(2,1)S(1)} collective-permute-done((bf16[1,336,512]{2,1,0:T(8,128)(2,1)S(1)}, bf16[1,336,512]{2,1,0:T(8,128)(2,1)S(1)}, u32[]{:S(2)}, u32[]{:S(2)}) %collective-permute-start.14) | collective-permute-done | bytes 344096 | tf_op jit(solution)/shard_map/ppermute | solution.py:351
  96.3 2.0 collective-permute-start.19
  99.6 5.4 %query.2.queries = bf16[2,512,256]{2,1,0:T(8,128)(2,1)S(1)} custom-call(bf16[1344,256]{1,0:T(8,128)(2,1)S(1)} %dynamic-slice_bitcast_fusion.own.state, bf16[1344,256]{1,0:T(8,128)(2,1)S(1)} %copy-done.6, f32[2,1344]{1,0:T(2,128)S(1)} %reshape.16.gain, f32[2,256,128]{2,1,0:T(8,128)S(1)} %pad_maximum_fusion.tables, ...), custom_call_target="tpu_custom_call" | custom-call | tf_op jit(solution)/shard_map/query/pallas_call | solution.py:169
  105.0 4.9 %attend.2 = (f32[2,512,256]{2,1,0:T(8,128)S(1)}, f32[8,256]{1,0:T(8,128)S(1)}, f32[8,256]{1,0:T(8,128)S(1)}) custom-call(s32[2,8]{1,0:T(2,128)S(1)} %copy-done.14, s32[2]{0:T(128)S(1)} %copy-done.15, bf16[2,512,256]{2,1,0:T(8,128)(2,1)S(1)} %query.2.queries, bf16[4,256,256]{2,1,0:T(8,128)(2,1)S(1)} %key_value.2.refs_0_, ...), custom_call_target="tpu_custom_call" | custom-call | tf_op jit(solution)/shard_map/attend/pallas_call | solution.py:251
  110.0 5.8 %out_project.2 = (bf16[1344,256]{1,0:T(8,128)(2,1)S(1)}, f32[1344,256]{1,0:T(8,128)S(1)}) custom-call(s32[2,8]{1,0:T(2,128)S(1)} %copy-done.14, s32[2]{0:T(128)S(1)} %copy-done.15, bf16[2,512,256]{2,1,0:T(8,128)(2,1)S(1)} %query.2.queries, bf16[4,256,256]{2,1,0:T(8,128)(2,1)S(1)} %collective-permute-done.23.window, ...), custom_call_target="tpu_custom_call" | custom-call | tf_op jit(solution)/shard_map/out_project/pallas_call | solution.py:314
  117.0 1.5 collective-permute-start.27
  118.5 14.0 %collective-permute-done.28 = bf16[1344,256]{1,0:T(8,128)(2,1)S(1)} collective-permute-done((bf16[1344,256]{1,0:T(8,128)(2,1)S(1)}, bf16[1344,256]{1,0:T(8,128)(2,1)S(1)}, u32[]{:S(2)}, u32[]{:S(2)}) %collective-permute-start.28) | collective-permute-done | bytes 688160 | tf_op jit(solution)/shard_map/ppermute | solution.py:386
  135.6 4.0 %collective-permute-start.35 = (bf16[1344,256]{1,0:T(8,128)(2,1)S(1)}, bf16[1344,256]{1,0:T(8,128)(2,1)S(1)}, u32[]{:S(2)}, u32[]{:S(2)}) collective-permute-start(bf16[1344,256]{1,0:T(8,128)(2,1)S(1)} %add_convert_fusion.2.own.state), channel_id=1, source_target_pairs={{16,0},{17,1},{18,2},{19,3},{20,4},{21,5},{22,6},{23,7},{24,8},{25... | collective-permute-start | bytes 2064392 | tf_op jit(solution)/shard_map/ppermute | solution.py:487
  139.7 9.4 %collective-permute-done.31.other = bf16[1344,256]{1,0:T(8,128)(2,1)S(1)} collective-permute-done((bf16[1344,256]{1,0:T(8,128)(2,1)S(1)}, bf16[1344,256]{1,0:T(8,128)(2,1)S(1)}, u32[]{:S(2)}, u32[]{:S(2)}) %collective-permute-start.31) | collective-permute-done | bytes 688160 | tf_op jit(solution)/shard_map/ppermute | solution.py:386
  150.1 1.2 collective-permute-start.33
  151.5 1.8 copy-done.2
  153.2 1.8 copy-done.3
  156.1 2.6 %key_value.3.refs_0_ = bf16[4,256,256]{2,1,0:T(8,128)(2,1)S(1)} custom-call(bf16[1344,256]{1,0:T(8,128)(2,1)S(1)} %add_convert_fusion.2.own.state, bf16[1344,256]{1,0:T(8,128)(2,1)S(1)} %copy-done.8, f32[2,1344]{1,0:T(2,128)S(1)} %reshape.17.gain, f32[2,256,128]{2,1,0:T(8,128)S(1)} %pad_maximum_fusion.tables, bf16[2688,512]{1,0:T(8,128)(2,1)S(1)} %copy-done.3, ...), custom_call_target="tpu_custom_call" | custom-call | tf_op jit(solution)/shard_map/key_value/pallas_call | solution.py:122
  159.1 17.1 %collective-permute-done.34.refs_1_ = bf16[4,256,256]{2,1,0:T(8,128)(2,1)S(1)} collective-permute-done((bf16[4,256,256]{2,1,0:T(8,128)(2,1)S(1)}, bf16[4,256,256]{2,1,0:T(8,128)(2,1)S(1)}, u32[]{:S(2)}, u32[]{:S(2)}) %collective-permute-start.34) | collective-permute-done | bytes 524320 | tf_op jit(solution)/shard_map/ppermute | solution.py:438
  177.8 5.1 %collective-permute-start.39 = (bf16[2,336,512]{2,1,0:T(8,128)(2,1)S(1)}, bf16[2,336,512]{2,1,0:T(8,128)(2,1)S(1)}, u32[]{:S(2)}, u32[]{:S(2)}) collective-permute-start(bf16[2,336,512]{2,1,0:T(8,128)(2,1)S(1)} %get-tuple-element.66.refs_0_), channel_id=1, source_target_pairs={{0,16},{16,0},{1,17},{17,1},{2,18},{18,2},{3,19},{19,3},{4,20},{20... | collective-permute-start | bytes 2064392 | tf_op jit(solution)/shard_map/ppermute | solution.py:383
  183.4 2.6 %collective-permute-done.37.refs_3_ = bf16[4,256,256]{2,1,0:T(8,128)(2,1)S(1)} collective-permute-done((bf16[4,256,256]{2,1,0:T(8,128)(2,1)S(1)}, bf16[4,256,256]{2,1,0:T(8,128)(2,1)S(1)}, u32[]{:S(2)}, u32[]{:S(2)}) %collective-permute-start.37) | collective-permute-done | bytes 524320 | tf_op jit(solution)/shard_map/ppermute | solution.py:441
  186.0 4.7 %collective-permute-start.41 = (bf16[2,336,512]{2,1,0:T(8,128)(2,1)}, bf16[2,336,512]{2,1,0:T(8,128)(2,1)S(1)}, u32[]{:S(2)}, u32[]{:S(2)}) collective-permute-start(bf16[2,336,512]{2,1,0:T(8,128)(2,1)} %collective-permute-done.29.refs_2_), channel_id=1, source_target_pairs={{0,16},{16,0},{1,17},{17,1},{2,18},{18,2},{3,19},{19,3},{4,20},{20... | collective-permute-start | bytes 2064392 | tf_op jit(solution)/shard_map/ppermute | solution.py:383
  190.7 2.6 %collective-permute-start.45 = (bf16[2,336,512]{2,1,0:T(8,128)(2,1)}, bf16[2,336,512]{2,1,0:T(8,128)(2,1)S(1)}, u32[]{:S(2)}, u32[]{:S(2)}) collective-permute-start(bf16[2,336,512]{2,1,0:T(8,128)(2,1)} %collective-permute-done.30.refs_6_), channel_id=1, source_target_pairs={{0,16},{16,0},{1,17},{17,1},{2,18},{18,2},{3,19},{19,3},{4,20},{20... | collective-permute-start | bytes 2064392 | tf_op jit(solution)/shard_map/ppermute | solution.py:383
  194.9 1.5 collective-permute-start.48
  197.2 7.4 %collective-permute-done.38.refs_4_ = bf16[1,336,512]{2,1,0:T(8,128)(2,1)S(1)} collective-permute-done((bf16[1,336,512]{2,1,0:T(8,128)(2,1)S(1)}, bf16[1,336,512]{2,1,0:T(8,128)(2,1)S(1)}, u32[]{:S(2)}, u32[]{:S(2)}) %collective-permute-start.38) | collective-permute-done | bytes 344096 | tf_op jit(solution)/shard_map/ppermute | solution.py:351
  204.6 1.3 collective-permute-start.43
  205.9 1.3 collective-permute-done.43.refs_12_
  207.2 5.2 %query.3.queries = bf16[2,512,256]{2,1,0:T(8,128)(2,1)S(1)} custom-call(bf16[1344,256]{1,0:T(8,128)(2,1)S(1)} %add_convert_fusion.2.own.state, bf16[1344,256]{1,0:T(8,128)(2,1)S(1)} %copy-done.9, f32[2,1344]{1,0:T(2,128)S(1)} %reshape.17.gain, f32[2,256,128]{2,1,0:T(8,128)S(1)} %pad_maximum_fusion.tables, ...), custom_call_target="tpu_custom_call" | custom-call | tf_op jit(solution)/shard_map/query/pallas_call | solution.py:169
  212.4 4.9 %attend.3 = (f32[2,512,256]{2,1,0:T(8,128)S(1)}, f32[8,256]{1,0:T(8,128)S(1)}, f32[8,256]{1,0:T(8,128)S(1)}) custom-call(s32[2,8]{1,0:T(2,128)S(1)} %copy-done.14, s32[2]{0:T(128)S(1)} %copy-done.15, bf16[2,512,256]{2,1,0:T(8,128)(2,1)S(1)} %query.3.queries, bf16[4,256,256]{2,1,0:T(8,128)(2,1)S(1)} %key_value.3.refs_0_, ...), custom_call_target="tpu_custom_call" | custom-call | tf_op jit(solution)/shard_map/attend/pallas_call | solution.py:251
  217.3 5.6 %out_project.3 = (bf16[1344,256]{1,0:T(8,128)(2,1)S(1)}, f32[1344,256]{1,0:T(8,128)S(1)}) custom-call(s32[2,8]{1,0:T(2,128)S(1)} %copy-done.14, s32[2]{0:T(128)S(1)} %copy-done.15, bf16[2,512,256]{2,1,0:T(8,128)(2,1)S(1)} %query.3.queries, bf16[4,256,256]{2,1,0:T(8,128)(2,1)S(1)} %collective-permute-done.47.window, ...), custom_call_target="tpu_custom_call" | custom-call | tf_op jit(solution)/shard_map/out_project/pallas_call | solution.py:314
  222.9 1.3 collective-permute-start.50
  224.2 2.5 %collective-permute-start.52 = (bf16[1344,256]{1,0:T(8,128)(2,1)S(1)}, bf16[1344,256]{1,0:T(8,128)(2,1)S(1)}, u32[]{:S(2)}, u32[]{:S(2)}) collective-permute-start(bf16[1344,256]{1,0:T(8,128)(2,1)S(1)} %get-tuple-element.87), channel_id=1, source_target_pairs={{16,17},{17,16},{18,19},{19,18},{20,21},{21,20},{22,23},{23,22},{2... | collective-permute-start | bytes 2064392 | tf_op jit(solution)/shard_map/ppermute | solution.py:492
  226.7 1.3 collective-permute-start.51
  228.0 12.1 %collective-permute-done.52 = bf16[1344,256]{1,0:T(8,128)(2,1)S(1)} collective-permute-done((bf16[1344,256]{1,0:T(8,128)(2,1)S(1)}, bf16[1344,256]{1,0:T(8,128)(2,1)S(1)}, u32[]{:S(2)}, u32[]{:S(2)}) %collective-permute-start.52) | collective-permute-done | bytes 688160 | tf_op jit(solution)/shard_map/ppermute | solution.py:492
  240.4 2.8 %collective-permute-done.51 = bf16[1344,256]{1,0:T(8,128)(2,1)S(1)} collective-permute-done((bf16[1344,256]{1,0:T(8,128)(2,1)S(1)}, bf16[1344,256]{1,0:T(8,128)(2,1)S(1)}, u32[]{:S(2)}, u32[]{:S(2)}) %collective-permute-start.51) | collective-permute-done | bytes 688160 | tf_op jit(solution)/shard_map/ppermute | solution.py:492
  (131 shorter events, 24.7 us)
Async XLA Ops:
  3.5 22.1 %collective-permute-start.8 = (bf16[2688,512]{1,0:T(8,128)(2,1)}, bf16[2688,512]{1,0:T(8,128)(2,1)}, u32[]{:S(2)}, u32[]{:S(2)}) collective-permute-start(bf16[2688,512]{1,0:T(8,128)(2,1)} %bitcast.23), channel_id=1, source_target_pairs={{0,16},{16,0},{1,17},{17,1},{2,18},{18,2},{3,19},{19,3},{4,20},{20... | collective-permute-start | bytes 8257544 | tf_op jit(solution)/shard_map/ppermute | solution.py:383
  3.6 26.5 %collective-permute-start.7 = (bf16[2688,512]{1,0:T(8,128)(2,1)}, bf16[2688,512]{1,0:T(8,128)(2,1)}, u32[]{:S(2)}, u32[]{:S(2)}) collective-permute-start(bf16[2688,512]{1,0:T(8,128)(2,1)} %bitcast.25), channel_id=1, source_target_pairs={{0,16},{16,0},{1,17},{17,1},{2,18},{18,2},{3,19},{19,3},{4,20},{20... | collective-permute-start | bytes 8257544 | tf_op jit(solution)/shard_map/ppermute | solution.py:383
  6.0 18.0 %collective-permute-start.3 = (bf16[2,336,512]{2,1,0:T(8,128)(2,1)S(1)}, bf16[2,336,512]{2,1,0:T(8,128)(2,1)}, u32[]{:S(2)}, u32[]{:S(2)}) collective-permute-start(bf16[2,336,512]{2,1,0:T(8,128)(2,1)S(1)} %get-tuple-element.96.refs_0_), channel_id=1, source_target_pairs={{0,4},{4,8},{8,12},{12,14},{14,10},{10,6},{6,2},{2,0},{1,5},{5,9},... | collective-permute-start | bytes 2064392 | tf_op jit(solution)/shard_map/ppermute | solution.py:347
  8.5 16.8 %collective-permute-start.5 = (bf16[2,336,512]{2,1,0:T(8,128)(2,1)S(1)}, bf16[2,336,512]{2,1,0:T(8,128)(2,1)}, u32[]{:S(2)}, u32[]{:S(2)}) collective-permute-start(bf16[2,336,512]{2,1,0:T(8,128)(2,1)S(1)} %get-tuple-element.96.refs_0_), channel_id=1, source_target_pairs={{4,0},{8,4},{12,8},{14,12},{10,14},{6,10},{2,6},{0,2},{5,1},{9,5},... | collective-permute-start | bytes 2064392 | tf_op jit(solution)/shard_map/ppermute | solution.py:348
  12.5 21.7 %collective-permute-start = (bf16[1344,256]{1,0:T(8,128)(2,1)S(1)}, bf16[1344,256]{1,0:T(8,128)(2,1)S(1)}, u32[]{:S(2)}, u32[]{:S(2)}) collective-permute-start(bf16[1344,256]{1,0:T(8,128)(2,1)S(1)} %dynamic-slice_bitcast_fusion.own.state), channel_id=1, source_target_pairs={{0,1},{1,0},{2,3},{3,2},{4,5},{5,4},{6,7},{7,6},{8,9},{9,8},{10,11... | collective-permute-start | bytes 2064392 | tf_op jit(solution)/shard_map/ppermute | solution.py:386
  24.1 16.4 %collective-permute-start.4 = (bf16[2,336,512]{2,1,0:T(8,128)(2,1)}, bf16[2,336,512]{2,1,0:T(8,128)(2,1)}, u32[]{:S(2)}, u32[]{:S(2)}) collective-permute-start(bf16[2,336,512]{2,1,0:T(8,128)(2,1)} %collective-permute-done.3.refs_1_), channel_id=1, source_target_pairs={{0,4},{4,8},{8,12},{12,14},{14,10},{10,6},{6,2},{2,0},{1,5},{5,9},... | collective-permute-start | bytes 2064392 | tf_op jit(solution)/shard_map/ppermute | solution.py:347
  25.3 15.8 %collective-permute-start.6 = (bf16[2,336,512]{2,1,0:T(8,128)(2,1)}, bf16[2,336,512]{2,1,0:T(8,128)(2,1)}, u32[]{:S(2)}, u32[]{:S(2)}) collective-permute-start(bf16[2,336,512]{2,1,0:T(8,128)(2,1)} %collective-permute-done.5.refs_7_), channel_id=1, source_target_pairs={{4,0},{8,4},{12,8},{14,12},{10,14},{6,10},{2,6},{0,2},{5,1},{9,5},... | collective-permute-start | bytes 2064392 | tf_op jit(solution)/shard_map/ppermute | solution.py:348
  38.9 15.9 %collective-permute-start.9 = (bf16[4,256,256]{2,1,0:T(8,128)(2,1)S(1)}, bf16[4,256,256]{2,1,0:T(8,128)(2,1)S(1)}, u32[]{:S(2)}, u32[]{:S(2)}) collective-permute-start(bf16[4,256,256]{2,1,0:T(8,128)(2,1)S(1)} %key_value.2.refs_0_), channel_id=1, source_target_pairs={{0,4},{2,6},{4,8},{6,10},{8,12},{10,14},{12,0},{14,2},{1,5},{3,7},... | collective-permute-start | bytes 1572872 | tf_op jit(solution)/shard_map/ppermute | solution.py:438
  54.7 29.3 %collective-permute-start.10 = (bf16[2,336,512]{2,1,0:T(8,128)(2,1)}, bf16[2,336,512]{2,1,0:T(8,128)(2,1)S(1)}, u32[]{:S(2)}, u32[]{:S(2)}) collective-permute-start(bf16[2,336,512]{2,1,0:T(8,128)(2,1)} %collective-permute-done.4.refs_2_), channel_id=1, source_target_pairs={{0,4},{4,8},{8,12},{12,14},{14,10},{10,6},{6,2},{2,0},{1,5},{5,9},... | collective-permute-start | bytes 2064392 | tf_op jit(solution)/shard_map/ppermute | solution.py:347
  54.8 26.4 %collective-permute-start.13 = (bf16[4,256,256]{2,1,0:T(8,128)(2,1)S(1)}, bf16[4,256,256]{2,1,0:T(8,128)(2,1)S(1)}, u32[]{:S(2)}, u32[]{:S(2)}) collective-permute-start(bf16[4,256,256]{2,1,0:T(8,128)(2,1)S(1)} %broadcast_select_fusion.9), channel_id=1, source_target_pairs={{0,2},{2,0},{4,6},{6,4},{8,10},{10,8},{12,14},{14,12},{1,3},{3,1},... | collective-permute-start | bytes 1572872 | tf_op jit(solution)/shard_map/ppermute | solution.py:441
  56.3 27.7 %collective-permute-start.12 = (bf16[4,256,256]{2,1,0:T(8,128)(2,1)S(1)}, bf16[4,256,256]{2,1,0:T(8,128)(2,1)S(1)}, u32[]{:S(2)}, u32[]{:S(2)}) collective-permute-start(bf16[4,256,256]{2,1,0:T(8,128)(2,1)S(1)} %collective-permute-done.9.refs_1_), channel_id=1, source_target_pairs={{0,4},{2,6},{4,8},{6,10},{8,12},{10,14},{12,0},{14,2},{1,5},{3,7},... | collective-permute-start | bytes 1572872 | tf_op jit(solution)/shard_map/ppermute | solution.py:438
  56.3 28.2 %collective-permute-start.11 = (bf16[2,336,512]{2,1,0:T(8,128)(2,1)}, bf16[2,336,512]{2,1,0:T(8,128)(2,1)S(1)}, u32[]{:S(2)}, u32[]{:S(2)}) collective-permute-start(bf16[2,336,512]{2,1,0:T(8,128)(2,1)} %collective-permute-done.6.refs_6_), channel_id=1, source_target_pairs={{4,0},{8,4},{12,8},{14,12},{10,14},{6,10},{2,6},{0,2},{5,1},{9,5},... | collective-permute-start | bytes 2064392 | tf_op jit(solution)/shard_map/ppermute | solution.py:348
  56.5 29.2 %collective-permute-start.15 = (bf16[2,336,512]{2,1,0:T(8,128)(2,1)S(1)}, bf16[2,336,512]{2,1,0:T(8,128)(2,1)S(1)}, u32[]{:S(2)}, u32[]{:S(2)}) collective-permute-start(bf16[2,336,512]{2,1,0:T(8,128)(2,1)S(1)} %get-tuple-element.96.refs_0_), channel_id=1, source_target_pairs={{0,16},{16,0},{1,17},{17,1},{2,18},{18,2},{3,19},{19,3},{4,20},{20... | collective-permute-start | bytes 2064392 | tf_op jit(solution)/shard_map/ppermute | solution.py:383
  81.2 4.8 %collective-permute-start.16 = (bf16[2,336,512]{2,1,0:T(8,128)(2,1)}, bf16[2,336,512]{2,1,0:T(8,128)(2,1)S(1)}, u32[]{:S(2)}, u32[]{:S(2)}) collective-permute-start(bf16[2,336,512]{2,1,0:T(8,128)(2,1)} %collective-permute-done.3.refs_1_), channel_id=1, source_target_pairs={{0,16},{16,0},{1,17},{17,1},{2,18},{18,2},{3,19},{19,3},{4,20},{20... | collective-permute-start | bytes 2064392 | tf_op jit(solution)/shard_map/ppermute | solution.py:383
  84.0 4.9 %collective-permute-start.17 = (bf16[2,336,512]{2,1,0:T(8,128)(2,1)}, bf16[2,336,512]{2,1,0:T(8,128)(2,1)S(1)}, u32[]{:S(2)}, u32[]{:S(2)}) collective-permute-start(bf16[2,336,512]{2,1,0:T(8,128)(2,1)} %collective-permute-done.4.refs_2_), channel_id=1, source_target_pairs={{0,16},{16,0},{1,17},{17,1},{2,18},{18,2},{3,19},{19,3},{4,20},{20... | collective-permute-start | bytes 2064392 | tf_op jit(solution)/shard_map/ppermute | solution.py:383
  84.5 6.4 %collective-permute-start.21 = (bf16[2,336,512]{2,1,0:T(8,128)(2,1)}, bf16[2,336,512]{2,1,0:T(8,128)(2,1)S(1)}, u32[]{:S(2)}, u32[]{:S(2)}) collective-permute-start(bf16[2,336,512]{2,1,0:T(8,128)(2,1)} %collective-permute-done.6.refs_6_), channel_id=1, source_target_pairs={{0,16},{16,0},{1,17},{17,1},{2,18},{18,2},{3,19},{19,3},{4,20},{20... | collective-permute-start | bytes 2064392 | tf_op jit(solution)/shard_map/ppermute | solution.py:383
  85.7 13.9 %collective-permute-start.18 = (bf16[2,336,512]{2,1,0:T(8,128)(2,1)S(1)}, bf16[2,336,512]{2,1,0:T(8,128)(2,1)S(1)}, u32[]{:S(2)}, u32[]{:S(2)}) collective-permute-start(bf16[2,336,512]{2,1,0:T(8,128)(2,1)S(1)} %collective-permute-done.10.refs_3_), channel_id=1, source_target_pairs={{0,16},{16,0},{1,17},{17,1},{2,18},{18,2},{3,19},{19,3},{4,20},{20... | collective-permute-start | bytes 2064392 | tf_op jit(solution)/shard_map/ppermute | solution.py:383
  86.0 13.5 %collective-permute-start.20 = (bf16[2,336,512]{2,1,0:T(8,128)(2,1)S(1)}, bf16[2,336,512]{2,1,0:T(8,128)(2,1)S(1)}, u32[]{:S(2)}, u32[]{:S(2)}) collective-permute-start(bf16[2,336,512]{2,1,0:T(8,128)(2,1)S(1)} %collective-permute-done.11.refs_5_), channel_id=1, source_target_pairs={{0,16},{16,0},{1,17},{17,1},{2,18},{18,2},{3,19},{19,3},{4,20},{20... | collective-permute-start | bytes 2064392 | tf_op jit(solution)/shard_map/ppermute | solution.py:383
  87.0 9.3 %collective-permute-start.14 = (bf16[1,336,512]{2,1,0:T(8,128)(2,1)S(1)}, bf16[1,336,512]{2,1,0:T(8,128)(2,1)S(1)}, u32[]{:S(2)}, u32[]{:S(2)}) collective-permute-start(bf16[1,336,512]{2,1,0:T(8,128)(2,1)S(1)} %slice.12), channel_id=1, source_target_pairs={{0,4},{4,8},{8,12},{12,14},{14,10},{10,6},{6,2},{2,0},{1,5},{5,9},... | collective-permute-start | bytes 1032200 | tf_op jit(solution)/shard_map/ppermute | solution.py:351
  89.0 9.3 %collective-permute-start.24 = (bf16[1,336,512]{2,1,0:T(8,128)(2,1)S(1)}, bf16[1,336,512]{2,1,0:T(8,128)(2,1)S(1)}, u32[]{:S(2)}, u32[]{:S(2)}) collective-permute-start(bf16[1,336,512]{2,1,0:T(8,128)(2,1)S(1)} %slice.13), channel_id=1, source_target_pairs={{4,0},{8,4},{12,8},{14,12},{10,14},{6,10},{2,6},{0,2},{5,1},{9,5},... | collective-permute-start | bytes 1032200 | tf_op jit(solution)/shard_map/ppermute | solution.py:352
  90.9 19.0 %collective-permute-start.23 = (bf16[4,256,256]{2,1,0:T(8,128)(2,1)S(1)}, bf16[4,256,256]{2,1,0:T(8,128)(2,1)S(1)}, u32[]{:S(2)}, u32[]{:S(2)}) collective-permute-start(bf16[4,256,256]{2,1,0:T(8,128)(2,1)S(1)} %broadcast_select_fusion.8), channel_id=1, source_target_pairs={{0,2},{2,0},{4,6},{6,4},{8,10},{10,8},{12,14},{14,12},{1,3},{3,1},... | collective-permute-start | bytes 1572872 | tf_op jit(solution)/shard_map/ppermute | solution.py:441
  98.3 11.7 %collective-permute-start.25 = (bf16[1,336,512]{2,1,0:T(8,128)(2,1)S(1)}, bf16[1,336,512]{2,1,0:T(8,128)(2,1)S(1)}, u32[]{:S(2)}, u32[]{:S(2)}) collective-permute-start(bf16[1,336,512]{2,1,0:T(8,128)(2,1)S(1)} %collective-permute-done.24.refs_4_), channel_id=1, source_target_pairs={{0,16},{16,0},{1,17},{17,1},{2,18},{18,2},{3,19},{19,3},{4,20},{20... | collective-permute-start | bytes 1032200 | tf_op jit(solution)/shard_map/ppermute | solution.py:383
  115.8 16.7 %collective-permute-start.28 = (bf16[1344,256]{1,0:T(8,128)(2,1)S(1)}, bf16[1344,256]{1,0:T(8,128)(2,1)S(1)}, u32[]{:S(2)}, u32[]{:S(2)}) collective-permute-start(bf16[1344,256]{1,0:T(8,128)(2,1)S(1)} %get-tuple-element.67), channel_id=1, source_target_pairs={{0,1},{1,0},{2,3},{3,2},{4,5},{5,4},{6,7},{7,6},{8,9},{9,8},{10,11... | collective-permute-start | bytes 2064392 | tf_op jit(solution)/shard_map/ppermute | solution.py:386
  117.0 16.3 %collective-permute-start.26 = (bf16[2,336,512]{2,1,0:T(8,128)(2,1)S(1)}, bf16[2,336,512]{2,1,0:T(8,128)(2,1)S(1)}, u32[]{:S(2)}, u32[]{:S(2)}) collective-permute-start(bf16[2,336,512]{2,1,0:T(8,128)(2,1)S(1)} %get-tuple-element.66.refs_0_), channel_id=1, source_target_pairs={{0,4},{4,8},{8,12},{12,14},{14,10},{10,6},{6,2},{2,0},{1,5},{5,9},... | collective-permute-start | bytes 2064392 | tf_op jit(solution)/shard_map/ppermute | solution.py:347
  117.0 16.3 %collective-permute-start.27 = (bf16[2,336,512]{2,1,0:T(8,128)(2,1)S(1)}, bf16[2,336,512]{2,1,0:T(8,128)(2,1)S(1)}, u32[]{:S(2)}, u32[]{:S(2)}) collective-permute-start(bf16[2,336,512]{2,1,0:T(8,128)(2,1)S(1)} %get-tuple-element.66.refs_0_), channel_id=1, source_target_pairs={{4,0},{8,4},{12,8},{14,12},{10,14},{6,10},{2,6},{0,2},{5,1},{9,5},... | collective-permute-start | bytes 2064392 | tf_op jit(solution)/shard_map/ppermute | solution.py:348
  133.5 15.5 %collective-permute-start.31 = (bf16[1344,256]{1,0:T(8,128)(2,1)S(1)}, bf16[1344,256]{1,0:T(8,128)(2,1)S(1)}, u32[]{:S(2)}, u32[]{:S(2)}) collective-permute-start(bf16[1344,256]{1,0:T(8,128)(2,1)S(1)} %add_convert_fusion.2.own.state), channel_id=1, source_target_pairs={{0,1},{1,0},{2,3},{3,2},{4,5},{5,4},{6,7},{7,6},{8,9},{9,8},{10,11... | collective-permute-start | bytes 2064392 | tf_op jit(solution)/shard_map/ppermute | solution.py:386
  134.2 15.7 %collective-permute-start.29 = (bf16[2,336,512]{2,1,0:T(8,128)(2,1)S(1)}, bf16[2,336,512]{2,1,0:T(8,128)(2,1)}, u32[]{:S(2)}, u32[]{:S(2)}) collective-permute-start(bf16[2,336,512]{2,1,0:T(8,128)(2,1)S(1)} %collective-permute-done.26.refs_1_), channel_id=1, source_target_pairs={{0,4},{4,8},{8,12},{12,14},{14,10},{10,6},{6,2},{2,0},{1,5},{5,9},... | collective-permute-start | bytes 2064392 | tf_op jit(solution)/shard_map/ppermute | solution.py:347
  134.5 15.4 %collective-permute-start.30 = (bf16[2,336,512]{2,1,0:T(8,128)(2,1)S(1)}, bf16[2,336,512]{2,1,0:T(8,128)(2,1)}, u32[]{:S(2)}, u32[]{:S(2)}) collective-permute-start(bf16[2,336,512]{2,1,0:T(8,128)(2,1)S(1)} %collective-permute-done.27.refs_7_), channel_id=1, source_target_pairs={{4,0},{8,4},{12,8},{14,12},{10,14},{6,10},{2,6},{0,2},{5,1},{9,5},... | collective-permute-start | bytes 2064392 | tf_op jit(solution)/shard_map/ppermute | solution.py:348
  135.6 23.4 %collective-permute-start.35 = (bf16[1344,256]{1,0:T(8,128)(2,1)S(1)}, bf16[1344,256]{1,0:T(8,128)(2,1)S(1)}, u32[]{:S(2)}, u32[]{:S(2)}) collective-permute-start(bf16[1344,256]{1,0:T(8,128)(2,1)S(1)} %add_convert_fusion.2.own.state), channel_id=1, source_target_pairs={{16,0},{17,1},{18,2},{19,3},{20,4},{21,5},{22,6},{23,7},{24,8},{25... | collective-permute-start | bytes 2064392 | tf_op jit(solution)/shard_map/ppermute | solution.py:487
  149.9 26.3 %collective-permute-start.32 = (bf16[2,336,512]{2,1,0:T(8,128)(2,1)}, bf16[2,336,512]{2,1,0:T(8,128)(2,1)S(1)}, u32[]{:S(2)}, u32[]{:S(2)}) collective-permute-start(bf16[2,336,512]{2,1,0:T(8,128)(2,1)} %collective-permute-done.29.refs_2_), channel_id=1, source_target_pairs={{0,4},{4,8},{8,12},{12,14},{14,10},{10,6},{6,2},{2,0},{1,5},{5,9},... | collective-permute-start | bytes 2064392 | tf_op jit(solution)/shard_map/ppermute | solution.py:347
  150.1 26.1 %collective-permute-start.33 = (bf16[2,336,512]{2,1,0:T(8,128)(2,1)}, bf16[2,336,512]{2,1,0:T(8,128)(2,1)}, u32[]{:S(2)}, u32[]{:S(2)}) collective-permute-start(bf16[2,336,512]{2,1,0:T(8,128)(2,1)} %collective-permute-done.30.refs_6_), channel_id=1, source_target_pairs={{4,0},{8,4},{12,8},{14,12},{10,14},{6,10},{2,6},{0,2},{5,1},{9,5},... | collective-permute-start | bytes 2064392 | tf_op jit(solution)/shard_map/ppermute | solution.py:348
  158.7 17.5 %collective-permute-start.34 = (bf16[4,256,256]{2,1,0:T(8,128)(2,1)S(1)}, bf16[4,256,256]{2,1,0:T(8,128)(2,1)S(1)}, u32[]{:S(2)}, u32[]{:S(2)}) collective-permute-start(bf16[4,256,256]{2,1,0:T(8,128)(2,1)S(1)} %key_value.3.refs_0_), channel_id=1, source_target_pairs={{0,4},{2,6},{4,8},{6,10},{8,12},{10,14},{12,0},{14,2},{1,5},{3,7},... | collective-permute-start | bytes 1572872 | tf_op jit(solution)/shard_map/ppermute | solution.py:438
  176.3 9.7 %collective-permute-start.37 = (bf16[4,256,256]{2,1,0:T(8,128)(2,1)S(1)}, bf16[4,256,256]{2,1,0:T(8,128)(2,1)S(1)}, u32[]{:S(2)}, u32[]{:S(2)}) collective-permute-start(bf16[4,256,256]{2,1,0:T(8,128)(2,1)S(1)} %broadcast_select_fusion.7), channel_id=1, source_target_pairs={{0,2},{2,0},{4,6},{6,4},{8,10},{10,8},{12,14},{14,12},{1,3},{3,1},... | collective-permute-start | bytes 1572872 | tf_op jit(solution)/shard_map/ppermute | solution.py:441
  177.2 13.5 %collective-permute-start.36 = (bf16[4,256,256]{2,1,0:T(8,128)(2,1)S(1)}, bf16[4,256,256]{2,1,0:T(8,128)(2,1)S(1)}, u32[]{:S(2)}, u32[]{:S(2)}) collective-permute-start(bf16[4,256,256]{2,1,0:T(8,128)(2,1)S(1)} %collective-permute-done.34.refs_1_), channel_id=1, source_target_pairs={{0,4},{2,6},{4,8},{6,10},{8,12},{10,14},{12,0},{14,2},{1,5},{3,7},... | collective-permute-start | bytes 1572872 | tf_op jit(solution)/shard_map/ppermute | solution.py:438
  177.8 16.5 %collective-permute-start.39 = (bf16[2,336,512]{2,1,0:T(8,128)(2,1)S(1)}, bf16[2,336,512]{2,1,0:T(8,128)(2,1)S(1)}, u32[]{:S(2)}, u32[]{:S(2)}) collective-permute-start(bf16[2,336,512]{2,1,0:T(8,128)(2,1)S(1)} %get-tuple-element.66.refs_0_), channel_id=1, source_target_pairs={{0,16},{16,0},{1,17},{17,1},{2,18},{18,2},{3,19},{19,3},{4,20},{20... | collective-permute-start | bytes 2064392 | tf_op jit(solution)/shard_map/ppermute | solution.py:383
  182.9 11.5 %collective-permute-start.40 = (bf16[2,336,512]{2,1,0:T(8,128)(2,1)S(1)}, bf16[2,336,512]{2,1,0:T(8,128)(2,1)S(1)}, u32[]{:S(2)}, u32[]{:S(2)}) collective-permute-start(bf16[2,336,512]{2,1,0:T(8,128)(2,1)S(1)} %copy-done.11), channel_id=1, source_target_pairs={{0,16},{16,0},{1,17},{17,1},{2,18},{18,2},{3,19},{19,3},{4,20},{20... | collective-permute-start | bytes 2064392 | tf_op jit(solution)/shard_map/ppermute | solution.py:383
  182.9 12.0 %collective-permute-start.46 = (bf16[2,336,512]{2,1,0:T(8,128)(2,1)S(1)}, bf16[2,336,512]{2,1,0:T(8,128)(2,1)S(1)}, u32[]{:S(2)}, u32[]{:S(2)}) collective-permute-start(bf16[2,336,512]{2,1,0:T(8,128)(2,1)S(1)} %copy-done.13), channel_id=1, source_target_pairs={{0,16},{16,0},{1,17},{17,1},{2,18},{18,2},{3,19},{19,3},{4,20},{20... | collective-permute-start | bytes 2064392 | tf_op jit(solution)/shard_map/ppermute | solution.py:383
  186.0 9.0 %collective-permute-start.41 = (bf16[2,336,512]{2,1,0:T(8,128)(2,1)}, bf16[2,336,512]{2,1,0:T(8,128)(2,1)S(1)}, u32[]{:S(2)}, u32[]{:S(2)}) collective-permute-start(bf16[2,336,512]{2,1,0:T(8,128)(2,1)} %collective-permute-done.29.refs_2_), channel_id=1, source_target_pairs={{0,16},{16,0},{1,17},{17,1},{2,18},{18,2},{3,19},{19,3},{4,20},{20... | collective-permute-start | bytes 2064392 | tf_op jit(solution)/shard_map/ppermute | solution.py:383
  190.7 5.8 %collective-permute-start.45 = (bf16[2,336,512]{2,1,0:T(8,128)(2,1)}, bf16[2,336,512]{2,1,0:T(8,128)(2,1)S(1)}, u32[]{:S(2)}, u32[]{:S(2)}) collective-permute-start(bf16[2,336,512]{2,1,0:T(8,128)(2,1)} %collective-permute-done.30.refs_6_), channel_id=1, source_target_pairs={{0,16},{16,0},{1,17},{17,1},{2,18},{18,2},{3,19},{19,3},{4,20},{20... | collective-permute-start | bytes 2064392 | tf_op jit(solution)/shard_map/ppermute | solution.py:383
  194.3 12.8 %collective-permute-start.42 = (bf16[2,336,512]{2,1,0:T(8,128)(2,1)S(1)}, bf16[2,336,512]{2,1,0:T(8,128)(2,1)S(1)}, u32[]{:S(2)}, u32[]{:S(2)}) collective-permute-start(bf16[2,336,512]{2,1,0:T(8,128)(2,1)S(1)} %collective-permute-done.32.refs_3_), channel_id=1, source_target_pairs={{0,16},{16,0},{1,17},{17,1},{2,18},{18,2},{3,19},{19,3},{4,20},{20... | collective-permute-start | bytes 2064392 | tf_op jit(solution)/shard_map/ppermute | solution.py:383
  194.4 12.7 %collective-permute-start.44 = (bf16[2,336,512]{2,1,0:T(8,128)(2,1)}, bf16[2,336,512]{2,1,0:T(8,128)(2,1)S(1)}, u32[]{:S(2)}, u32[]{:S(2)}) collective-permute-start(bf16[2,336,512]{2,1,0:T(8,128)(2,1)} %collective-permute-done.33.refs_5_), channel_id=1, source_target_pairs={{0,16},{16,0},{1,17},{17,1},{2,18},{18,2},{3,19},{19,3},{4,20},{20... | collective-permute-start | bytes 2064392 | tf_op jit(solution)/shard_map/ppermute | solution.py:383
  194.9 9.6 %collective-permute-start.38 = (bf16[1,336,512]{2,1,0:T(8,128)(2,1)S(1)}, bf16[1,336,512]{2,1,0:T(8,128)(2,1)S(1)}, u32[]{:S(2)}, u32[]{:S(2)}) collective-permute-start(bf16[1,336,512]{2,1,0:T(8,128)(2,1)S(1)} %slice.14), channel_id=1, source_target_pairs={{0,4},{4,8},{8,12},{12,14},{14,10},{10,6},{6,2},{2,0},{1,5},{5,9},... | collective-permute-start | bytes 1032200 | tf_op jit(solution)/shard_map/ppermute | solution.py:351
  194.9 10.9 %collective-permute-start.48 = (bf16[1,336,512]{2,1,0:T(8,128)(2,1)S(1)}, bf16[1,336,512]{2,1,0:T(8,128)(2,1)S(1)}, u32[]{:S(2)}, u32[]{:S(2)}) collective-permute-start(bf16[1,336,512]{2,1,0:T(8,128)(2,1)S(1)} %slice.15), channel_id=1, source_target_pairs={{4,0},{8,4},{12,8},{14,12},{10,14},{6,10},{2,6},{0,2},{5,1},{9,5},... | collective-permute-start | bytes 1032200 | tf_op jit(solution)/shard_map/ppermute | solution.py:352
  196.5 20.8 %collective-permute-start.47 = (bf16[4,256,256]{2,1,0:T(8,128)(2,1)S(1)}, bf16[4,256,256]{2,1,0:T(8,128)(2,1)S(1)}, u32[]{:S(2)}, u32[]{:S(2)}) collective-permute-start(bf16[4,256,256]{2,1,0:T(8,128)(2,1)S(1)} %broadcast_select_fusion.6), channel_id=1, source_target_pairs={{0,2},{2,0},{4,6},{6,4},{8,10},{10,8},{12,14},{14,12},{1,3},{3,1},... | collective-permute-start | bytes 1572872 | tf_op jit(solution)/shard_map/ppermute | solution.py:441
  205.9 11.4 %collective-permute-start.49 = (bf16[1,336,512]{2,1,0:T(8,128)(2,1)S(1)}, bf16[1,336,512]{2,1,0:T(8,128)(2,1)S(1)}, u32[]{:S(2)}, u32[]{:S(2)}) collective-permute-start(bf16[1,336,512]{2,1,0:T(8,128)(2,1)S(1)} %collective-permute-done.48.refs_4_), channel_id=1, source_target_pairs={{0,16},{16,0},{1,17},{17,1},{2,18},{18,2},{3,19},{19,3},{4,20},{20... | collective-permute-start | bytes 1032200 | tf_op jit(solution)/shard_map/ppermute | solution.py:383
  222.9 20.4 %collective-permute-start.50 = (f32[1344,256]{1,0:T(8,128)S(1)}, f32[1344,256]{1,0:T(8,128)S(1)}, u32[]{:S(2)}, u32[]{:S(2)}) collective-permute-start(f32[1344,256]{1,0:T(8,128)S(1)} %get-tuple-element.86), channel_id=1, source_target_pairs={{0,16},{1,17},{2,18},{3,19},{4,20},{5,21},{6,22},{7,23},{8,24},{9,... | collective-permute-start | bytes 4128776 | tf_op jit(solution)/shard_map/ppermute | solution.py:493
  224.2 15.9 %collective-permute-start.52 = (bf16[1344,256]{1,0:T(8,128)(2,1)S(1)}, bf16[1344,256]{1,0:T(8,128)(2,1)S(1)}, u32[]{:S(2)}, u32[]{:S(2)}) collective-permute-start(bf16[1344,256]{1,0:T(8,128)(2,1)S(1)} %get-tuple-element.87), channel_id=1, source_target_pairs={{16,17},{17,16},{18,19},{19,18},{20,21},{21,20},{22,23},{23,22},{2... | collective-permute-start | bytes 2064392 | tf_op jit(solution)/shard_map/ppermute | solution.py:492
  226.7 16.5 %collective-permute-start.51 = (bf16[1344,256]{1,0:T(8,128)(2,1)S(1)}, bf16[1344,256]{1,0:T(8,128)(2,1)S(1)}, u32[]{:S(2)}, u32[]{:S(2)}) collective-permute-start(bf16[1344,256]{1,0:T(8,128)(2,1)S(1)} %get-tuple-element.87), channel_id=1, source_target_pairs={{0,17},{1,16},{2,19},{3,18},{4,21},{5,20},{6,23},{7,22},{8,25},{9,... | collective-permute-start | bytes 2064392 | tf_op jit(solution)/shard_map/ppermute | solution.py:492
  (25 other events, 203.5 us)

commit v5 on v4

--- a/solution.py
+++ b/solution.py
@@ -442,6 +442,7 @@
 
     ring = Ring(shards[0], count)
     ring.step()
+    key_value_weights[0] = ring.close(*key_value_weights[0])
     states = []
     for layer in range(LAYERS):
         ring.step()

time: 245 us -> 249 us (1.016)
  Pallas kernels: 37.1 us -> 40 us
  other arithmetic: 14.6 us -> 17.4 us
    ppermute x4, waiting for transfers between devices: 30.8 us -> 37.5 us  [shifted(): return lax.ppermute(value, 'seq', up)]
    ppermute x6, waiting for transfers between devices: 10.3 us -> 5.49 us  [step(): self.forward.append(lax.ppermute(self.forward[-1], 'seq', self.onward))]
    unnamed x40 -> x46, local copies, waits for them, and re-layouts: 8.1 us -> 7.21 us
  transfers between devices with their start and end apart: 53 -> 53, of which waited for: 22 -> 20; matrix products, arithmetic and copies ran while one was open for 5% -> 6% of each run, Pallas kernels for 11% -> 11%
where the time goes in v5:
time: 249 us; the launch traced here: 248 us
  waiting for transfers between devices  126 us (51%)
  starting transfers between devices  55.2 us (22%)
  Pallas kernels  40 us (16%)
  other arithmetic  17.4 us (7%)
  local copies, waits for them, and re-layouts  8.49 us (3%)
    ppermute x4, waiting for transfers between devices, shifted(): return lax.ppermute(value, 'seq', up)  37.5 us
    ppermute x22, starting transfers between devices, across_chip(): return lax.ppermute(value, 'segment', SWAP)  27.7 us
    ppermute x4, waiting for transfers between devices, swapped(): return lax.ppermute(jnp.where(even, near, far), 'seq', beside)  24 us
    ppermute x3, waiting for transfers between devices, across_tp(): return lax.ppermute(value, 'tp', SWAP)  22.8 us
    ppermute x2, waiting for transfers between devices, per_device(): arrived = [lax.ppermute(leave, ('segment', 'tp'), pair) for pair in pairs]  15.3 us
    ppermute x2, waiting for transfers between devices, step(): lax.ppermute(self.forward[-1][:1], 'seq', self.onward)  12.1 us
    pallas_call x2, Pallas kernels, out_project(): call(functools.partial(out_kernel, count, distance, reach), (jax.ShapeDty...  11.5 us
    pallas_call x2, Pallas kernels, query(): call(functools.partial(query_kernel, count), jax.ShapeDtypeStruct((2, col...  10.9 us
  transfers between devices with their start and end apart: 53, of which 20 were waited for; matrix products, arithmetic and copies ran while one was open for 6% of the time, Pallas kernels for 11%

profile of v5, /device:TPU:1, one launch (start us, length us, event | category | flops | bytes accessed | tf_op | source)
XLA Modules:
  0.0 247.9 jit_solution(3015464502238107184)
XLA Ops:
  0.0 1.2 fusion.5
  1.4 2.2 collective-permute-done.1
  4.2 2.4 collective-permute-start
  7.3 2.4 broadcast_select_fusion.4
  9.7 1.3 collective-permute-start.3
  12.4 4.1 %broadcast_select_fusion = (bf16[2688,512]{1,0:T(8,128)(2,1)}, bf16[2688,512]{1,0:T(8,128)(2,1)S(1)}) fusion(bf16[2688,512]{1,0:T(8,128)(2,1)} %collective-permute-done.6, bf16[2688,512]{1,0:T(8,128)(2,1)S(1)} %bitcast.24, pred[]{:T(512)S(6)} %eq.8), kind=kLoop, calls=%fused_computation | loop fusion | flops 2752512 | bytes 11010049 | tf_op jit(solution)/shard_map/jit(_where)/select_n | solution.py:410
  16.6 4.9 %broadcast_select_fusion.1 = (bf16[2688,512]{1,0:T(8,128)(2,1)}, bf16[2688,512]{1,0:T(8,128)(2,1)}) fusion(bf16[2688,512]{1,0:T(8,128)(2,1)} %collective-permute-done.5, bf16[2688,512]{1,0:T(8,128)(2,1)S(1)} %bitcast.26, pred[]{:T(512)S(6)} %eq.8), kind=kLoop, calls=%fused_computation.1 | loop fusion | flops 2752512 | bytes 11010049 | tf_op jit(solution)/shard_map/jit(_where)/select_n | solution.py:410
  21.5 4.7 %collective-permute-done.3.refs_1_ = bf16[2,336,512]{2,1,0:T(8,128)(2,1)} collective-permute-done((bf16[2,336,512]{2,1,0:T(8,128)(2,1)S(1)}, bf16[2,336,512]{2,1,0:T(8,128)(2,1)}, u32[]{:S(2)}, u32[]{:S(2)}) %collective-permute-start.3) | collective-permute-done | bytes 688160 | tf_op jit(solution)/shard_map/ppermute | solution.py:347
  27.2 1.3 collective-permute-start.7
  29.5 1.8 copy-done.4
  32.2 4.5 %key_value.2.refs_0_ = bf16[4,256,256]{2,1,0:T(8,128)(2,1)} custom-call(bf16[1344,256]{1,0:T(8,128)(2,1)S(1)} %dynamic-slice_bitcast_fusion.own.state, bf16[1344,256]{1,0:T(8,128)(2,1)} %collective-permute-done.other, f32[2,1344]{1,0:T(2,128)S(1)} %reshape.16.gain, f32[2,256,128]{2,1,0:T(8,128)S(1)} %copy-done.5, bf16[2688,512]{1,0:T(8,128)(2,1)S(1)} %copy-done.4, ...), custom_call_target="tpu_custom_call" | custom-call | tf_op jit(solution)/shard_map/key_value/pallas_call | solution.py:122
  36.8 1.3 collective-permute-start.9
  38.2 18.6 %collective-permute-done.9.refs_1_ = bf16[4,256,256]{2,1,0:T(8,128)(2,1)S(1)} collective-permute-done((bf16[4,256,256]{2,1,0:T(8,128)(2,1)}, bf16[4,256,256]{2,1,0:T(8,128)(2,1)S(1)}, u32[]{:S(2)}, u32[]{:S(2)}) %collective-permute-start.9) | collective-permute-done | bytes 524320 | tf_op jit(solution)/shard_map/ppermute | solution.py:438
  59.4 3.6 %collective-permute-start.15 = (bf16[2,336,512]{2,1,0:T(8,128)(2,1)S(1)}, bf16[2,336,512]{2,1,0:T(8,128)(2,1)S(1)}, u32[]{:S(2)}, u32[]{:S(2)}) collective-permute-start(bf16[2,336,512]{2,1,0:T(8,128)(2,1)S(1)} %copy-done.9), channel_id=1, source_target_pairs={{0,16},{16,0},{1,17},{17,1},{2,18},{18,2},{3,19},{19,3},{4,20},{20... | collective-permute-start | bytes 2064392 | tf_op jit(solution)/shard_map/ppermute | solution.py:383
  63.0 19.1 %collective-permute-done.13.refs_3_ = bf16[4,256,256]{2,1,0:T(8,128)(2,1)S(1)} collective-permute-done((bf16[4,256,256]{2,1,0:T(8,128)(2,1)S(1)}, bf16[4,256,256]{2,1,0:T(8,128)(2,1)S(1)}, u32[]{:S(2)}, u32[]{:S(2)}) %collective-permute-start.13) | collective-permute-done | bytes 524320 | tf_op jit(solution)/shard_map/ppermute | solution.py:441
  82.1 3.9 %collective-permute-start.16 = (bf16[2,336,512]{2,1,0:T(8,128)(2,1)}, bf16[2,336,512]{2,1,0:T(8,128)(2,1)S(1)}, u32[]{:S(2)}, u32[]{:S(2)}) collective-permute-start(bf16[2,336,512]{2,1,0:T(8,128)(2,1)} %collective-permute-done.3.refs_1_), channel_id=1, source_target_pairs={{0,16},{16,0},{1,17},{17,1},{2,18},{18,2},{3,19},{19,3},{4,20},{20... | collective-permute-start | bytes 2064392 | tf_op jit(solution)/shard_map/ppermute | solution.py:383
  89.0 2.0 collective-permute-done.17.refs_10_
  91.0 1.9 collective-permute-done.21.refs_14_
  92.9 5.3 %collective-permute-done.14.refs_4_ = bf16[1,336,512]{2,1,0:T(8,128)(2,1)S(1)} collective-permute-done((bf16[1,336,512]{2,1,0:T(8,128)(2,1)S(1)}, bf16[1,336,512]{2,1,0:T(8,128)(2,1)S(1)}, u32[]{:S(2)}, u32[]{:S(2)}) %collective-permute-start.14) | collective-permute-done | bytes 344096 | tf_op jit(solution)/shard_map/ppermute | solution.py:351
  98.3 2.0 collective-permute-start.19
  101.6 5.6 %query.2.queries = bf16[2,512,256]{2,1,0:T(8,128)(2,1)S(1)} custom-call(bf16[1344,256]{1,0:T(8,128)(2,1)S(1)} %dynamic-slice_bitcast_fusion.own.state, bf16[1344,256]{1,0:T(8,128)(2,1)} %collective-permute-done.other, f32[2,1344]{1,0:T(2,128)S(1)} %reshape.16.gain, f32[2,256,128]{2,1,0:T(8,128)S(1)} %copy-done.6, bf16[2,336,512]{2,1,0:T(8,128)(2,1)S(1)} %copy-done.9, ...), custom_call_target="tpu_custom_call" | custom-call | tf_op jit(solution)/shard_map/query/pallas_call | solution.py:169
  107.2 5.4 %attend.2 = (f32[2,512,256]{2,1,0:T(8,128)S(1)}, f32[8,256]{1,0:T(8,128)S(1)}, f32[8,256]{1,0:T(8,128)S(1)}) custom-call(s32[2,8]{1,0:T(2,128)S(1)} %copy-done.16, s32[2]{0:T(128)S(1)} %copy-done.17, bf16[2,512,256]{2,1,0:T(8,128)(2,1)S(1)} %query.2.queries, bf16[4,256,256]{2,1,0:T(8,128)(2,1)} %key_value.2.refs_0_, ...), custom_call_target="tpu_custom_call" | custom-call | tf_op jit(solution)/shard_map/attend/pallas_call | solution.py:251
  112.7 5.9 %out_project.2 = (bf16[1344,256]{1,0:T(8,128)(2,1)S(1)}, f32[1344,256]{1,0:T(8,128)S(1)}) custom-call(s32[2,8]{1,0:T(2,128)S(1)} %copy-done.16, s32[2]{0:T(128)S(1)} %copy-done.17, bf16[2,512,256]{2,1,0:T(8,128)(2,1)S(1)} %query.2.queries, bf16[4,256,256]{2,1,0:T(8,128)(2,1)S(1)} %collective-permute-done.23.window, ...), custom_call_target="tpu_custom_call" | custom-call | tf_op jit(solution)/shard_map/out_project/pallas_call | solution.py:314
  118.9 1.5 collective-permute-start.27
  120.4 14.9 %collective-permute-done.28 = bf16[1344,256]{1,0:T(8,128)(2,1)S(1)} collective-permute-done((bf16[1344,256]{1,0:T(8,128)(2,1)S(1)}, bf16[1344,256]{1,0:T(8,128)(2,1)S(1)}, u32[]{:S(2)}, u32[]{:S(2)}) %collective-permute-start.28) | collective-permute-done | bytes 688160 | tf_op jit(solution)/shard_map/ppermute | solution.py:386
  138.1 5.1 %collective-permute-start.35 = (bf16[1344,256]{1,0:T(8,128)(2,1)S(1)}, bf16[1344,256]{1,0:T(8,128)(2,1)}, u32[]{:S(2)}, u32[]{:S(2)}) collective-permute-start(bf16[1344,256]{1,0:T(8,128)(2,1)S(1)} %add_convert_fusion.2.own.state), channel_id=1, source_target_pairs={{16,0},{17,1},{18,2},{19,3},{20,4},{21,5},{22,6},{23,7},{24,8},{25... | collective-permute-start | bytes 2064392 | tf_op jit(solution)/shard_map/ppermute | solution.py:488
  143.2 7.8 %collective-permute-done.31.other = bf16[1344,256]{1,0:T(8,128)(2,1)S(1)} collective-permute-done((bf16[1344,256]{1,0:T(8,128)(2,1)S(1)}, bf16[1344,256]{1,0:T(8,128)(2,1)S(1)}, u32[]{:S(2)}, u32[]{:S(2)}) %collective-permute-start.31) | collective-permute-done | bytes 688160 | tf_op jit(solution)/shard_map/ppermute | solution.py:386
  153.4 1.8 copy-done.2
  155.2 1.8 copy-done.3
  157.0 2.7 %key_value.3.refs_0_ = bf16[4,256,256]{2,1,0:T(8,128)(2,1)S(1)} custom-call(bf16[1344,256]{1,0:T(8,128)(2,1)S(1)} %add_convert_fusion.2.own.state, bf16[1344,256]{1,0:T(8,128)(2,1)S(1)} %collective-permute-done.31.other, f32[2,1344]{1,0:T(2,128)S(1)} %reshape.17.gain, f32[2,256,128]{2,1,0:T(8,128)S(1)} %copy-done.6, bf16[2688,512]{1,0:T(8,128)(2,1)S(1)} %copy-done.3, ...), custom_call_target="tpu_custom_call" | custom-call | tf_op jit(solution)/shard_map/key_value/pallas_call | solution.py:122
  160.9 19.0 %collective-permute-done.34.refs_1_ = bf16[4,256,256]{2,1,0:T(8,128)(2,1)S(1)} collective-permute-done((bf16[4,256,256]{2,1,0:T(8,128)(2,1)S(1)}, bf16[4,256,256]{2,1,0:T(8,128)(2,1)S(1)}, u32[]{:S(2)}, u32[]{:S(2)}) %collective-permute-start.34) | collective-permute-done | bytes 524320 | tf_op jit(solution)/shard_map/ppermute | solution.py:438
  180.2 4.3 %collective-permute-start.39 = (bf16[2,336,512]{2,1,0:T(8,128)(2,1)S(1)}, bf16[2,336,512]{2,1,0:T(8,128)(2,1)S(1)}, u32[]{:S(2)}, u32[]{:S(2)}) collective-permute-start(bf16[2,336,512]{2,1,0:T(8,128)(2,1)S(1)} %copy-done.7), channel_id=1, source_target_pairs={{0,16},{16,0},{1,17},{17,1},{2,18},{18,2},{3,19},{19,3},{4,20},{20... | collective-permute-start | bytes 2064392 | tf_op jit(solution)/shard_map/ppermute | solution.py:383
  185.1 4.8 %collective-permute-done.37.refs_3_ = bf16[4,256,256]{2,1,0:T(8,128)(2,1)S(1)} collective-permute-done((bf16[4,256,256]{2,1,0:T(8,128)(2,1)S(1)}, bf16[4,256,256]{2,1,0:T(8,128)(2,1)S(1)}, u32[]{:S(2)}, u32[]{:S(2)}) %collective-permute-start.37) | collective-permute-done | bytes 524320 | tf_op jit(solution)/shard_map/ppermute | solution.py:441
  189.9 4.4 %collective-permute-start.41 = (bf16[2,336,512]{2,1,0:T(8,128)(2,1)}, bf16[2,336,512]{2,1,0:T(8,128)(2,1)S(1)}, u32[]{:S(2)}, u32[]{:S(2)}) collective-permute-start(bf16[2,336,512]{2,1,0:T(8,128)(2,1)} %collective-permute-done.29.refs_2_), channel_id=1, source_target_pairs={{0,16},{16,0},{1,17},{17,1},{2,18},{18,2},{3,19},{19,3},{4,20},{20... | collective-permute-start | bytes 2064392 | tf_op jit(solution)/shard_map/ppermute | solution.py:383
  194.3 2.0 collective-permute-start.45
  198.0 1.5 collective-permute-start.48
  199.5 1.3 collective-permute-start.47
  200.8 6.8 %collective-permute-done.38.refs_4_ = bf16[1,336,512]{2,1,0:T(8,128)(2,1)S(1)} collective-permute-done((bf16[1,336,512]{2,1,0:T(8,128)(2,1)S(1)}, bf16[1,336,512]{2,1,0:T(8,128)(2,1)S(1)}, u32[]{:S(2)}, u32[]{:S(2)}) %collective-permute-start.38) | collective-permute-done | bytes 344096 | tf_op jit(solution)/shard_map/ppermute | solution.py:351
  207.6 1.3 collective-permute-start.43
  208.9 1.3 collective-permute-done.43.refs_12_
  210.2 5.2 %query.3.queries = bf16[2,512,256]{2,1,0:T(8,128)(2,1)S(1)} custom-call(bf16[1344,256]{1,0:T(8,128)(2,1)S(1)} %add_convert_fusion.2.own.state, bf16[1344,256]{1,0:T(8,128)(2,1)S(1)} %copy-done.11, f32[2,1344]{1,0:T(2,128)S(1)} %reshape.17.gain, f32[2,256,128]{2,1,0:T(8,128)S(1)} %copy-done.6, bf16[2,336,512]{2,1,0:T(8,128)(2,1)S(1)} %copy-done.7, ...), custom_call_target="tpu_custom_call" | custom-call | tf_op jit(solution)/shard_map/query/pallas_call | solution.py:169
  215.5 4.9 %attend.3 = (f32[2,512,256]{2,1,0:T(8,128)S(1)}, f32[8,256]{1,0:T(8,128)S(1)}, f32[8,256]{1,0:T(8,128)S(1)}) custom-call(s32[2,8]{1,0:T(2,128)S(1)} %copy-done.16, s32[2]{0:T(128)S(1)} %copy-done.17, bf16[2,512,256]{2,1,0:T(8,128)(2,1)S(1)} %query.3.queries, bf16[4,256,256]{2,1,0:T(8,128)(2,1)S(1)} %key_value.3.refs_0_, ...), custom_call_target="tpu_custom_call" | custom-call | tf_op jit(solution)/shard_map/attend/pallas_call | solution.py:251
  220.4 5.6 %out_project.3 = (bf16[1344,256]{1,0:T(8,128)(2,1)S(1)}, f32[1344,256]{1,0:T(8,128)S(1)}) custom-call(s32[2,8]{1,0:T(2,128)S(1)} %copy-done.16, s32[2]{0:T(128)S(1)} %copy-done.17, bf16[2,512,256]{2,1,0:T(8,128)(2,1)S(1)} %query.3.queries, bf16[4,256,256]{2,1,0:T(8,128)(2,1)S(1)} %collective-permute-done.47.window, ...), custom_call_target="tpu_custom_call" | custom-call | tf_op jit(solution)/shard_map/out_project/pallas_call | solution.py:314
  226.1 1.3 collective-permute-start.50
  227.4 2.1 collective-permute-start.52
  229.5 1.3 collective-permute-start.51
  230.8 12.9 %collective-permute-done.52 = bf16[1344,256]{1,0:T(8,128)(2,1)S(1)} collective-permute-done((bf16[1344,256]{1,0:T(8,128)(2,1)S(1)}, bf16[1344,256]{1,0:T(8,128)(2,1)S(1)}, u32[]{:S(2)}, u32[]{:S(2)}) %collective-permute-start.52) | collective-permute-done | bytes 688160 | tf_op jit(solution)/shard_map/ppermute | solution.py:493
  244.0 2.5 collective-permute-done.51
  (137 shorter events, 23.8 us)
Async XLA Ops:
  3.6 7.6 %collective-permute-start.6 = (bf16[2688,512]{1,0:T(8,128)(2,1)}, bf16[2688,512]{1,0:T(8,128)(2,1)}, u32[]{:S(2)}, u32[]{:S(2)}) collective-permute-start(bf16[2688,512]{1,0:T(8,128)(2,1)} %bitcast.23), channel_id=1, source_target_pairs={{0,16},{16,0},{1,17},{17,1},{2,18},{18,2},{3,19},{19,3},{4,20},{20... | collective-permute-start | bytes 8257544 | tf_op jit(solution)/shard_map/ppermute | solution.py:383
  3.7 12.8 %collective-permute-start.5 = (bf16[2688,512]{1,0:T(8,128)(2,1)}, bf16[2688,512]{1,0:T(8,128)(2,1)}, u32[]{:S(2)}, u32[]{:S(2)}) collective-permute-start(bf16[2688,512]{1,0:T(8,128)(2,1)} %bitcast.25), channel_id=1, source_target_pairs={{0,16},{16,0},{1,17},{17,1},{2,18},{18,2},{3,19},{19,3},{4,20},{20... | collective-permute-start | bytes 8257544 | tf_op jit(solution)/shard_map/ppermute | solution.py:383
  4.2 25.3 %collective-permute-start = (bf16[1344,256]{1,0:T(8,128)(2,1)S(1)}, bf16[1344,256]{1,0:T(8,128)(2,1)}, u32[]{:S(2)}, u32[]{:S(2)}) collective-permute-start(bf16[1344,256]{1,0:T(8,128)(2,1)S(1)} %dynamic-slice_bitcast_fusion.own.state), channel_id=1, source_target_pairs={{0,1},{1,0},{2,3},{3,2},{4,5},{5,4},{6,7},{7,6},{8,9},{9,8},{10,11... | collective-permute-start | bytes 2064392 | tf_op jit(solution)/shard_map/ppermute | solution.py:386
  9.7 16.5 %collective-permute-start.3 = (bf16[2,336,512]{2,1,0:T(8,128)(2,1)S(1)}, bf16[2,336,512]{2,1,0:T(8,128)(2,1)}, u32[]{:S(2)}, u32[]{:S(2)}) collective-permute-start(bf16[2,336,512]{2,1,0:T(8,128)(2,1)S(1)} %get-tuple-element.104.refs_0_), channel_id=1, source_target_pairs={{0,4},{4,8},{8,12},{12,14},{14,10},{10,6},{6,2},{2,0},{1,5},{5,9},... | collective-permute-start | bytes 2064392 | tf_op jit(solution)/shard_map/ppermute | solution.py:347
  11.0 16.1 %collective-permute-start.4 = (bf16[2,336,512]{2,1,0:T(8,128)(2,1)S(1)}, bf16[2,336,512]{2,1,0:T(8,128)(2,1)}, u32[]{:S(2)}, u32[]{:S(2)}) collective-permute-start(bf16[2,336,512]{2,1,0:T(8,128)(2,1)S(1)} %get-tuple-element.104.refs_0_), channel_id=1, source_target_pairs={{4,0},{8,4},{12,8},{14,12},{10,14},{6,10},{2,6},{0,2},{5,1},{9,5},... | collective-permute-start | bytes 2064392 | tf_op jit(solution)/shard_map/ppermute | solution.py:348
  11.2 18.2 %collective-permute-start.2 = (f32[1,2688]{1,0:T(1,128)S(1)}, f32[1,2688]{1,0:T(1,128)S(1)}, u32[]{:S(2)}, u32[]{:S(2)}) collective-permute-start(f32[1,2688]{1,0:T(1,128)S(1)} %copy-done.22), channel_id=1, source_target_pairs={{0,16},{16,0},{1,17},{17,1},{2,18},{18,2},{3,19},{19,3},{4,20},{20... | collective-permute-start | bytes 32264 | tf_op jit(solution)/shard_map/ppermute | solution.py:383
  27.2 29.5 %collective-permute-start.7 = (bf16[2,336,512]{2,1,0:T(8,128)(2,1)}, bf16[2,336,512]{2,1,0:T(8,128)(2,1)}, u32[]{:S(2)}, u32[]{:S(2)}) collective-permute-start(bf16[2,336,512]{2,1,0:T(8,128)(2,1)} %collective-permute-done.3.refs_1_), channel_id=1, source_target_pairs={{0,4},{4,8},{8,12},{12,14},{14,10},{10,6},{6,2},{2,0},{1,5},{5,9},... | collective-permute-start | bytes 2064392 | tf_op jit(solution)/shard_map/ppermute | solution.py:347
  28.5 28.3 %collective-permute-start.8 = (bf16[2,336,512]{2,1,0:T(8,128)(2,1)}, bf16[2,336,512]{2,1,0:T(8,128)(2,1)}, u32[]{:S(2)}, u32[]{:S(2)}) collective-permute-start(bf16[2,336,512]{2,1,0:T(8,128)(2,1)} %collective-permute-done.4.refs_7_), channel_id=1, source_target_pairs={{4,0},{8,4},{12,8},{14,12},{10,14},{6,10},{2,6},{0,2},{5,1},{9,5},... | collective-permute-start | bytes 2064392 | tf_op jit(solution)/shard_map/ppermute | solution.py:348
  36.8 19.9 %collective-permute-start.9 = (bf16[4,256,256]{2,1,0:T(8,128)(2,1)}, bf16[4,256,256]{2,1,0:T(8,128)(2,1)S(1)}, u32[]{:S(2)}, u32[]{:S(2)}) collective-permute-start(bf16[4,256,256]{2,1,0:T(8,128)(2,1)} %key_value.2.refs_0_), channel_id=1, source_target_pairs={{0,4},{2,6},{4,8},{6,10},{8,12},{10,14},{12,0},{14,2},{1,5},{3,7},... | collective-permute-start | bytes 1572872 | tf_op jit(solution)/shard_map/ppermute | solution.py:438
  56.7 29.3 %collective-permute-start.10 = (bf16[2,336,512]{2,1,0:T(8,128)(2,1)}, bf16[2,336,512]{2,1,0:T(8,128)(2,1)S(1)}, u32[]{:S(2)}, u32[]{:S(2)}) collective-permute-start(bf16[2,336,512]{2,1,0:T(8,128)(2,1)} %collective-permute-done.7.refs_2_), channel_id=1, source_target_pairs={{0,4},{4,8},{8,12},{12,14},{14,10},{10,6},{6,2},{2,0},{1,5},{5,9},... | collective-permute-start | bytes 2064392 | tf_op jit(solution)/shard_map/ppermute | solution.py:347
  57.9 24.2 %collective-permute-start.13 = (bf16[4,256,256]{2,1,0:T(8,128)(2,1)S(1)}, bf16[4,256,256]{2,1,0:T(8,128)(2,1)S(1)}, u32[]{:S(2)}, u32[]{:S(2)}) collective-permute-start(bf16[4,256,256]{2,1,0:T(8,128)(2,1)S(1)} %broadcast_select_fusion.9), channel_id=1, source_target_pairs={{0,2},{2,0},{4,6},{6,4},{8,10},{10,8},{12,14},{14,12},{1,3},{3,1},... | collective-permute-start | bytes 1572872 | tf_op jit(solution)/shard_map/ppermute | solution.py:441
  58.3 27.7 %collective-permute-start.12 = (bf16[4,256,256]{2,1,0:T(8,128)(2,1)S(1)}, bf16[4,256,256]{2,1,0:T(8,128)(2,1)S(1)}, u32[]{:S(2)}, u32[]{:S(2)}) collective-permute-start(bf16[4,256,256]{2,1,0:T(8,128)(2,1)S(1)} %collective-permute-done.9.refs_1_), channel_id=1, source_target_pairs={{0,4},{2,6},{4,8},{6,10},{8,12},{10,14},{12,0},{14,2},{1,5},{3,7},... | collective-permute-start | bytes 1572872 | tf_op jit(solution)/shard_map/ppermute | solution.py:438
  58.3 28.2 %collective-permute-start.11 = (bf16[2,336,512]{2,1,0:T(8,128)(2,1)}, bf16[2,336,512]{2,1,0:T(8,128)(2,1)S(1)}, u32[]{:S(2)}, u32[]{:S(2)}) collective-permute-start(bf16[2,336,512]{2,1,0:T(8,128)(2,1)} %collective-permute-done.8.refs_6_), channel_id=1, source_target_pairs={{4,0},{8,4},{12,8},{14,12},{10,14},{6,10},{2,6},{0,2},{5,1},{9,5},... | collective-permute-start | bytes 2064392 | tf_op jit(solution)/shard_map/ppermute | solution.py:348
  59.4 28.3 %collective-permute-start.15 = (bf16[2,336,512]{2,1,0:T(8,128)(2,1)S(1)}, bf16[2,336,512]{2,1,0:T(8,128)(2,1)S(1)}, u32[]{:S(2)}, u32[]{:S(2)}) collective-permute-start(bf16[2,336,512]{2,1,0:T(8,128)(2,1)S(1)} %copy-done.9), channel_id=1, source_target_pairs={{0,16},{16,0},{1,17},{17,1},{2,18},{18,2},{3,19},{19,3},{4,20},{20... | collective-permute-start | bytes 2064392 | tf_op jit(solution)/shard_map/ppermute | solution.py:383
  82.1 5.9 %collective-permute-start.16 = (bf16[2,336,512]{2,1,0:T(8,128)(2,1)}, bf16[2,336,512]{2,1,0:T(8,128)(2,1)S(1)}, u32[]{:S(2)}, u32[]{:S(2)}) collective-permute-start(bf16[2,336,512]{2,1,0:T(8,128)(2,1)} %collective-permute-done.3.refs_1_), channel_id=1, source_target_pairs={{0,16},{16,0},{1,17},{17,1},{2,18},{18,2},{3,19},{19,3},{4,20},{20... | collective-permute-start | bytes 2064392 | tf_op jit(solution)/shard_map/ppermute | solution.py:383
  86.5 6.4 %collective-permute-start.21 = (bf16[2,336,512]{2,1,0:T(8,128)(2,1)}, bf16[2,336,512]{2,1,0:T(8,128)(2,1)S(1)}, u32[]{:S(2)}, u32[]{:S(2)}) collective-permute-start(bf16[2,336,512]{2,1,0:T(8,128)(2,1)} %collective-permute-done.8.refs_6_), channel_id=1, source_target_pairs={{0,16},{16,0},{1,17},{17,1},{2,18},{18,2},{3,19},{19,3},{4,20},{20... | collective-permute-start | bytes 2064392 | tf_op jit(solution)/shard_map/ppermute | solution.py:383
  87.7 13.8 %collective-permute-start.18 = (bf16[2,336,512]{2,1,0:T(8,128)(2,1)S(1)}, bf16[2,336,512]{2,1,0:T(8,128)(2,1)S(1)}, u32[]{:S(2)}, u32[]{:S(2)}) collective-permute-start(bf16[2,336,512]{2,1,0:T(8,128)(2,1)S(1)} %collective-permute-done.10.refs_3_), channel_id=1, source_target_pairs={{0,16},{16,0},{1,17},{17,1},{2,18},{18,2},{3,19},{19,3},{4,20},{20... | collective-permute-start | bytes 2064392 | tf_op jit(solution)/shard_map/ppermute | solution.py:383
  88.0 13.5 %collective-permute-start.20 = (bf16[2,336,512]{2,1,0:T(8,128)(2,1)S(1)}, bf16[2,336,512]{2,1,0:T(8,128)(2,1)S(1)}, u32[]{:S(2)}, u32[]{:S(2)}) collective-permute-start(bf16[2,336,512]{2,1,0:T(8,128)(2,1)S(1)} %collective-permute-done.11.refs_5_), channel_id=1, source_target_pairs={{0,16},{16,0},{1,17},{17,1},{2,18},{18,2},{3,19},{19,3},{4,20},{20... | collective-permute-start | bytes 2064392 | tf_op jit(solution)/shard_map/ppermute | solution.py:383
  89.0 9.3 %collective-permute-start.14 = (bf16[1,336,512]{2,1,0:T(8,128)(2,1)S(1)}, bf16[1,336,512]{2,1,0:T(8,128)(2,1)S(1)}, u32[]{:S(2)}, u32[]{:S(2)}) collective-permute-start(bf16[1,336,512]{2,1,0:T(8,128)(2,1)S(1)} %slice.12), channel_id=1, source_target_pairs={{0,4},{4,8},{8,12},{12,14},{14,10},{10,6},{6,2},{2,0},{1,5},{5,9},... | collective-permute-start | bytes 1032200 | tf_op jit(solution)/shard_map/ppermute | solution.py:351
  91.0 9.3 %collective-permute-start.24 = (bf16[1,336,512]{2,1,0:T(8,128)(2,1)S(1)}, bf16[1,336,512]{2,1,0:T(8,128)(2,1)S(1)}, u32[]{:S(2)}, u32[]{:S(2)}) collective-permute-start(bf16[1,336,512]{2,1,0:T(8,128)(2,1)S(1)} %slice.13), channel_id=1, source_target_pairs={{4,0},{8,4},{12,8},{14,12},{10,14},{6,10},{2,6},{0,2},{5,1},{9,5},... | collective-permute-start | bytes 1032200 | tf_op jit(solution)/shard_map/ppermute | solution.py:352
  92.9 19.7 %collective-permute-start.23 = (bf16[4,256,256]{2,1,0:T(8,128)(2,1)S(1)}, bf16[4,256,256]{2,1,0:T(8,128)(2,1)S(1)}, u32[]{:S(2)}, u32[]{:S(2)}) collective-permute-start(bf16[4,256,256]{2,1,0:T(8,128)(2,1)S(1)} %broadcast_select_fusion.8), channel_id=1, source_target_pairs={{0,2},{2,0},{4,6},{6,4},{8,10},{10,8},{12,14},{14,12},{1,3},{3,1},... | collective-permute-start | bytes 1572872 | tf_op jit(solution)/shard_map/ppermute | solution.py:441
  100.3 12.4 %collective-permute-start.25 = (bf16[1,336,512]{2,1,0:T(8,128)(2,1)S(1)}, bf16[1,336,512]{2,1,0:T(8,128)(2,1)S(1)}, u32[]{:S(2)}, u32[]{:S(2)}) collective-permute-start(bf16[1,336,512]{2,1,0:T(8,128)(2,1)S(1)} %collective-permute-done.24.refs_4_), channel_id=1, source_target_pairs={{0,16},{16,0},{1,17},{17,1},{2,18},{18,2},{3,19},{19,3},{4,20},{20... | collective-permute-start | bytes 1032200 | tf_op jit(solution)/shard_map/ppermute | solution.py:383
  118.6 16.7 %collective-permute-start.28 = (bf16[1344,256]{1,0:T(8,128)(2,1)S(1)}, bf16[1344,256]{1,0:T(8,128)(2,1)S(1)}, u32[]{:S(2)}, u32[]{:S(2)}) collective-permute-start(bf16[1344,256]{1,0:T(8,128)(2,1)S(1)} %get-tuple-element.75), channel_id=1, source_target_pairs={{0,1},{1,0},{2,3},{3,2},{4,5},{5,4},{6,7},{7,6},{8,9},{9,8},{10,11... | collective-permute-start | bytes 2064392 | tf_op jit(solution)/shard_map/ppermute | solution.py:386
  118.9 16.4 %collective-permute-start.26 = (bf16[2,336,512]{2,1,0:T(8,128)(2,1)S(1)}, bf16[2,336,512]{2,1,0:T(8,128)(2,1)S(1)}, u32[]{:S(2)}, u32[]{:S(2)}) collective-permute-start(bf16[2,336,512]{2,1,0:T(8,128)(2,1)S(1)} %copy-done.7), channel_id=1, source_target_pairs={{0,4},{4,8},{8,12},{12,14},{14,10},{10,6},{6,2},{2,0},{1,5},{5,9},... | collective-permute-start | bytes 2064392 | tf_op jit(solution)/shard_map/ppermute | solution.py:347
  118.9 16.4 %collective-permute-start.27 = (bf16[2,336,512]{2,1,0:T(8,128)(2,1)S(1)}, bf16[2,336,512]{2,1,0:T(8,128)(2,1)S(1)}, u32[]{:S(2)}, u32[]{:S(2)}) collective-permute-start(bf16[2,336,512]{2,1,0:T(8,128)(2,1)S(1)} %copy-done.7), channel_id=1, source_target_pairs={{4,0},{8,4},{12,8},{14,12},{10,14},{6,10},{2,6},{0,2},{5,1},{9,5},... | collective-permute-start | bytes 2064392 | tf_op jit(solution)/shard_map/ppermute | solution.py:348
  135.4 15.6 %collective-permute-start.31 = (bf16[1344,256]{1,0:T(8,128)(2,1)S(1)}, bf16[1344,256]{1,0:T(8,128)(2,1)S(1)}, u32[]{:S(2)}, u32[]{:S(2)}) collective-permute-start(bf16[1344,256]{1,0:T(8,128)(2,1)S(1)} %add_convert_fusion.2.own.state), channel_id=1, source_target_pairs={{0,1},{1,0},{2,3},{3,2},{4,5},{5,4},{6,7},{7,6},{8,9},{9,8},{10,11... | collective-permute-start | bytes 2064392 | tf_op jit(solution)/shard_map/ppermute | solution.py:386
  136.7 15.2 %collective-permute-start.29 = (bf16[2,336,512]{2,1,0:T(8,128)(2,1)S(1)}, bf16[2,336,512]{2,1,0:T(8,128)(2,1)}, u32[]{:S(2)}, u32[]{:S(2)}) collective-permute-start(bf16[2,336,512]{2,1,0:T(8,128)(2,1)S(1)} %collective-permute-done.26.refs_1_), channel_id=1, source_target_pairs={{0,4},{4,8},{8,12},{12,14},{14,10},{10,6},{6,2},{2,0},{1,5},{5,9},... | collective-permute-start | bytes 2064392 | tf_op jit(solution)/shard_map/ppermute | solution.py:347
  137.0 14.9 %collective-permute-start.30 = (bf16[2,336,512]{2,1,0:T(8,128)(2,1)S(1)}, bf16[2,336,512]{2,1,0:T(8,128)(2,1)}, u32[]{:S(2)}, u32[]{:S(2)}) collective-permute-start(bf16[2,336,512]{2,1,0:T(8,128)(2,1)S(1)} %collective-permute-done.27.refs_7_), channel_id=1, source_target_pairs={{4,0},{8,4},{12,8},{14,12},{10,14},{6,10},{2,6},{0,2},{5,1},{9,5},... | collective-permute-start | bytes 2064392 | tf_op jit(solution)/shard_map/ppermute | solution.py:348
  138.1 22.8 %collective-permute-start.35 = (bf16[1344,256]{1,0:T(8,128)(2,1)S(1)}, bf16[1344,256]{1,0:T(8,128)(2,1)}, u32[]{:S(2)}, u32[]{:S(2)}) collective-permute-start(bf16[1344,256]{1,0:T(8,128)(2,1)S(1)} %add_convert_fusion.2.own.state), channel_id=1, source_target_pairs={{16,0},{17,1},{18,2},{19,3},{20,4},{21,5},{22,6},{23,7},{24,8},{25... | collective-permute-start | bytes 2064392 | tf_op jit(solution)/shard_map/ppermute | solution.py:488
  151.9 28.0 %collective-permute-start.32 = (bf16[2,336,512]{2,1,0:T(8,128)(2,1)}, bf16[2,336,512]{2,1,0:T(8,128)(2,1)S(1)}, u32[]{:S(2)}, u32[]{:S(2)}) collective-permute-start(bf16[2,336,512]{2,1,0:T(8,128)(2,1)} %collective-permute-done.29.refs_2_), channel_id=1, source_target_pairs={{0,4},{4,8},{8,12},{12,14},{14,10},{10,6},{6,2},{2,0},{1,5},{5,9},... | collective-permute-start | bytes 2064392 | tf_op jit(solution)/shard_map/ppermute | solution.py:347
  152.3 27.6 %collective-permute-start.33 = (bf16[2,336,512]{2,1,0:T(8,128)(2,1)}, bf16[2,336,512]{2,1,0:T(8,128)(2,1)}, u32[]{:S(2)}, u32[]{:S(2)}) collective-permute-start(bf16[2,336,512]{2,1,0:T(8,128)(2,1)} %collective-permute-done.30.refs_6_), channel_id=1, source_target_pairs={{4,0},{8,4},{12,8},{14,12},{10,14},{6,10},{2,6},{0,2},{5,1},{9,5},... | collective-permute-start | bytes 2064392 | tf_op jit(solution)/shard_map/ppermute | solution.py:348
  160.5 19.3 %collective-permute-start.34 = (bf16[4,256,256]{2,1,0:T(8,128)(2,1)S(1)}, bf16[4,256,256]{2,1,0:T(8,128)(2,1)S(1)}, u32[]{:S(2)}, u32[]{:S(2)}) collective-permute-start(bf16[4,256,256]{2,1,0:T(8,128)(2,1)S(1)} %key_value.3.refs_0_), channel_id=1, source_target_pairs={{0,4},{2,6},{4,8},{6,10},{8,12},{10,14},{12,0},{14,2},{1,5},{3,7},... | collective-permute-start | bytes 1572872 | tf_op jit(solution)/shard_map/ppermute | solution.py:438
  179.9 10.0 %collective-permute-start.37 = (bf16[4,256,256]{2,1,0:T(8,128)(2,1)S(1)}, bf16[4,256,256]{2,1,0:T(8,128)(2,1)S(1)}, u32[]{:S(2)}, u32[]{:S(2)}) collective-permute-start(bf16[4,256,256]{2,1,0:T(8,128)(2,1)S(1)} %broadcast_select_fusion.7), channel_id=1, source_target_pairs={{0,2},{2,0},{4,6},{6,4},{8,10},{10,8},{12,14},{14,12},{1,3},{3,1},... | collective-permute-start | bytes 1572872 | tf_op jit(solution)/shard_map/ppermute | solution.py:441
  180.2 14.1 %collective-permute-start.36 = (bf16[4,256,256]{2,1,0:T(8,128)(2,1)S(1)}, bf16[4,256,256]{2,1,0:T(8,128)(2,1)S(1)}, u32[]{:S(2)}, u32[]{:S(2)}) collective-permute-start(bf16[4,256,256]{2,1,0:T(8,128)(2,1)S(1)} %collective-permute-done.34.refs_1_), channel_id=1, source_target_pairs={{0,4},{2,6},{4,8},{6,10},{8,12},{10,14},{12,0},{14,2},{1,5},{3,7},... | collective-permute-start | bytes 1572872 | tf_op jit(solution)/shard_map/ppermute | solution.py:438
  180.2 17.2 %collective-permute-start.39 = (bf16[2,336,512]{2,1,0:T(8,128)(2,1)S(1)}, bf16[2,336,512]{2,1,0:T(8,128)(2,1)S(1)}, u32[]{:S(2)}, u32[]{:S(2)}) collective-permute-start(bf16[2,336,512]{2,1,0:T(8,128)(2,1)S(1)} %copy-done.7), channel_id=1, source_target_pairs={{0,16},{16,0},{1,17},{17,1},{2,18},{18,2},{3,19},{19,3},{4,20},{20... | collective-permute-start | bytes 2064392 | tf_op jit(solution)/shard_map/ppermute | solution.py:383
  184.5 12.9 %collective-permute-start.40 = (bf16[2,336,512]{2,1,0:T(8,128)(2,1)S(1)}, bf16[2,336,512]{2,1,0:T(8,128)(2,1)S(1)}, u32[]{:S(2)}, u32[]{:S(2)}) collective-permute-start(bf16[2,336,512]{2,1,0:T(8,128)(2,1)S(1)} %copy-done.13), channel_id=1, source_target_pairs={{0,16},{16,0},{1,17},{17,1},{2,18},{18,2},{3,19},{19,3},{4,20},{20... | collective-permute-start | bytes 2064392 | tf_op jit(solution)/shard_map/ppermute | solution.py:383
  184.6 13.4 %collective-permute-start.46 = (bf16[2,336,512]{2,1,0:T(8,128)(2,1)S(1)}, bf16[2,336,512]{2,1,0:T(8,128)(2,1)S(1)}, u32[]{:S(2)}, u32[]{:S(2)}) collective-permute-start(bf16[2,336,512]{2,1,0:T(8,128)(2,1)S(1)} %copy-done.15), channel_id=1, source_target_pairs={{0,16},{16,0},{1,17},{17,1},{2,18},{18,2},{3,19},{19,3},{4,20},{20... | collective-permute-start | bytes 2064392 | tf_op jit(solution)/shard_map/ppermute | solution.py:383
  189.9 8.1 %collective-permute-start.41 = (bf16[2,336,512]{2,1,0:T(8,128)(2,1)}, bf16[2,336,512]{2,1,0:T(8,128)(2,1)S(1)}, u32[]{:S(2)}, u32[]{:S(2)}) collective-permute-start(bf16[2,336,512]{2,1,0:T(8,128)(2,1)} %collective-permute-done.29.refs_2_), channel_id=1, source_target_pairs={{0,16},{16,0},{1,17},{17,1},{2,18},{18,2},{3,19},{19,3},{4,20},{20... | collective-permute-start | bytes 2064392 | tf_op jit(solution)/shard_map/ppermute | solution.py:383
  194.3 5.2 %collective-permute-start.45 = (bf16[2,336,512]{2,1,0:T(8,128)(2,1)}, bf16[2,336,512]{2,1,0:T(8,128)(2,1)S(1)}, u32[]{:S(2)}, u32[]{:S(2)}) collective-permute-start(bf16[2,336,512]{2,1,0:T(8,128)(2,1)} %collective-permute-done.30.refs_6_), channel_id=1, source_target_pairs={{0,16},{16,0},{1,17},{17,1},{2,18},{18,2},{3,19},{19,3},{4,20},{20... | collective-permute-start | bytes 2064392 | tf_op jit(solution)/shard_map/ppermute | solution.py:383
  197.4 12.8 %collective-permute-start.42 = (bf16[2,336,512]{2,1,0:T(8,128)(2,1)S(1)}, bf16[2,336,512]{2,1,0:T(8,128)(2,1)S(1)}, u32[]{:S(2)}, u32[]{:S(2)}) collective-permute-start(bf16[2,336,512]{2,1,0:T(8,128)(2,1)S(1)} %collective-permute-done.32.refs_3_), channel_id=1, source_target_pairs={{0,16},{16,0},{1,17},{17,1},{2,18},{18,2},{3,19},{19,3},{4,20},{20... | collective-permute-start | bytes 2064392 | tf_op jit(solution)/shard_map/ppermute | solution.py:383
  197.5 12.7 %collective-permute-start.44 = (bf16[2,336,512]{2,1,0:T(8,128)(2,1)}, bf16[2,336,512]{2,1,0:T(8,128)(2,1)S(1)}, u32[]{:S(2)}, u32[]{:S(2)}) collective-permute-start(bf16[2,336,512]{2,1,0:T(8,128)(2,1)} %collective-permute-done.33.refs_5_), channel_id=1, source_target_pairs={{0,16},{16,0},{1,17},{17,1},{2,18},{18,2},{3,19},{19,3},{4,20},{20... | collective-permute-start | bytes 2064392 | tf_op jit(solution)/shard_map/ppermute | solution.py:383
  198.0 9.6 %collective-permute-start.38 = (bf16[1,336,512]{2,1,0:T(8,128)(2,1)S(1)}, bf16[1,336,512]{2,1,0:T(8,128)(2,1)S(1)}, u32[]{:S(2)}, u32[]{:S(2)}) collective-permute-start(bf16[1,336,512]{2,1,0:T(8,128)(2,1)S(1)} %slice.14), channel_id=1, source_target_pairs={{0,4},{4,8},{8,12},{12,14},{14,10},{10,6},{6,2},{2,0},{1,5},{5,9},... | collective-permute-start | bytes 1032200 | tf_op jit(solution)/shard_map/ppermute | solution.py:351
  198.0 10.9 %collective-permute-start.48 = (bf16[1,336,512]{2,1,0:T(8,128)(2,1)S(1)}, bf16[1,336,512]{2,1,0:T(8,128)(2,1)S(1)}, u32[]{:S(2)}, u32[]{:S(2)}) collective-permute-start(bf16[1,336,512]{2,1,0:T(8,128)(2,1)S(1)} %slice.15), channel_id=1, source_target_pairs={{4,0},{8,4},{12,8},{14,12},{10,14},{6,10},{2,6},{0,2},{5,1},{9,5},... | collective-permute-start | bytes 1032200 | tf_op jit(solution)/shard_map/ppermute | solution.py:352
  199.5 20.9 %collective-permute-start.47 = (bf16[4,256,256]{2,1,0:T(8,128)(2,1)S(1)}, bf16[4,256,256]{2,1,0:T(8,128)(2,1)S(1)}, u32[]{:S(2)}, u32[]{:S(2)}) collective-permute-start(bf16[4,256,256]{2,1,0:T(8,128)(2,1)S(1)} %broadcast_select_fusion.6), channel_id=1, source_target_pairs={{0,2},{2,0},{4,6},{6,4},{8,10},{10,8},{12,14},{14,12},{1,3},{3,1},... | collective-permute-start | bytes 1572872 | tf_op jit(solution)/shard_map/ppermute | solution.py:441
  208.9 11.5 %collective-permute-start.49 = (bf16[1,336,512]{2,1,0:T(8,128)(2,1)S(1)}, bf16[1,336,512]{2,1,0:T(8,128)(2,1)S(1)}, u32[]{:S(2)}, u32[]{:S(2)}) collective-permute-start(bf16[1,336,512]{2,1,0:T(8,128)(2,1)S(1)} %collective-permute-done.48.refs_4_), channel_id=1, source_target_pairs={{0,16},{16,0},{1,17},{17,1},{2,18},{18,2},{3,19},{19,3},{4,20},{20... | collective-permute-start | bytes 1032200 | tf_op jit(solution)/shard_map/ppermute | solution.py:383
  226.1 20.4 %collective-permute-start.50 = (f32[1344,256]{1,0:T(8,128)S(1)}, f32[1344,256]{1,0:T(8,128)S(1)}, u32[]{:S(2)}, u32[]{:S(2)}) collective-permute-start(f32[1344,256]{1,0:T(8,128)S(1)} %get-tuple-element.94), channel_id=1, source_target_pairs={{0,16},{1,17},{2,18},{3,19},{4,20},{5,21},{6,22},{7,23},{8,24},{9,... | collective-permute-start | bytes 4128776 | tf_op jit(solution)/shard_map/ppermute | solution.py:494
  227.4 16.3 %collective-permute-start.52 = (bf16[1344,256]{1,0:T(8,128)(2,1)S(1)}, bf16[1344,256]{1,0:T(8,128)(2,1)S(1)}, u32[]{:S(2)}, u32[]{:S(2)}) collective-permute-start(bf16[1344,256]{1,0:T(8,128)(2,1)S(1)} %get-tuple-element.95), channel_id=1, source_target_pairs={{16,17},{17,16},{18,19},{19,18},{20,21},{21,20},{22,23},{23,22},{2... | collective-permute-start | bytes 2064392 | tf_op jit(solution)/shard_map/ppermute | solution.py:493
  229.5 16.9 %collective-permute-start.51 = (bf16[1344,256]{1,0:T(8,128)(2,1)S(1)}, bf16[1344,256]{1,0:T(8,128)(2,1)S(1)}, u32[]{:S(2)}, u32[]{:S(2)}) collective-permute-start(bf16[1344,256]{1,0:T(8,128)(2,1)S(1)} %get-tuple-element.95), channel_id=1, source_target_pairs={{0,17},{1,16},{2,19},{3,18},{4,21},{5,20},{6,23},{7,22},{8,25},{9,... | collective-permute-start | bytes 2064392 | tf_op jit(solution)/shard_map/ppermute | solution.py:493
  (28 other events, 247.4 us)
